TPU v7x, 32 devices: a whole 2x2x4 slice. The times are simulated.
32 devices in a mesh: pos: 2 (over x), seq: 16 (over z, y, core).
Axes of the slice: x: 2, y: 2, z: 4, core: 2. Of those that a mesh axis runs over, the one named last changes fastest.
Arguments:
- tokens: bfloat16 [16, 1024, 768], P('seq', 'pos'), may hold values from -6 to 6
- segment_ids: int32 [16, 1024], P('seq'), may hold values from 0 to 5, never falling along the last dimension, each value on 1 to 512 neighbouring positions
- first_gain: float32 [768], replicated, may hold values from 0.5 to 1.5
- first_bias: float32 [768], replicated, may hold values from -1.5 to 1.5
- w_qkv: bfloat16 [768, 2304], replicated, may hold values from -0.21875 to 0.21875
- query_gain: float32 [64], replicated, may hold values from 0.7 to 1.5
- key_gain: float32 [64], replicated, may hold values from 0.7 to 1.5
- w_out: bfloat16 [768, 768], replicated, may hold values from -2.5 to 2.5
- second_gain: float32 [768], replicated, may hold values from 0.5 to 1.5
- second_bias: float32 [768], replicated, may hold values from -1.5 to 1.5
- w_up: bfloat16 [768, 3072], P(None, 'seq'), may hold values from -0.21875 to 0.21875
- w_down: bfloat16 [768, 3072], P(None, 'seq'), may hold values from -0.109375 to 0.109375
- out_grad: bfloat16 [16, 1024, 768], P('seq', 'pos'), may hold values from -6 to 6
Outputs:
- block_out: bfloat16 [16, 1024, 768], P('seq', 'pos')
- input_grad: float32 [16, 1024, 768], P('seq', 'pos')
- first_gain_grad: float32 [768], replicated
- first_bias_grad: float32 [768], replicated
- qkv_grad: float32 [768, 2304], replicated
- query_gain_grad: float32 [64], replicated
- key_gain_grad: float32 [64], replicated
- proj_grad: float32 [768, 768], replicated
- second_gain_grad: float32 [768], replicated
- second_bias_grad: float32 [768], replicated
- up_grad: float32 [768, 3072], P(None, 'seq')
- down_grad: float32 [768, 3072], P(None, 'seq')
Inputs may be any that keep to these rules, and one draw needn't show every extreme that they name: `segment_ids`: in each sequence image numbers start at 0, never fall, each of the 6 images holds 1 to 512 patches, and one holds exactly 512.
All inputs are finite; a program needn't handle non-finite values.
Results may differ from a plain program's by a relative error of at most 0.015.
Values may be sent and summed in bfloat16 or wider, within the bound.
A program may use at most 768 MiB of HBM per device.

v0:
```python
import jax
import jax.numpy as jnp
from jax import lax
from jax.sharding import PartitionSpec as P

EPS = 1e-06


def layer_norm(rows, gain, shift):
    average = jnp.mean(rows, axis=-1, keepdims=True)
    centred = rows - average
    spread = jnp.mean(centred * centred, axis=-1, keepdims=True)
    return centred * lax.rsqrt(spread + EPS) * gain + shift


def head_norm(values, gain):
    average = jnp.mean(values, axis=-1, keepdims=True)
    centred = values - average
    spread = jnp.mean(centred * centred, axis=-1, keepdims=True)
    return centred * lax.rsqrt(spread + EPS) * gain


def qk_norms(raw_query, raw_keys, query_gain, key_gain):
    return (head_norm(raw_query, query_gain), head_norm(raw_keys, key_gain))


def gelu_exact(values):
    return jax.nn.gelu(values, approximate=False)


def gelu_back(pre, upstream):
    return jax.vjp(gelu_exact, pre)[1](upstream)[0]


def group_size(count, length):
    for option in range(1, count + 1):
        if count % option == 0 and option * length >= 512:
            return option
    return count


def rows_product(left, right):
    return lax.dot_general(
        left, right, (((0,), (0,)), ((), ())), preferred_element_type=jnp.float32
    )


def cols_product(left, right):
    return lax.dot_general(
        left, right, (((1,), (1,)), ((), ())), preferred_element_type=jnp.float32
    )


def local(
    tokens,
    segment_ids,
    first_gain,
    first_bias,
    w_qkv,
    query_gain,
    key_gain,
    w_out,
    second_gain,
    second_bias,
    w_up,
    w_down,
    out_grad,
):
    seqs_here, local_len, width = tokens.shape
    full_len = segment_ids.shape[1]
    head_dim = query_gain.shape[0]
    heads = width // head_dim
    rows_here = seqs_here * local_len
    scale = head_dim ** (-0.5)
    offset = lax.axis_index("pos") * local_len
    query_marks = lax.dynamic_slice_in_dim(segment_ids, offset, local_len, 1)
    block = group_size(seqs_here, local_len)
    count_blocks = seqs_here // block

    def split(array):
        return array.reshape((count_blocks, block) + array.shape[1:])

    inputs = tokens.astype(jnp.float32).reshape(rows_here, width)
    normed_low = layer_norm(inputs, first_gain, first_bias).astype(jnp.bfloat16)
    mixed = jnp.dot(normed_low, w_qkv, preferred_element_type=jnp.float32).reshape(
        rows_here, 3, heads, head_dim
    )
    raw_query = mixed[:, 0]
    raw_keys = mixed[:, 1]
    query = (
        head_norm(raw_query, query_gain)
        .astype(jnp.bfloat16)
        .reshape(seqs_here, local_len, heads, head_dim)
    )
    keys_local = (
        head_norm(raw_keys, key_gain).astype(jnp.bfloat16).reshape(seqs_here, local_len, width)
    )
    values_local = mixed[:, 2].astype(jnp.bfloat16).reshape(seqs_here, local_len, width)
    keys_all, values_all = (
        lax.all_gather(keys_local, "pos", axis=1, tiled=True),
        lax.all_gather(values_local, "pos", axis=1, tiled=True),
    )
    keys_four = keys_all.reshape(seqs_here, full_len, heads, head_dim)
    values_four = values_all.reshape(seqs_here, full_len, heads, head_dim)

    def scores_for(query_blk, keys_blk, query_lab, key_lab):
        raw = (
            jnp.einsum("bqhd,bkhd->bhqk", query_blk, keys_blk, preferred_element_type=jnp.float32)
            * scale
        )
        allowed = (query_lab[:, :, None] == key_lab[:, None, :])[:, None]
        return jnp.where(allowed, raw, -1e30)

    def forward_block(packed):
        query_blk, keys_blk, values_blk, query_lab, key_lab = packed
        scores = scores_for(query_blk, keys_blk, query_lab, key_lab)
        peak = jnp.max(scores, axis=-1, keepdims=True)
        expd = jnp.exp(scores - peak)
        totals = jnp.sum(expd, axis=-1, keepdims=True)
        probs = (expd / totals).astype(jnp.bfloat16)
        result = jnp.einsum(
            "bhqk,bkhd->bqhd", probs, values_blk, preferred_element_type=jnp.float32
        )
        return (result, peak + jnp.log(totals))

    attended, log_totals = lax.map(
        forward_block,
        (
            split(query),
            split(keys_four),
            split(values_four),
            split(query_marks),
            split(segment_ids),
        ),
    )
    attended_low = attended.astype(jnp.bfloat16).reshape(rows_here, width)
    middle = inputs + jnp.dot(attended_low, w_out, preferred_element_type=jnp.float32)
    second_low = layer_norm(middle, second_gain, second_bias).astype(jnp.bfloat16)
    grad_out = out_grad.reshape(rows_here, width)
    grad_float = grad_out.astype(jnp.float32)
    up_all, down_all = (
        lax.all_gather(w_up, "seq", axis=1, tiled=True),
        lax.all_gather(w_down, "seq", axis=1, tiled=True),
    )
    pre = jnp.dot(second_low, up_all, preferred_element_type=jnp.float32)
    hidden = gelu_exact(pre).astype(jnp.bfloat16)
    block_out = (middle + cols_product(hidden, down_all)).astype(jnp.bfloat16)
    grad_hidden = jnp.dot(grad_out, down_all, preferred_element_type=jnp.float32)
    grad_pre = gelu_back(pre, grad_hidden).astype(jnp.bfloat16)
    down_full = rows_product(grad_out, hidden)
    up_full = rows_product(second_low, grad_pre)
    grad_second = cols_product(grad_pre, up_all)
    up_part, down_part = (
        lax.psum_scatter(
            up_full.astype(jnp.bfloat16), "seq", scatter_dimension=1, tiled=True
        ).astype(jnp.float32),
        lax.psum_scatter(
            down_full.astype(jnp.bfloat16), "seq", scatter_dimension=1, tiled=True
        ).astype(jnp.float32),
    )
    up_grad, down_grad = (
        lax.psum(up_part.astype(jnp.bfloat16), "pos").astype(jnp.float32),
        lax.psum(down_part.astype(jnp.bfloat16), "pos").astype(jnp.float32),
    )
    second_back = jax.vjp(layer_norm, middle, second_gain, second_bias)[1]
    grad_middle_part, second_gain_part, second_bias_part = second_back(grad_second)
    grad_middle = grad_float + grad_middle_part
    grad_branch = grad_middle.astype(jnp.bfloat16)
    proj_part = rows_product(attended_low, grad_branch)
    grad_attended = (
        cols_product(grad_branch, w_out)
        .astype(jnp.bfloat16)
        .reshape(seqs_here, local_len, heads, head_dim)
    )

    def backward_block(packed):
        query_blk, keys_blk, values_blk, query_lab, key_lab, log_blk, grad_blk = packed
        scores = scores_for(query_blk, keys_blk, query_lab, key_lab)
        probs = jnp.exp(scores - log_blk)
        grad_probs = jnp.einsum(
            "bqhd,bkhd->bhqk", grad_blk, values_blk, preferred_element_type=jnp.float32
        )
        grad_values = jnp.einsum(
            "bhqk,bqhd->bkhd",
            probs.astype(jnp.bfloat16),
            grad_blk,
            preferred_element_type=jnp.float32,
        )
        inner = jnp.sum(probs * grad_probs, axis=-1, keepdims=True)
        grad_scores = (probs * (grad_probs - inner) * scale).astype(jnp.bfloat16)
        grad_query = jnp.einsum(
            "bhqk,bkhd->bqhd", grad_scores, keys_blk, preferred_element_type=jnp.float32
        )
        grad_keys = jnp.einsum(
            "bhqk,bqhd->bkhd", grad_scores, query_blk, preferred_element_type=jnp.float32
        )
        return (grad_query, grad_keys, grad_values)

    grad_query, grad_keys, grad_values = lax.map(
        backward_block,
        (
            split(query),
            split(keys_four),
            split(values_four),
            split(query_marks),
            split(segment_ids),
            log_totals,
            split(grad_attended),
        ),
    )
    grad_keys = grad_keys.reshape(seqs_here, full_len, width)
    grad_values = grad_values.reshape(seqs_here, full_len, width)
    keys_grad, values_grad = (
        lax.psum_scatter(
            grad_keys.astype(jnp.bfloat16), "pos", scatter_dimension=1, tiled=True
        ).astype(jnp.float32),
        lax.psum_scatter(
            grad_values.astype(jnp.bfloat16), "pos", scatter_dimension=1, tiled=True
        ).astype(jnp.float32),
    )
    norm_back = jax.vjp(qk_norms, raw_query, raw_keys, query_gain, key_gain)[1]
    grad_raw_query, grad_raw_keys, query_gain_part, key_gain_part = norm_back(
        (
            grad_query.reshape(rows_here, heads, head_dim),
            keys_grad.reshape(rows_here, heads, head_dim),
        )
    )
    grad_mixed = (
        jnp.stack(
            [grad_raw_query, grad_raw_keys, values_grad.reshape(rows_here, heads, head_dim)], axis=1
        )
        .reshape(rows_here, 3 * width)
        .astype(jnp.bfloat16)
    )
    qkv_part = rows_product(normed_low, grad_mixed)
    grad_normed = cols_product(grad_mixed, w_qkv)
    first_back = jax.vjp(layer_norm, inputs, first_gain, first_bias)[1]
    grad_input_part, first_gain_part, first_bias_part = first_back(grad_normed)
    input_grad = (grad_middle + grad_input_part).reshape(seqs_here, local_len, width)
    (
        qkv_grad,
        proj_grad,
        first_gain_grad,
        first_bias_grad,
        query_gain_grad,
        key_gain_grad,
        second_gain_grad,
        second_bias_grad,
    ) = lax.psum(
        (
            qkv_part,
            proj_part,
            first_gain_part,
            first_bias_part,
            query_gain_part,
            key_gain_part,
            second_gain_part,
            second_bias_part,
        ),
        ("pos", "seq"),
    )
    return (
        block_out.reshape(seqs_here, local_len, width),
        input_grad,
        first_gain_grad,
        first_bias_grad,
        qkv_grad,
        query_gain_grad,
        key_gain_grad,
        proj_grad,
        second_gain_grad,
        second_bias_grad,
        up_grad,
        down_grad,
    )


def solution(mesh):
    placed = (
        P("seq", "pos", None),
        P("seq", None),
        P(),
        P(),
        P(),
        P(),
        P(),
        P(),
        P(),
        P(),
        P(None, "seq"),
        P(None, "seq"),
        P("seq", "pos", None),
    )
    return jax.shard_map(
        local,
        mesh=mesh,
        in_specs=placed,
        out_specs=(
            P("seq", "pos", None),
            P("seq", "pos", None),
            P(),
            P(),
            P(),
            P(),
            P(),
            P(),
            P(),
            P(),
            P(None, "seq"),
            P(None, "seq"),
        ),
        check_vma=False,
    )
```

profile of v0, /device:TPU:0, one launch (start us, length us, event | category | flops | bytes accessed | tf_op | source)
XLA Modules:
  0.0 738.9 jit_solution(17519455962714971245)
XLA Ops:
  11.4 5.8 copy.30
  31.0 25.8 %all-gather.7.cloned.1.call-done = bf16[1,1024,768]{1,2,0:T(8,128)(2,1)} async-done(((bf16[1,512,768]{1,2,0:T(8,128)(2,1)}), bf16[1,1024,768]{1,2,0:T(8,128)(2,1)}) %all-gather.7.cloned.1.call-update) | async-done | bytes 1572880 | tf_op jit(solution)/shard_map/all_gather | solution.py:100
  56.7 15.4 %fusion.3 = (f32[12,512]{1,0:T(8,128)S(1)}, f32[12,512,1024]{2,1,0:T(8,128)}) fusion(pred[512,1024]{1,0:T(8,128)(4,1)S(1)} %broadcast_compare_fusion, bf16[1024,12,64]{0,2,1:T(8,128)(2,1)} %bitcast.180, f32[512,3,12,64]{0,3,2,1:T(8,128)} %copy-done.2, f32[64]{0:T(128)S(1)} %copy-done.49, f32[512,12]{0,1:T(8,128)S(1)} %fusion.60, ...), kind=kOutput, calls=%fused_computation.9 | convolution fusion | flops 825747456 | bytes 28909824 | tf_op jit(solution)/shard_map/while/body/eval_jaxpr/bqhd,bkhd->bhqk/dot_general | solution.py:108
  72.1 12.0 %fusion.2 = f32[12,512]{1,0:T(8,128)S(1)} fusion(f32[12,512,1024]{2,1,0:T(8,128)} %get-tuple-element.103, f32[12,512]{1,0:T(8,128)S(1)} %get-tuple-element.102, pred[512,1024]{1,0:T(8,128)(4,1)S(1)} %broadcast_compare_fusion), kind=kLoop, calls=%fused_computation.8 | loop fusion | flops 25159680 | bytes 25739264 | tf_op jit(solution)/shard_map/while/body/eval_jaxpr/reduce_sum | solution.py:119
  86.1 11.8 %fusion.48 = bf16[12,64,512]{2,1,0:T(8,128)(2,1)S(1)} fusion(bf16[1024,12,64]{0,2,1:T(8,128)(2,1)} %bitcast.174, f32[12,512,1024]{2,1,0:T(8,128)} %get-tuple-element.103, f32[12,512]{1,0:T(8,128)S(1)} %fusion.2, f32[12,512]{1,0:T(8,128)S(1)} %get-tuple-element.102, pred[512,1024]{1,0:T(8,128)(4,1)S(1)} %broadcast_compare_fusion), kind=kOutput, calls=%fused_computation.90 | convolution fusion | flops 837156864 | bytes 28098560 | tf_op jit(solution)/shard_map/while/body/eval_jaxpr/bhqk,bkhd->bqhd/dot_general | solution.py:121
  100.0 41.5 %all-gather.9.cloned.1.call-done = bf16[768,3072]{0,1:T(8,128)(2,1)} async-done(((bf16[768,192]{0,1:T(8,128)(2,1)}), bf16[768,3072]{0,1:T(8,128)(2,1)}) %all-gather.9.cloned.1.call-update) | async-done | bytes 4718608 | tf_op jit(solution)/shard_map/all_gather | solution.py:142
  141.5 19.9 %multiply_convert_fusion.1 = (bf16[512,3072]{1,0:T(8,128)(2,1)}, f32[512,3072]{1,0:T(8,128)}, f32[512,3072]{1,0:T(8,128)}) fusion(bf16[768,3072]{0,1:T(8,128)(2,1)} %all-gather.9.cloned.1.call-done, f32[512,768]{1,0:T(8,128)S(1)} %get-tuple-element.105, f32[768]{0:T(1024)} %param.22, f32[768]{0:T(1024)} %param.21, f32[512]{0:T(512)S(1)} %fusion.63, ...), kind=kOutput, calls=%fused_computation.18 | convolution fusion | flops 2520121344 | bytes 22030336 | tf_op jit(solution)/shard_map/dot_general | solution.py:145
  161.4 33.9 %all-gather.11.cloned.1.call-done = bf16[768,3072]{0,1:T(8,128)(2,1)} async-done(((bf16[768,192]{0,1:T(8,128)(2,1)}), bf16[768,3072]{0,1:T(8,128)(2,1)}) %all-gather.11.cloned.1.call-update) | async-done | bytes 4718608 | tf_op jit(solution)/shard_map/all_gather | solution.py:143
  195.4 10.4 %add_convert_fusion = bf16[512,3072]{1,0:T(8,128)(2,1)S(1)} fusion(f32[512,3072]{1,0:T(8,128)} %get-tuple-element.98, f32[512,3072]{1,0:T(8,128)} %get-tuple-element.106, bf16[768,3072]{0,1:T(8,128)(2,1)} %all-gather.11.cloned.1.call-done, bf16[1,512,768]{2,1,0:T(8,128)(2,1)} %param.25), kind=kOutput, calls=%fused_computation.17 | convolution fusion | flops 2437939200 | bytes 21233664 | tf_op jit(solution)/shard_map/dot_general | solution.py:148
  215.3 11.5 %fusion.89 = f32[12,512,1024]{2,1,0:T(8,128)} fusion(bf16[512,12,64]{0,2,1:T(8,128)(2,1)S(1)} %bitcast.172, bf16[1024,12,64]{0,2,1:T(8,128)(2,1)} %bitcast.175), kind=kOutput, calls=%fused_computation.141 | convolution fusion | flops 805306368 | bytes 27525120 | tf_op jit(solution)/shard_map/while/body/eval_jaxpr/bqhd,bkhd->bhqk/dot_general | solution.py:180
  226.8 54.4 %fusion.28 = bf16[12,64,1024]{2,1,0:T(8,128)(2,1)} fusion(f32[12,512,1024]{2,1,0:T(8,128)} %fusion.89, f32[12,512]{1,0:T(8,128)S(1)} %copy-done.41, f32[12,512,1024]{2,1,0:T(8,128)} %get-tuple-element.103, pred[512,1024]{1,0:T(8,128)(4,1)} %copy-done.12, f32[512,3,12,64]{0,3,2,1:T(8,128)} %copy-done.2, f32[64]{0:T(128)S(1)} %copy-done.49, ...), kind=kOutput, calls=%fused_computation.51 | convolution fusion | flops 876878848 | bytes 104989184 | tf_op jit(solution)/shard_map/while/body/eval_jaxpr/bhqk,bqhd->bkhd/dot_general | solution.py:194
  281.3 6.9 convolution_convert_fusion.1
  289.3 6.8 fusion.21
  297.1 13.0 %fusion.31 = bf16[12,64,1024]{2,1,0:T(8,128)(2,1)} fusion(bf16[512,12,64]{0,2,1:T(8,128)(2,1)S(1)} %bitcast.173, f32[12,512]{1,0:T(8,128)S(1)} %copy-done.41, f32[12,512,1024]{2,1,0:T(8,128)} %get-tuple-element.103, pred[512,1024]{1,0:T(8,128)(4,1)S(1)} %copy-done.13), kind=kOutput, calls=%fused_computation.52 | convolution fusion | flops 831258624 | bytes 28073984 | tf_op jit(solution)/shard_map/while/body/eval_jaxpr/bhqk,bqhd->bkhd/dot_general | solution.py:183
  315.0 53.7 %multiply_reduce_fusion.4 = (f32[512,12]{0,1:T(8,128)S(1)}, f32[512,12]{0,1:T(8,128)S(1)}, f32[12,64,512]{2,1,0:T(8,128)}) fusion(f32[512,3,12,64]{0,3,2,1:T(8,128)} %copy-done.2, f32[64]{0:T(128)S(1)} %copy-done.49, f32[512,12]{0,1:T(8,128)S(1)} %copy-done.27, f32[512,12,64]{0,2,1:T(8,128)S(1)} %bitcast.169, f32[64]{0:T(128)S(1)} %copy-done.50, ...), kind=kOutput, calls=%fused_computation.79 | convolution fusion | flops 877652992 | bytes 109757440 | tf_op jit(solution)/shard_map/while/body/eval_jaxpr/bhqk,bkhd->bqhd/dot_general | solution.py:191
  376.8 9.2 %reduce-scatter.9.cloned.1.call-done = bf16[768,192]{0,1:T(8,128)(2,1)} async-done(((bf16[768,3072]{0,1:T(8,128)(2,1)}), bf16[768,192]{0,1:T(8,128)(2,1)}) %reduce-scatter.9.cloned.1.call-update) | async-done | bytes 294928 | tf_op jit(solution)/shard_map/reduce_scatter | solution.py:154
  386.0 78.7 %reduce-scatter.11.cloned.1.call-done = bf16[768,192]{0,1:T(8,128)(2,1)} async-done(((bf16[768,3072]{0,1:T(8,128)(2,1)}), bf16[768,192]{0,1:T(8,128)(2,1)}) %reduce-scatter.11.cloned.1.call-update) | async-done | bytes 294928 | tf_op jit(solution)/shard_map/reduce_scatter | solution.py:157
  465.0 27.9 %reduce-scatter.7.cloned.1.call-done = bf16[1,512,768]{1,2,0:T(8,128)(2,1)} async-done(((bf16[1,1024,768]{1,2,0:T(8,128)(2,1)}), bf16[1,512,768]{1,2,0:T(8,128)(2,1)}) %reduce-scatter.7.cloned.1.call-update) | async-done | bytes 786448 | tf_op jit(solution)/shard_map/reduce_scatter | solution.py:217
  496.0 5.3 fusion.58
  502.7 6.9 fusion.49
  510.1 5.0 fusion.83
  517.0 41.0 %all-reduce = (f32[768]{0:T(1024)}, f32[768]{0:T(1024)}, f32[64]{0:T(128)}, f32[64]{0:T(128)}, f32[768]{0:T(1024)}, /*index=5*/f32[768]{0:T(1024)}) all-reduce(f32[768]{0:T(1024)S(1)} %get-tuple-element.80, f32[768]{0:T(1024)S(1)} %get-tuple-element.83, ...), channel_id=1, replica_groups=mesh['pos'=2,'seq'=16] {'pos','seq'}, use_global_device_ids=true, to_apply=%region_22.23 | all-reduce | flops 3200 | bytes 25600 | tf_op jit(solution)/shard_map/psum | solution.py:249
  565.0 158.7 %all-reduce.6.cloned.1.call-done = (f32[768,2304]{1,0:T(8,128)}, f32[768,768]{1,0:T(8,128)}) async-done(((f32[768,2304]{1,0:T(8,128)}, f32[768,768]{1,0:T(8,128)}), (f32[768,2304]{1,0:T(8,128)}, f32[768,768]{1,0:T(8,128)})) %all-reduce.6.cloned.1.call-update) | async-done | bytes 9437200 | tf_op jit(solution)/shard_map/psum | solution.py:249
  723.7 6.6 copy.37
  (190 shorter events, 61.6 us)
Async XLA Ops:
  7.2 90.8 %copy-start = (bf16[768,768]{1,0:T(8,128)(2,1)S(1)}, bf16[768,768]{1,0:T(8,128)(2,1)}, u32[]{:S(2)}) copy-start(bf16[768,768]{1,0:T(8,128)(2,1)} %param.20) | copy-start | bytes 3538948
  7.2 49.5 %all-gather.7.cloned.1.call-start = ((), (), s32[]{:S(2)}) async-start(), calls=%async_computation.5 | async-start | bytes 2359296 | tf_op jit(solution)/shard_map/all_gather | solution.py:100
  22.1 34.6 %copy-start.26 = (f32[512,12]{0,1:T(8,128)}, f32[512,12]{0,1:T(8,128)S(1)}, u32[]{:S(2)}) copy-start(f32[512,12]{0,1:T(8,128)S(1)} %get-tuple-element.111) | copy-start | bytes 73732
  26.6 30.1 %copy-start.49 = (f32[64]{0:T(128)S(1)}, f32[64]{0:T(128)}, u32[]{:S(2)}) copy-start(f32[64]{0:T(128)} %param.18) | copy-start | bytes 772
  26.7 59.4 %all-gather.5.cloned.1.call-start = ((), (), s32[]{:S(2)}) async-start(), calls=%async_computation.4 | async-start | bytes 2359296 | tf_op jit(solution)/shard_map/all_gather | solution.py:101
  29.1 112.4 %all-gather.9.cloned.1.call-start = ((), (), s32[]{:S(2)}) async-start(), calls=%async_computation.6 | async-start | bytes 5013504 | tf_op jit(solution)/shard_map/all_gather | solution.py:142
  29.9 165.5 %all-gather.11.cloned.1.call-start = ((), (), s32[]{:S(2)}) async-start(), calls=%async_computation.7 | async-start | bytes 5013504 | tf_op jit(solution)/shard_map/all_gather | solution.py:143
  30.5 283.1 %reduce-scatter.5.cloned.1.call-start = ((), (), s32[]{:S(2)}) async-start(), calls=%async_computation.8 | async-start | bytes 2359296 | tf_op jit(solution)/shard_map/reduce_scatter | solution.py:214
  30.5 41.6 %copy-start.29 = (f32[512,12]{0,1:T(8,128)}, f32[512,12]{0,1:T(8,128)S(1)}, u32[]{:S(2)}) copy-start(f32[512,12]{0,1:T(8,128)S(1)} %fusion.60) | copy-start | bytes 73732
  30.9 55.1 %copy-start.12 = (pred[512,1024]{1,0:T(8,128)(4,1)}, pred[512,1024]{1,0:T(8,128)(4,1)S(1)}, u32[]{:S(2)}) copy-start(pred[512,1024]{1,0:T(8,128)(4,1)S(1)} %broadcast_compare_fusion) | copy-start | bytes 1572868
  98.9 182.4 %copy-start.9 = (f32[512,768]{1,0:T(8,128)}, f32[512,768]{1,0:T(8,128)S(1)}, u32[]{:S(2)}) copy-start(f32[512,768]{1,0:T(8,128)S(1)} %get-tuple-element.105) | copy-start | bytes 4718596
  226.8 54.5 %copy-start.54 = (f32[768]{0:T(1024)S(1)}, f32[768]{0:T(1024)}, u32[]{:S(2)}) copy-start(f32[768]{0:T(1024)} %param.21) | copy-start | bytes 9220
  226.8 54.5 %copy-start.56 = (f32[768]{0:T(1024)S(1)}, f32[768]{0:T(1024)}, u32[]{:S(2)}) copy-start(f32[768]{0:T(1024)} %param.22) | copy-start | bytes 9220
  281.2 104.8 %reduce-scatter.9.cloned.1.call-start = ((), (), s32[]{:S(2)}) async-start(), calls=%async_computation.10 | async-start | bytes 5013504 | tf_op jit(solution)/shard_map/reduce_scatter | solution.py:154
  288.2 176.5 %reduce-scatter.11.cloned.1.call-start = ((), (), s32[]{:S(2)}) async-start(), calls=%async_computation.11 | async-start | bytes 5013504 | tf_op jit(solution)/shard_map/reduce_scatter | solution.py:157
  296.1 14.2 %copy-start.19 = (bf16[512,768]{1,0:T(8,128)(2,1)S(1)}, bf16[512,768]{1,0:T(8,128)(2,1)}, u32[]{:S(2)}) copy-start(bf16[512,768]{1,0:T(8,128)(2,1)} %copy-done.18) | copy-start | bytes 2359300
  296.1 196.8 %reduce-scatter.7.cloned.1.call-start = ((), (), s32[]{:S(2)}) async-start(), calls=%async_computation.9 | async-start | bytes 2359296 | tf_op jit(solution)/shard_map/reduce_scatter | solution.py:217
  310.2 251.1 %all-reduce.8.cloned.1.call-start = ((), (), s32[]{:S(2)}) async-start(), calls=%async_computation.13 | async-start | bytes 1179648 | tf_op jit(solution)/shard_map/psum | solution.py:162
  315.0 53.7 %copy-start.36 = (f32[512,12]{0,1:T(8,128)S(1)}, f32[512,12]{0,1:T(8,128)}, u32[]{:S(2)}) copy-start(f32[512,12]{0,1:T(8,128)} %copy-done.35) | copy-start | bytes 73732
  315.0 53.7 %copy-start.34 = (f32[512,12]{0,1:T(8,128)S(1)}, f32[512,12]{0,1:T(8,128)}, u32[]{:S(2)}) copy-start(f32[512,12]{0,1:T(8,128)} %copy-done.33) | copy-start | bytes 73732
  315.0 53.8 %copy-start.25 = (f32[512,12]{0,1:T(8,128)S(1)}, f32[512,12]{0,1:T(8,128)}, u32[]{:S(2)}) copy-start(f32[512,12]{0,1:T(8,128)} %copy-done.24) | copy-start | bytes 73732
  464.7 259.0 %all-reduce.6.cloned.1.call-start = ((), (), s32[]{:S(2)}) async-start(), calls=%async_computation.12 | async-start | bytes 18874368 | tf_op jit(solution)/shard_map/psum | solution.py:249
  515.1 43.0 %copy-start.6 = (f32[512,768]{1,0:T(8,128)S(1)}, f32[512,768]{1,0:T(8,128)}, u32[]{:S(2)}) copy-start(f32[512,768]{1,0:T(8,128)} %copy-done.5) | copy-start | bytes 4718596
  515.1 42.9 %copy-start.16 = (bf16[1,512,768]{2,1,0:T(8,128)(2,1)S(1)}, bf16[1,512,768]{2,1,0:T(8,128)(2,1)}, u32[]{:S(2)}) copy-start(bf16[1,512,768]{2,1,0:T(8,128)(2,1)} %param.25) | copy-start | bytes 2359300
  (46 other events, 215.8 us)
Sparse Core Ops, SparseCore 0:
  26.8 29.8 all-gather.6
  58.9 27.1 all-gather.4
  88.4 53.1 all-gather.8
  143.7 51.6 all-gather.10
  281.3 24.6 reduce-scatter.4
  310.3 75.5 reduce-scatter.8
  389.8 74.7 reduce-scatter.10
  467.5 25.3 reduce-scatter.6
  495.2 30.2 all-reduce.7
  531.9 191.7 all-reduce.5
where the time goes:
time: 747 us; the launch traced here: 739 us
  waiting for transfers between devices  379 us (51%)
  matrix products  234 us (31%)
  blocking collectives  41 us (5%)
  other arithmetic  38.5 us (5%)
  local copies, waits for them, and re-layouts  29.9 us (4%)
  between operations  15.4 us (2%)
    psum x1, waiting for transfers between devices, local(): lax.psum((qkv_part, proj_part, first_gain_part, first_bias_part, query_ga...  159 us
    reduce_scatter x1, waiting for transfers between devices, local(): lax.psum_scatter(down_full.astype(jnp.bfloat16), 'seq', scatter_dimension...  78.7 us
    dot_general x1, matrix products, backward_block(): jnp.einsum('bhqk,bqhd->bkhd', grad_scores, query_blk, preferred_element_t...  54.4 us
    dot_general x1, matrix products, backward_block(): jnp.einsum('bhqk,bkhd->bqhd', grad_scores, keys_blk, preferred_element_ty...  53.7 us
    all_gather x1, waiting for transfers between devices, local(): lax.all_gather(w_up, 'seq', axis=1, tiled=True)  41.5 us
    psum x1, blocking collectives, local(): lax.psum((qkv_part, proj_part, first_gain_part, first_bias_part, query_ga...  41 us
    all_gather x1, waiting for transfers between devices, local(): lax.all_gather(w_down, 'seq', axis=1, tiled=True)  33.9 us
    reduce_scatter x1, waiting for transfers between devices, local(): lax.psum_scatter(grad_values.astype(jnp.bfloat16), 'pos', scatter_dimensi...  27.9 us
  transfers between devices with their start and end apart: 10, of which 8 were waited for; matrix products, arithmetic and copies ran while one was open for 25% of the time, Pallas kernels for 0%

commit v1 on v0

--- a/solution.py
+++ b/solution.py
@@ -1,9 +1,730 @@
+import functools
 import jax
 import jax.numpy as jnp
 from jax import lax
+from jax.experimental import pallas as pl
+from jax.experimental.pallas import tpu as pltpu
 from jax.sharding import PartitionSpec as P
 
 EPS = 1e-06
+F32 = jnp.float32
+BF16 = jnp.bfloat16
+LOG2E = 1.4426950408889634
+BIG = 16384.0
+TILE = 256
+NT = (((1,), (1,)), ((), ()))
+NN = (((1,), (0,)), ((), ()))
+TN = (((0,), (0,)), ((), ()))
+
+
+def dot(a, b, dims=NN):
+    return lax.dot_general(a, b, dims, preferred_element_type=F32)
+
+
+def two(x):
+    hi = x.astype(BF16)
+    return hi, (x - hi.astype(F32)).astype(BF16)
+
+
+def group_sum(x, ones):
+    hi, lo = two(x)
+    return dot(hi, ones) + dot(lo, ones)
+
+
+def rows_norm(x):
+    average = jnp.mean(x, axis=-1, keepdims=True)
+    centred = x - average
+    spread = jnp.mean(centred * centred, axis=-1, keepdims=True)
+    scale = lax.rsqrt(spread + EPS)
+    return centred * scale, scale
+
+
+def tile_of(i, size=TILE):
+    return pl.ds(pl.multiple_of(i * size, size), size)
+
+
+def fwd_body(own, rem, fq, fk, g1, b1, wqkv, qg, kg, wout, g2, b2, ones,
+             normed, kk, vv, rq, rk, qaug, att, mid, sec, qq):
+    n, width = own.shape
+    hd = width // (width // 64)
+    cols = ones.shape[0]
+
+    def project(x, base, queries):
+        rows = tile_of(base)
+        low = (rows_norm(x)[0] * g1[...] + b1[...]).astype(BF16)
+        normed[rows, :] = low
+        for block in range(0 if queries else width // cols, 3 * width // cols):
+            raw = dot(low, wqkv[:, block * cols:(block + 1) * cols])
+            part, at = divmod(block * cols, width)
+            lanes = slice(at, at + cols)
+            if part == 2:
+                vv[rows, lanes] = raw.astype(BF16)
+                continue
+            centred = raw - group_sum(raw, ones[...]) * (1 / 64)
+            scale = lax.rsqrt(group_sum(centred * centred, ones[...]) * (1 / 64) + EPS)
+            if part == 0:
+                qq[rows, lanes] = (centred * scale * qg[:, lanes]).astype(BF16)
+                rq[rows, lanes] = scale
+            else:
+                kk[rows, lanes] = (centred * scale * kg[:, lanes]).astype(BF16)
+                rk[rows, lanes] = scale
+
+    def own_tile(i, c):
+        project(own[tile_of(i), :].astype(F32), i, True)
+        return c
+
+    def rem_tile(i, c):
+        project(rem[tile_of(i), :].astype(F32), i + n // TILE, False)
+        return c
+
+    lax.fori_loop(0, n // TILE, own_tile, 0)
+    lax.fori_loop(0, n // TILE, rem_tile, 0)
+
+    def pair(p, c):
+        lanes = tile_of(p, 128)
+        k, v = kk[:, lanes], vv[:, lanes]
+        feat = fk[...]
+        low_k = lax.broadcasted_iota(jnp.int32, k.shape, 1) < 64
+        one = jnp.ones_like(v)
+        ks = (jnp.where(low_k, k, feat), jnp.where(low_k, feat, k))
+        vs = (jnp.where(low_k, v, one), jnp.where(low_k, one, v))
+        lane = lax.broadcasted_iota(jnp.int32, (TILE, 128), 1)
+        low = lane < 64
+
+        def tile(t, c):
+            rows = tile_of(t)
+            q, mask = qq[rows, lanes], fq[rows, :]
+            res = []
+            for a in range(2):
+                qa = jnp.where(low, q, mask) if a == 0 else jnp.where(low, mask, q)
+                e = jnp.exp2(dot(qa, ks[a], NT) * (LOG2E / 8)).astype(BF16)
+                o = dot(e, vs[a])
+                res.append(o)
+                shift = jnp.log(o) * -8.0
+                hi, lo = two(shift)
+                lo2 = (shift - hi.astype(F32) - lo.astype(F32)).astype(BF16)
+                s = 64 * (1 - a)
+                qaug[p * 2 + a, rows, :] = jnp.where(
+                    lane == s + 6, hi, jnp.where(lane == s + 7, lo, jnp.where(lane == s + 8, lo2, qa)))
+            num = jnp.where(low, res[0], res[1])
+            den = pltpu.roll(jnp.where(low, res[1], res[0]), 64, 1)
+            att[rows, lanes] = (num / den).astype(BF16)
+            return c
+
+        lax.fori_loop(0, n // TILE, tile, 0)
+        return c
+
+    lax.fori_loop(0, width // 128, pair, 0)
+
+    def out_tile(i, c):
+        rows = tile_of(i)
+        m = own[rows, :].astype(F32) + dot(att[rows, :], wout[...])
+        mid[rows, :] = m
+        sec[rows, :] = (rows_norm(m)[0] * g2[...] + b2[...]).astype(BF16)
+        return c
+
+    lax.fori_loop(0, n // TILE, out_tile, 0)
+
+
+def bwd_body(own, rem, gsec, mid, gy, fk, g1, wqkv, qg, kg, wout, g2, ones, swap,
+             normed, kk, vv, rq, rk, qaug, att,
+             gall, gn_own, gn_rem, gmid, small, gbr, gat, gmix, dk, dv):
+    n, width = own.shape
+    pairs = width // 128
+    small[...] = jnp.zeros_like(small)
+
+    def mid_tile(i, c):
+        rows = tile_of(i)
+        xh, r = rows_norm(mid[rows, :])
+        dy = gsec[rows, :]
+        small[2:3, :] += jnp.sum(dy * xh, axis=0, keepdims=True)
+        small[3:4, :] += jnp.sum(dy, axis=0, keepdims=True)
+        gd = dy * g2[...]
+        dx = r * (gd - jnp.mean(gd, -1, keepdims=True) - xh * jnp.mean(gd * xh, -1, keepdims=True))
+        gm = gy[rows, :].astype(F32) + dx
+        gmid[rows, :] = gm
+        low = gm.astype(BF16)
+        gbr[rows, :] = low
+        gat[rows, :] = dot(low, wout[...], NT).astype(BF16)
+        return c
+
+    lax.fori_loop(0, n // TILE, mid_tile, 0)
+
+    def proj_tile(i, c):
+        cols = tile_of(i)
+        gall[cols, 3 * width:] = dot(att[:, cols], gbr[...], TN).astype(BF16)
+        return c
+
+    lax.fori_loop(0, width // TILE, proj_tile, 0)
+
+    def pair(p, c):
+        lanes = tile_of(p, 128)
+        lane = lax.broadcasted_iota(jnp.int32, (n, 128), 1)
+        low_q = lane < 64
+        do = gat[:, lanes]
+        delta = -group_sum(do.astype(F32) * att[:, lanes].astype(F32), swap[...])
+        hi, lo = two(delta)
+        zero = jnp.zeros_like(do)
+        das = []
+        for a in range(2):
+            s = 64 * (1 - a)
+            extra = jnp.where(lane == s, hi, jnp.where(lane == s + 1, lo, zero))
+            das.append(jnp.where(low_q, do, extra) if a == 0 else jnp.where(low_q, extra, do))
+        low = lax.broadcasted_iota(jnp.int32, (TILE, 128), 1) < 64
+
+        def keys(t, acc):
+            rows = tile_of(t)
+            k, v, feat = kk[rows, lanes], vv[rows, lanes], fk[rows, :]
+            one = jnp.ones_like(v)
+            dks, dvs, out = [], [], []
+            for a in range(2):
+                ka = jnp.where(low, k, feat) if a == 0 else jnp.where(low, feat, k)
+                va = jnp.where(low, v, one) if a == 0 else jnp.where(low, one, v)
+                qa = qaug[p * 2 + a]
+                e = jnp.exp2(dot(ka, qa, NT) * (LOG2E / 8))
+                ds = (e * dot(va, das[a], NT)).astype(BF16)
+                dvs.append(dot(e.astype(BF16), das[a]))
+                dks.append(dot(ds, qa))
+                out.append(acc[a] + dot(ka, ds, TN))
+            dk[rows, :] = jnp.where(low, dks[0], dks[1])
+            gmix[rows, tile_of(p + 2 * pairs, 128)] = jnp.where(low, dvs[0], dvs[1]).astype(BF16)
+            return tuple(out)
+
+        zeros = jnp.zeros((128, n), F32)
+        acc = lax.fori_loop(0, 2 * n // TILE, keys, (zeros, zeros))
+        low_s = lax.broadcasted_iota(jnp.int32, (128, n), 0) < 64
+        dq = jnp.where(low_s, acc[0], acc[1]).T
+        gain = qg[:, lanes]
+
+        def norm_back(dy, y, r, gain):
+            dy = dy * 0.125
+            prod = dy * y.astype(F32)
+            gd = dy * gain
+            m1 = group_sum(gd, ones[...]) * (1 / 64)
+            m2 = group_sum(prod, ones[...]) * (1 / 64)
+            inv = 1.0 / gain
+            return r * (gd - m1 - y.astype(F32) * inv * m2), jnp.sum(prod, 0, keepdims=True) * inv
+
+        low_half = lane < 64
+        qa = jnp.where(low_half, qaug[p * 2], qaug[p * 2 + 1])
+        dx, gg = norm_back(dq, qa, rq[:, lanes], gain)
+        gmix[0:n, lanes] = dx.astype(BF16)
+        small[4:5, lanes] = gg
+        dx, gg = norm_back(dk[...], kk[:, lanes], rk[:, lanes], kg[:, lanes])
+        gmix[:, tile_of(p + pairs, 128)] = dx.astype(BF16)
+        small[5:6, lanes] = gg
+        return c
+
+    lax.fori_loop(0, pairs, pair, 0)
+
+    def qkv_tile(i, c):
+        cols = tile_of(i)
+        gall[cols, 0:width] = dot(normed[0:n, cols], gmix[0:n, 0:width], TN).astype(BF16)
+        for part in (1, 2):
+            at = slice(part * width, (part + 1) * width)
+            gall[cols, at] = dot(normed[:, cols], gmix[:, at], TN).astype(BF16)
+        return c
+
+    lax.fori_loop(0, width // TILE, qkv_tile, 0)
+
+    def gain_sums(x, gn):
+        xh, _ = rows_norm(x.astype(F32))
+        small[0:1, :] += jnp.sum(gn * xh, axis=0, keepdims=True)
+        small[1:2, :] += jnp.sum(gn, axis=0, keepdims=True)
+
+    def own_tile(i, c):
+        rows = tile_of(i)
+        gn = dot(gmix[rows, :], wqkv[...], NT)
+        gn_own[rows, :] = gn
+        gain_sums(own[rows, :], gn)
+        return c
+
+    def rem_tile(i, c):
+        rows, at = tile_of(i), tile_of(i + n // TILE)
+        gn = dot(gmix[at, width:], wqkv[:, width:], NT)
+        gn_rem[rows, :] = gn.astype(BF16)
+        gain_sums(rem[rows, :], gn)
+        return c
+
+    lax.fori_loop(0, n // TILE, own_tile, 0)
+    lax.fori_loop(0, n // TILE, rem_tile, 0)
+
+
+VM = pl.BlockSpec(memory_space=pltpu.VMEM)
+LIMIT = 60 * 1024 * 1024
+
+
+def sds(shape, dtype):
+    return jax.ShapeDtypeStruct(shape, dtype)
+
+
+def fwd_call(own, rem, fq, fk, g1, b1, wqkv, qg, kg, wout, g2, b2, ones):
+    n, width = own.shape
+    heads = width // 64
+    outs = (sds((2 * n, width), BF16), sds((2 * n, width), BF16), sds((2 * n, width), BF16),
+            sds((n, width), F32), sds((2 * n, width), F32), sds((heads, n, 128), BF16),
+            sds((n, width), BF16), sds((n, width), F32), sds((n, width), BF16))
+    return pl.pallas_call(
+        fwd_body, out_shape=outs, in_specs=[VM] * 13, out_specs=tuple([VM] * 9),
+        scratch_shapes=[pltpu.VMEM((n, width), BF16)],
+        compiler_params=pltpu.CompilerParams(vmem_limit_bytes=LIMIT),
+        name="fwd",
+    )(own, rem, fq, fk, g1, b1, wqkv, qg, kg, wout, g2, b2, ones)
+
+
+def bwd_call(*args):
+    own = args[0]
+    n, width = own.shape
+    outs = (sds((width, 4 * width), BF16), sds((n, width), F32),
+            sds((n, width), BF16), sds((n, width), F32), sds((8, width), F32))
+    return pl.pallas_call(
+        bwd_body, out_shape=outs, in_specs=[VM] * 21, out_specs=tuple([VM] * 5),
+        scratch_shapes=[pltpu.VMEM((n, width), BF16), pltpu.VMEM((n, width), BF16),
+                        pltpu.VMEM((2 * n, 3 * width), BF16), pltpu.VMEM((2 * n, 128), F32),
+                        pltpu.VMEM((8, 128), F32)],
+        compiler_params=pltpu.CompilerParams(vmem_limit_bytes=LIMIT),
+        name="bwd",
+    )(*args)
+
+
+def ring_places(n_seq):
+    s = lax.axis_index("seq")
+    core, chip = s % 2, s // 2
+    chips = n_seq // 2
+    half = chips // 2
+    odd = chip % 2
+    place = (1 - odd) * (chip // 2) + odd * (chips - 1 - chip // 2)
+
+    def device(p):
+        far = p // half
+        return ((1 - far) * 2 * p + far * (2 * (chips - 1 - p) + 1)) * 2 + core
+
+    right = device((place + 1) % chips)
+    left = device((place + chips - 1) % chips)
+    return core, place, right, left, s + 1 - 2 * core
+
+
+def copy_to(src, dst, send, recv, target):
+    return pltpu.make_async_remote_copy(
+        src_ref=src, dst_ref=dst, send_sem=send, recv_sem=recv, device_id=target,
+        device_id_type=pl.DeviceIdType.MESH)
+
+
+def greet(targets):
+    barrier = pltpu.get_barrier_semaphore()
+    for t in targets:
+        pl.semaphore_signal(barrier, inc=1, device_id=t, device_id_type=pl.DeviceIdType.MESH)
+    pl.semaphore_wait(barrier, len(targets))
+
+
+def ffn_body(n_seq, sec, gy, mid, w_own, out, gsec, grads,
+             sx, sg, wbuf, accin, accout, first, hid, gpre, blk, gs, prec,
+             wsend, wrecv, asend, arecv, psend, precv):
+    n, width = sec.shape
+    f = w_own.shape[1]
+    h = f // 2
+    chips = n_seq // 2
+    core, place, right, left, partner = ring_places(n_seq)
+    right, left, partner = {"seq": right}, {"seq": left}, {"seq": partner}
+    greet((right, left, partner))
+
+    shares = (copy_to(sec, sx.at[pl.ds(n, n)], psend.at[0], precv.at[0], partner),
+              copy_to(gy, sg.at[pl.ds(n, n)], psend.at[1], precv.at[1], partner))
+    parts = (copy_to(blk.at[pl.ds(n, n)], prec.at[0], psend.at[2], precv.at[2], partner),
+             copy_to(gs.at[pl.ds(n, n)], prec.at[1], psend.at[3], precv.at[3], partner))
+
+    def w_copy(d, s):
+        rows = pl.ds(d * h, h)
+        return copy_to(wbuf.at[s, :, rows], wbuf.at[s + 1, :, rows], wsend.at[d, s], wrecv.at[d, s],
+                       left if d else right)
+
+    def w_first(d):
+        rows = pl.ds(d * h, h)
+        return copy_to(w_own.at[:, rows], wbuf.at[1, :, rows], wsend.at[d, 0], wrecv.at[d, 0],
+                       left if d else right)
+
+    def a_copy(d, s):
+        rows = pl.ds(d * h, h)
+        return copy_to(accout.at[s - 1, :, rows], accin.at[s - 1, :, rows], asend.at[d, s - 1],
+                       arecv.at[d, s - 1], left if d else right)
+
+    for d in range(2):
+        w_first(d).start()
+    for c in shares:
+        c.start()
+    wbuf[0] = w_own[...]
+    sx[0:n, :] = sec[...]
+    sg[0:n, :] = gy[...]
+    blk[...] = jnp.zeros_like(blk)
+    gs[...] = jnp.zeros_like(gs)
+    for c in shares:
+        c.wait_recv()
+
+    def step(s, carry):
+        @pl.when(s > 0)
+        def _():
+            for d in range(2):
+                w_copy(d, s - 1).wait_recv()
+
+            @pl.when(s < chips - 1)
+            def _():
+                for d in range(2):
+                    w_copy(d, s).start()
+
+        def tile(i, c):
+            rows = tile_of(i)
+            up, down = wbuf[s, 0], wbuf[s, 1]
+            pre = dot(sx[rows, :], up, NT)
+            gh = dot(sg[rows, :], down, NT)
+            cdf = 0.5 + 0.5 * lax.erf(pre * 0.7071067811865476)
+            slope = cdf + pre * (jnp.exp(-0.5 * pre * pre) * 0.3989422804014327)
+            a = (pre * cdf).astype(BF16)
+            b = (gh * slope).astype(BF16)
+            hid[rows, :] = a
+            gpre[rows, :] = b
+            blk[rows, :] += dot(a, down)
+            gs[rows, :] += dot(b, up)
+            return c
+
+        lax.fori_loop(0, 2 * n // TILE, tile, 0)
+
+        @pl.when(s > 1)
+        def _():
+            for d in range(2):
+                a_copy(d, s - 1).wait_recv()
+
+        def block(j, c):
+            cols = tile_of(j)
+            for k, (lhs, rhs) in enumerate(((gpre, sx), (hid, sg))):
+                part = dot(lhs[...], rhs[:, cols], TN)
+
+                @pl.when(s == 0)
+                def _():
+                    first[k, :, cols] = part
+
+                @pl.when(s == 1)
+                def _():
+                    accout[0, k, :, cols] = part.astype(BF16)
+
+                @pl.when(s > 1)
+                def _():
+                    accout[s - 1, k, :, cols] = (part + accin[s - 2, k, :, cols].astype(F32)).astype(BF16)
+            return c
+
+        lax.fori_loop(0, width // TILE, block, 0)
+
+        @pl.when(s > 0)
+        def _():
+            for d in range(2):
+                a_copy(d, s).start()
+        return carry
+
+    lax.fori_loop(0, chips, step, 0)
+    for c in parts:
+        c.start()
+    for c in parts:
+        c.wait_recv()
+    out[...] = (mid[...] + (blk[0:n, :] + prec[0])).astype(BF16)
+    gsec[...] = gs[0:n, :] + prec[1]
+    for d in range(2):
+        a_copy(d, chips - 1).wait_recv()
+    grads[...] = (first[...] + accin[chips - 2].astype(F32)).astype(BF16)
+
+    def drain(s, c):
+        for d in range(2):
+            a_copy(d, s + 1).wait_send()
+
+            @pl.when(s > 0)
+            def _():
+                w_copy(d, s).wait_send()
+        return c
+
+    lax.fori_loop(0, chips - 1, drain, 0)
+    for d in range(2):
+        w_first(d).wait_send()
+    for c in shares + parts:
+        c.wait_send()
+
+
+def ffn_call(n_seq, sec, gy, mid, w_own):
+    n, width = sec.shape
+    f = w_own.shape[1]
+    chips = n_seq // 2
+    V, D = pltpu.VMEM, pltpu.SemaphoreType.DMA
+    return pl.pallas_call(
+        functools.partial(ffn_body, n_seq),
+        out_shape=(sds((n, width), BF16), sds((n, width), F32), sds((2, f, width), BF16)),
+        in_specs=[VM] * 4, out_specs=(VM,) * 3,
+        scratch_shapes=[
+            V((2 * n, width), BF16), V((2 * n, width), BF16), V((chips, 2, f, width), BF16),
+            V((chips - 1, 2, f, width), BF16), V((chips - 1, 2, f, width), BF16),
+            V((2, f, width), F32), V((2 * n, f), BF16), V((2 * n, f), BF16),
+            V((2 * n, width), F32), V((2 * n, width), F32), V((2, n, width), F32),
+            D((2, chips - 1)), D((2, chips - 1)), D((2, chips - 1)), D((2, chips - 1)), D((4,)), D((4,))],
+        compiler_params=pltpu.CompilerParams(
+            vmem_limit_bytes=LIMIT, collective_id=1, has_side_effects=True),
+        name="ffn",
+    )(sec, gy, mid, w_own)
+
+
+SPLIT = 2
+
+
+def sum_body(n_seq, g, small, own, gn_own, gn_rem, gmid, g1, out, sout, igrad,
+             pbuf, accin, accout, xin, xout, fin, srec, sring, gback,
+             psend, precv, asend, arecv, xsend, xrecv, fsend, frecv, qsend, qrecv, ssend, srecv, gsend, grecv):
+    rows, cols = g.shape
+    chips = n_seq // 2
+    half = rows // 2
+    cr = half // chips
+    cw = cols // (2 * SPLIT)
+    core, place, right, left, partner = ring_places(n_seq)
+    x = lax.axis_index("pos")
+    right, left, partner, across = {"seq": right}, {"seq": left}, {"seq": partner}, {"pos": 1 - x}
+    greet((right, left, partner, across))
+
+    def chunk(p):
+        return (p + 2 * chips) % chips
+
+    def at(d, k):
+        return pl.ds((d * SPLIT + k) * cw, cw)
+
+    def rows_of(c, p):
+        return pl.ds(pl.multiple_of(c * half + p * cr, cr), cr)
+
+    def p_copy(q):
+        return copy_to(g.at[rows_of(1 - core, q)], pbuf.at[q], psend.at[q], precv.at[q], partner)
+
+    def a_copy(d, k, s):
+        return copy_to(accout.at[s, d * SPLIT + k], accin.at[s, d * SPLIT + k], asend.at[s, d * SPLIT + k],
+                       arecv.at[s, d * SPLIT + k], left if d else right)
+
+    def x_copy(d, k):
+        i = d * SPLIT + k
+        return copy_to(xout.at[i], xin.at[i], xsend.at[i], xrecv.at[i], across)
+
+    def f_copy(d, k, s):
+        p = chunk(place + s) if d else chunk(place - s)
+        ref = fin.at[rows_of(core, p), at(d, k)]
+        return copy_to(ref, ref, fsend.at[s, d * SPLIT + k], frecv.at[s, d * SPLIT + k], left if d else right)
+
+    def f_recv(d, k, s):
+        p = chunk(place + s + 1) if d else chunk(place - s - 1)
+        ref = fin.at[rows_of(core, p), at(d, k)]
+        return copy_to(ref, ref, fsend.at[s, d * SPLIT + k], frecv.at[s, d * SPLIT + k], left if d else right)
+
+    def q_copy(d, k, s):
+        p = chunk(place + s) if d else chunk(place - s)
+        ref = fin.at[rows_of(core, p), at(d, k)]
+        return copy_to(ref, ref, qsend.at[s, d * SPLIT + k], qrecv.at[s, d * SPLIT + k], partner)
+
+    def q_recv(d, k, s):
+        p = chunk(place + s) if d else chunk(place - s)
+        ref = fin.at[rows_of(1 - core, p), at(d, k)]
+        return copy_to(ref, ref, qsend.at[s, d * SPLIT + k], qrecv.at[s, d * SPLIT + k], partner)
+
+    def s_copy(s):
+        return copy_to(sring.at[chunk(place - s)], sring.at[chunk(place - s)], ssend.at[s], srecv.at[s], right)
+
+    def s_recv(s):
+        p = chunk(place - s - 1)
+        return copy_to(sring.at[p], sring.at[p], ssend.at[s], srecv.at[s], right)
+
+    both = [(d, k) for k in range(SPLIT) for d in range(2)]
+    back = copy_to(gn_rem, gback, gsend.at[0], grecv.at[0], across)
+    small_p = copy_to(small, srec.at[0], gsend.at[1], grecv.at[1], partner)
+    small_x = copy_to(srec.at[1], srec.at[2], gsend.at[2], grecv.at[2], across)
+
+    def order(s):
+        return chunk(place - s), chunk(place + s)
+
+    small_p.start()
+    for s in range(1, chips // 2 + 1):
+        for q in order(s)[: 1 if 2 * s == chips else 2]:
+            p_copy(q).start()
+    p_copy(place).start()
+    back.start()
+
+    def part(d, k, q):
+        cs = at(d, k)
+        return g[rows_of(core, q), cs].astype(F32) + pbuf[q, :, cs].astype(F32)
+
+    def reduce_step(s, c):
+        @pl.when(s <= chips // 2)
+        def _():
+            p_copy(chunk(place - s)).wait_recv()
+
+            @pl.when(2 * s < chips)
+            def _():
+                p_copy(chunk(place + s)).wait_recv()
+
+        for d, k in both:
+            q = chunk(place + s) if d else chunk(place - s)
+
+            @pl.when(s == 1)
+            def _():
+                accout[s - 1, d * SPLIT + k] = part(d, k, q).astype(BF16)
+
+            @pl.when(s > 1)
+            def _():
+                a_copy(d, k, s - 2).wait_recv()
+                accout[s - 1, d * SPLIT + k] = (part(d, k, q) + accin[s - 2, d * SPLIT + k].astype(F32)).astype(BF16)
+
+            a_copy(d, k, s - 1).start()
+        return c
+
+    lax.fori_loop(1, chips, reduce_step, 0)
+    p_copy(place).wait_recv()
+    for d, k in both:
+        a_copy(d, k, chips - 2).wait_recv()
+        xout[d * SPLIT + k] = (part(d, k, place) + accin[chips - 2, d * SPLIT + k].astype(F32)).astype(BF16)
+        x_copy(d, k).start()
+    small_p.wait_recv()
+    srec[1] = small[...] + srec[0]
+    small_x.start()
+    back.wait_recv()
+    n = own.shape[0]
+
+    def norm_tile(i, c):
+        rs = tile_of(i)
+        xh, r = rows_norm(own[rs, :].astype(F32))
+        dy = (gn_own[rs, :] + gback[rs, :].astype(F32)) * g1[...]
+        dx = r * (dy - jnp.mean(dy, -1, keepdims=True) - xh * jnp.mean(dy * xh, -1, keepdims=True))
+        igrad[rs, :] = gmid[rs, :] + dx
+        return c
+
+    lax.fori_loop(0, n // TILE, norm_tile, 0)
+    small_x.wait_recv()
+    sring[place] = srec[1] + srec[2]
+    s_copy(0).start()
+    for d, k in both:
+        x_copy(d, k).wait_recv()
+        i = d * SPLIT + k
+        fin[rows_of(core, place), at(d, k)] = (xout[i].astype(F32) + xin[i].astype(F32)).astype(BF16)
+        f_copy(d, k, 0).start()
+        q_copy(d, k, 0).start()
+
+    def gather_step(s, c):
+        for d, k in both:
+            f_recv(d, k, s - 1).wait_recv()
+
+            @pl.when(s < chips - 1)
+            def _():
+                f_copy(d, k, s).start()
+
+            q_copy(d, k, s).start()
+        s_recv(s - 1).wait_recv()
+
+        @pl.when(s < chips - 1)
+        def _():
+            s_copy(s).start()
+        return c
+
+    lax.fori_loop(1, chips, gather_step, 0)
+
+    def finish(s, c):
+        for d, k in both:
+            q_recv(d, k, s).wait_recv()
+        return c
+
+    lax.fori_loop(0, chips, finish, 0)
+    total = sring[0]
+    for s in range(1, chips):
+        total = total + sring[s]
+    sout[...] = total
+
+    def widen(i, c):
+        rs = pl.ds(pl.multiple_of(i * 32, 32), 32)
+        out[rs, :] = fin[rs, :].astype(F32)
+        return c
+
+    lax.fori_loop(0, rows // 32, widen, 0)
+
+    def drain(s, c):
+        for d, k in both:
+            q_copy(d, k, s).wait_send()
+
+            @pl.when(s < chips - 1)
+            def _():
+                a_copy(d, k, s).wait_send()
+                f_copy(d, k, s).wait_send()
+
+        @pl.when(s < chips - 1)
+        def _():
+            s_copy(s).wait_send()
+        p_copy(s).wait_send()
+        return c
+
+    lax.fori_loop(0, chips, drain, 0)
+    for d, k in both:
+        x_copy(d, k).wait_send()
+    for c in (back, small_p, small_x):
+        c.wait_send()
+
+
+def sum_call(n_seq, g, small, own, gn_own, gn_rem, gmid, g1):
+    rows, cols = g.shape
+    n, width = own.shape
+    chips = n_seq // 2
+    cr, lanes, cw = rows // 2 // chips, 2 * SPLIT, cols // (2 * SPLIT)
+    V, D = pltpu.VMEM, pltpu.SemaphoreType.DMA
+    return pl.pallas_call(
+        functools.partial(sum_body, n_seq),
+        out_shape=(sds((rows, cols), F32), sds(small.shape, F32), sds((n, width), F32)),
+        in_specs=[VM] * 7, out_specs=(VM,) * 3,
+        scratch_shapes=[
+            V((chips, cr, cols), BF16), V((chips - 1, lanes, cr, cw), BF16), V((chips - 1, lanes, cr, cw), BF16),
+            V((lanes, cr, cw), BF16), V((lanes, cr, cw), BF16), V((rows, cols), BF16),
+            V((3,) + small.shape, F32), V((chips,) + small.shape, F32), V((n, width), BF16),
+            D((chips,)), D((chips,)), D((chips - 1, lanes)), D((chips - 1, lanes)), D((lanes,)), D((lanes,)),
+            D((chips - 1, lanes)), D((chips - 1, lanes)), D((chips, lanes)), D((chips, lanes)),
+            D((chips - 1,)), D((chips - 1,)), D((3,)), D((3,))],
+        compiler_params=pltpu.CompilerParams(
+            vmem_limit_bytes=LIMIT, collective_id=2, has_side_effects=True),
+        name="sums",
+    )(g, small, own, gn_own, gn_rem, gmid, g1)
+
+
+def features(marks):
+    lane = lax.broadcasted_iota(jnp.int32, (1, 128), 1) % 64
+    same = marks[:, None] == lane
+    extra = (lane >= 6) & (lane <= 8)
+    keys = jnp.where(extra, 1.0, jnp.where(same & (lane < 6), 1.0, 0.0)).astype(BF16)
+    query = jnp.where((lane < 6) & ~same, -BIG, 0.0).astype(BF16)
+    return query, keys
+
+
+def local_one(tokens, segment_ids, first_gain, first_bias, w_qkv, query_gain, key_gain, w_out,
+              second_gain, second_bias, w_up, w_down, out_grad):
+    _, n, width = tokens.shape
+    heads = width // query_gain.shape[0]
+    me = lax.axis_index("pos")
+    own = tokens[0]
+    rem = lax.ppermute(own, "pos", [(0, 1), (1, 0)])
+    marks = lax.dynamic_slice_in_dim(segment_ids[0], me * n, n)
+    far = lax.dynamic_slice_in_dim(segment_ids[0], (1 - me) * n, n)
+    fq, fk = features(marks)
+    fk = jnp.concatenate([fk, features(far)[1]], 0)
+    row = lambda v: v.reshape(1, -1)
+    qg, kg = row(jnp.tile(query_gain, heads)), row(jnp.tile(key_gain, heads))
+    group = jnp.arange(256) // 64
+    ones = (group[:, None] == group[None, :]).astype(BF16)
+    swap = (group[:128, None] != group[None, :128]).astype(BF16)
+    g1, b1, g2, b2 = row(first_gain), row(first_bias), row(second_gain), row(second_bias)
+    normed, kk, vv, rq, rk, qaug, att, mid, sec = fwd_call(
+        own, rem, fq, fk, g1, b1, w_qkv, qg, kg, w_out, g2, b2, ones)
+    gy = out_grad[0]
+    n_seq = lax.axis_size("seq")
+    w_own = jnp.stack([w_up.T, w_down.T])
+    block_out, gsec, grads = ffn_call(n_seq, sec, gy, mid, w_own)
+    g, gn_own, gn_rem, gmid, small = bwd_call(
+        own, rem, gsec, mid, gy, fk, g1, w_qkv, qg, kg, w_out, g2, ones[:128, :128], swap,
+        normed, kk, vv, rq, rk, qaug, att)
+    grads = lax.psum(grads, "pos").astype(F32)
+    g, small, input_grad = sum_call(n_seq, g, small, own, gn_own, gn_rem, gmid, g1)
+    fold = lambda v: v.reshape(heads, -1).sum(0)
+    return (block_out[None], input_grad[None], small[0], small[1], g[:, :3 * width], fold(small[4]), fold(small[5]),
+            g[:, 3 * width:], small[2], small[3], grads[0].T, grads[1].T)
 
 
 def layer_norm(rows, gain, shift):
@@ -276,38 +997,16 @@
 
 
 def solution(mesh):
-    placed = (
-        P("seq", "pos", None),
-        P("seq", None),
-        P(),
-        P(),
-        P(),
-        P(),
-        P(),
-        P(),
-        P(),
-        P(),
-        P(None, "seq"),
-        P(None, "seq"),
-        P("seq", "pos", None),
-    )
-    return jax.shard_map(
-        local,
-        mesh=mesh,
-        in_specs=placed,
-        out_specs=(
-            P("seq", "pos", None),
-            P("seq", "pos", None),
-            P(),
-            P(),
-            P(),
-            P(),
-            P(),
-            P(),
-            P(),
-            P(),
-            P(None, "seq"),
-            P(None, "seq"),
-        ),
-        check_vma=False,
-    )
+    placed = (P("seq", "pos", None), P("seq", None), P(), P(), P(), P(), P(), P(), P(), P(),
+              P(None, "seq"), P(None, "seq"), P("seq", "pos", None))
+    outs = (P("seq", "pos", None), P("seq", "pos", None), P(), P(), P(), P(), P(), P(), P(), P(),
+            P(None, "seq"), P(None, "seq"))
+
+    def step(*args):
+        def run(*local_args):
+            one = local_args[0].shape[0] == 1 and mesh.shape["pos"] == 2
+            return (local_one if one else local)(*local_args)
+
+        return jax.shard_map(run, mesh=mesh, in_specs=placed, out_specs=outs, check_vma=False)(*args)
+
+    return step

time: 747 us -> 310 us (0.41)
  waiting for transfers between devices: 379 us -> 5.08 us
  Pallas kernels: 0 us -> 255 us
  matrix products: 234 us -> 0 us
  blocking collectives: 41 us -> 0 us
  other arithmetic: 38.5 us -> 7.15 us
    pallas_call x0 -> x4, Pallas kernels: none -> 255 us  [the longest x1 104 us: ffn_call(): pl.pallas_call(functools.partial(ffn_body, n_seq), out_shape=(sds((n, wid...]
    dot_general x18 -> x0, matrix products: 234 us -> none  [the longest x1 54.4 us: backward_block(): jnp.einsum('bhqk,bqhd->bkhd', grad_scores, query_blk, preferred_element_t...]
    psum x2 -> x1, waiting for transfers between devices: 159 us -> 0.01 us  [local_one(): grads = lax.psum(grads, 'pos').astype(F32)]
    reduce_scatter x4 -> x0, waiting for transfers between devices: 116 us -> none  [the longest x1 78.7 us: local(): lax.psum_scatter(down_full.astype(jnp.bfloat16), 'seq', scatter_dimension...]
    all_gather x4 -> x0, waiting for transfers between devices: 103 us -> none  [the longest x1 41.5 us: local(): lax.all_gather(w_up, 'seq', axis=1, tiled=True)]
    psum x1 -> x0, blocking collectives: 41 us -> none  [local(): lax.psum((qkv_part, proj_part, first_gain_part, first_bias_part, query_ga...]
    unnamed x123 -> x10, local copies, waits for them, and re-layouts: 25.3 us -> 3.25 us
    reduce_sum x11 -> x2, other arithmetic: 21.8 us -> 1.06 us  [local_one(): fold = lambda v: v.reshape(heads, -1).sum(0)]
  transfers between devices with their start and end apart: 10 -> 2, of which waited for: 8 -> 1; matrix products, arithmetic and copies ran while one was open for 25% -> 8% of each run, Pallas kernels for 0% -> 39%
where the time goes in v1:
time: 310 us; the launch traced here: 309 us
  Pallas kernels  255 us (82%)
  local copies, waits for them, and re-layouts  24.6 us (8%)
  between operations  14.1 us (5%)
  other arithmetic  7.15 us (2%)
  waiting for transfers between devices  5.08 us (2%)
    pallas_call x1, Pallas kernels, ffn_call(): pl.pallas_call(functools.partial(ffn_body, n_seq), out_shape=(sds((n, wid...  104 us
    pallas_call x1, Pallas kernels, sum_call(): pl.pallas_call(functools.partial(sum_body, n_seq), out_shape=(sds((rows,...  75.4 us
    pallas_call x1, Pallas kernels, bwd_call(): pl.pallas_call(bwd_body, out_shape=outs, in_specs=[VM] * 21, out_specs=tu...  46.5 us
    pallas_call x1, Pallas kernels, fwd_call(): pl.pallas_call(fwd_body, out_shape=outs, in_specs=[VM] * 13, out_specs=tu...  29.5 us
    slice x1, local copies, waits for them, and re-layouts, local_one(): g[:, :3 * width]  6.43 us
  transfers between devices with their start and end apart: 2, of which 1 were waited for; matrix products, arithmetic and copies ran while one was open for 8% of the time, Pallas kernels for 39%

profile of v1, /device:TPU:0, one launch (start us, length us, event | category | flops | bytes accessed | tf_op | source)
XLA Modules:
  0.0 309.2 jit_solution(16891877702753907484)
XLA Ops:
  7.2 3.0 collective-permute-start
  10.3 1.3 reshape.97.g1
  11.5 1.3 reshape.99.g2
  12.8 1.3 reshape.98.b1
  14.1 1.3 reshape.100.b2
  18.0 0.7 constant_dynamic-slice_fusion
  18.7 0.9 select_convert_fusion.1
  19.6 0.7 pad_maximum_fusion.1.fk
  20.3 1.9 pad_maximum_fusion.w_own
  22.2 0.7 compare_convert_fusion.ones
  23.0 5.1 %collective-permute-done.rem = bf16[512,768]{1,0:T(8,128)(2,1)S(1)} collective-permute-done((bf16[512,768]{1,0:T(8,128)(2,1)}, bf16[512,768]{1,0:T(8,128)(2,1)S(1)}, u32[]{:S(2)}, u32[]{:S(2)}) %collective-permute-start) | collective-permute-done | bytes 786464 | tf_op jit(solution)/shard_map/ppermute | solution.py:703
  28.0 0.9 copy-done
  28.9 29.5 %fwd.1 = (bf16[1024,768]{1,0:T(8,128)(2,1)}, bf16[1024,768]{1,0:T(8,128)(2,1)}, bf16[1024,768]{1,0:T(8,128)(2,1)}, f32[512,768]{1,0:T(8,128)}, f32[1024,768]{1,0...) custom-call(bf16[512,768]{1,0:T(8,128)(2,1)} %bitcast.21, ...), custom_call_target="tpu_custom_call" | custom-call | tf_op jit(solution)/shard_map/fwd/pallas_call | solution.py:267
  58.4 103.8 %ffn.1 = (bf16[512,768]{1,0:T(8,128)(2,1)}, f32[512,768]{1,0:T(8,128)}, bf16[2,192,768]{2,1,0:T(8,128)(2,1)}) custom-call(bf16[512,768]{1,0:T(8,128)(2,1)} %get-tuple-element.32.sec, bf16[512,768]{1,0:T(8,128)(2,1)} %bitcast.24, f32[512,768]{1,0:T(8,128)} %get-tuple-element.33.mid, bf16[2,192,768]{2,1,0:T(8,128)(2,1)} %pad_maximum_fusion.w_own), custom_call_target="tpu_custom_call" | custom-call | tf_op jit(solution)/shard_map/ffn/pallas_call | solution.py:454
  162.3 1.4 slice.49.ones
  163.6 0.7 compare_convert_fusion.1.swap
  164.3 46.5 %bwd.1 = (bf16[768,3072]{1,0:T(8,128)(2,1)}, f32[512,768]{1,0:T(8,128)}, bf16[512,768]{1,0:T(8,128)(2,1)}, f32[512,768]{1,0:T(8,128)}, f32[8,768]{1,0:T(8,128)}) custom-call(bf16[512,768]{1,0:T(8,128)(2,1)} %bitcast.22, bf16[512,768]{1,0:T(8,128)(2,1)} %copy-done, f32[512,768]{1,0:T(8,128)} %get-tuple-element.35.gsec, f32[512,768]{1,0:T(8,128)} %get-tuple-element.33.mid, ...), custom_call_target="tpu_custom_call" | custom-call | tf_op jit(solution)/shard_map/bwd/pallas_call | solution.py:280
  210.8 75.4 %sums.1 = (f32[768,3072]{1,0:T(8,128)}, f32[8,768]{1,0:T(8,128)}, f32[512,768]{1,0:T(8,128)}) custom-call(bf16[768,3072]{1,0:T(8,128)(2,1)} %get-tuple-element.43.g, f32[8,768]{1,0:T(8,128)} %get-tuple-element.44.small, bf16[512,768]{1,0:T(8,128)(2,1)} %bitcast.23, f32[512,768]{1,0:T(8,128)} %get-tuple-element.45.gn_own, ...), custom_call_target="tpu_custom_call" | custom-call | tf_op jit(solution)/shard_map/sums/pallas_call | solution.py:671
  286.2 3.2 %slice.44 = f32[768,768]{1,0:T(8,128)} slice(f32[768,3072]{1,0:T(8,128)} %get-tuple-element.50), slice={[0:768], [2304:3072]} | slice | bytes 4718592 | tf_op jit(solution)/shard_map/slice | solution.py:727
  289.5 6.4 %slice.41 = f32[768,2304]{1,0:T(8,128)} slice(f32[768,3072]{1,0:T(8,128)} %get-tuple-element.50), slice={[0:768], [0:2304]} | slice | bytes 14155776 | tf_op jit(solution)/shard_map/slice | solution.py:726
  297.7 1.1 convert_element_type.25
  298.9 1.1 slice_bitcast_fusion
  300.3 0.9 copy.28
  301.2 1.1 copy.29
  (23 shorter events, 4.9 us)
Async XLA Ops:
  7.2 290.6 %all-reduce.2.cloned.1.call-start = ((), (), s32[]{:S(2)}) async-start(), calls=%async_computation | async-start | bytes 1179648 | tf_op jit(solution)/shard_map/psum | solution.py:723
  7.2 20.8 %collective-permute-start = (bf16[512,768]{1,0:T(8,128)(2,1)}, bf16[512,768]{1,0:T(8,128)(2,1)S(1)}, u32[]{:S(2)}, u32[]{:S(2)}) collective-permute-start(bf16[512,768]{1,0:T(8,128)(2,1)} %bitcast.20), channel_id=1, source_target_pairs={{0,16},{16,0},{1,17},{17,1},{2,18},{18,2},{3,19},{19,3},{4,20},{20... | collective-permute-start | bytes 2359304 | tf_op jit(solution)/shard_map/ppermute | solution.py:703
  28.0 0.9 copy-start
  289.4 6.4 %copy-start.3 = (f32[8,768]{1,0:T(8,128)S(1)}, f32[8,768]{1,0:T(8,128)}, u32[]{:S(2)}) copy-start(f32[8,768]{1,0:T(8,128)} %get-tuple-element.49) | copy-start | bytes 73732
  298.9 1.4 copy-start.2
  298.9 2.3 copy-start.1
Sparse Core Ops, SparseCore 0:
  162.4 29.3 all-reduce.1

commit v2 on v0

--- a/solution.py
+++ b/solution.py
@@ -1,9 +1,808 @@
+import functools
 import jax
 import jax.numpy as jnp
 from jax import lax
+from jax.experimental import pallas as pl
+from jax.experimental.pallas import tpu as pltpu
 from jax.sharding import PartitionSpec as P
 
 EPS = 1e-06
+F32 = jnp.float32
+BF16 = jnp.bfloat16
+LOG2E = 1.4426950408889634
+BIG = 16384.0
+TILE = 256
+NT = (((1,), (1,)), ((), ()))
+NN = (((1,), (0,)), ((), ()))
+TN = (((0,), (0,)), ((), ()))
+
+
+def dot(a, b, dims=NN):
+    return lax.dot_general(a, b, dims, preferred_element_type=F32)
+
+
+def two(x):
+    hi = x.astype(BF16)
+    return hi, (x - hi.astype(F32)).astype(BF16)
+
+
+def group_sum(x, ones):
+    hi, lo = two(x)
+    return dot(hi, ones) + dot(lo, ones)
+
+
+def rows_norm(x):
+    average = jnp.mean(x, axis=-1, keepdims=True)
+    centred = x - average
+    spread = jnp.mean(centred * centred, axis=-1, keepdims=True)
+    scale = lax.rsqrt(spread + EPS)
+    return centred * scale, scale
+
+
+def tile_of(i, size=TILE):
+    return pl.ds(pl.multiple_of(i * size, size), size)
+
+
+VM = pl.BlockSpec(memory_space=pltpu.VMEM)
+LIMIT = 60 * 1024 * 1024
+
+
+def sds(shape, dtype):
+    return jax.ShapeDtypeStruct(shape, dtype)
+
+
+def ring_places(n_seq):
+    s = lax.axis_index("seq")
+    core, chip = s % 2, s // 2
+    chips = n_seq // 2
+    half = chips // 2
+    odd = chip % 2
+    place = (1 - odd) * (chip // 2) + odd * (chips - 1 - chip // 2)
+
+    def device(p):
+        far = p // half
+        return ((1 - far) * 2 * p + far * (2 * (chips - 1 - p) + 1)) * 2 + core
+
+    right = device((place + 1) % chips)
+    left = device((place + chips - 1) % chips)
+    return core, place, right, left, s + 1 - 2 * core
+
+
+def copy_to(src, dst, send, recv, target):
+    return pltpu.make_async_remote_copy(
+        src_ref=src, dst_ref=dst, send_sem=send, recv_sem=recv, device_id=target,
+        device_id_type=pl.DeviceIdType.MESH)
+
+
+def greet(targets):
+    barrier = pltpu.get_barrier_semaphore()
+    for t in targets:
+        pl.semaphore_signal(barrier, inc=1, device_id=t, device_id_type=pl.DeviceIdType.MESH)
+    pl.semaphore_wait(barrier, len(targets))
+
+
+SPLIT = 2
+
+
+def sum_body(n_seq, g, small, own, gn_rem, base, g1, fin, sout, igrad,
+             pbuf, accin, accout, xin, xout, srec, sring, gback,
+             psend, precv, asend, arecv, xsend, xrecv, fsend, frecv, qsend, qrecv, ssend, srecv, gsend, grecv):
+    rows, cols = g.shape
+    chips = n_seq // 2
+    half = rows // 2
+    cr = half // chips
+    cw = cols // (2 * SPLIT)
+    core, place, right, left, partner = ring_places(n_seq)
+    x = lax.axis_index("pos")
+    right, left, partner, across = {"seq": right}, {"seq": left}, {"seq": partner}, {"pos": 1 - x}
+    greet((right, left, partner, across))
+
+    def chunk(p):
+        return (p + 2 * chips) % chips
+
+    def at(d, k):
+        return pl.ds((d * SPLIT + k) * cw, cw)
+
+    def rows_of(c, p):
+        return pl.ds(pl.multiple_of(c * half + p * cr, cr), cr)
+
+    def p_copy(q):
+        return copy_to(g.at[rows_of(1 - core, q)], pbuf.at[q], psend.at[q], precv.at[q], partner)
+
+    def a_copy(d, k, s):
+        return copy_to(accout.at[s, d * SPLIT + k], accin.at[s, d * SPLIT + k], asend.at[s, d * SPLIT + k],
+                       arecv.at[s, d * SPLIT + k], left if d else right)
+
+    def x_copy(d, k):
+        i = d * SPLIT + k
+        return copy_to(xout.at[i], xin.at[i], xsend.at[i], xrecv.at[i], across)
+
+    def f_copy(d, k, s):
+        p = chunk(place + s) if d else chunk(place - s)
+        ref = fin.at[rows_of(core, p), at(d, k)]
+        return copy_to(ref, ref, fsend.at[s, d * SPLIT + k], frecv.at[s, d * SPLIT + k], left if d else right)
+
+    def f_recv(d, k, s):
+        p = chunk(place + s + 1) if d else chunk(place - s - 1)
+        ref = fin.at[rows_of(core, p), at(d, k)]
+        return copy_to(ref, ref, fsend.at[s, d * SPLIT + k], frecv.at[s, d * SPLIT + k], left if d else right)
+
+    def q_copy(d, k, s):
+        p = chunk(place + s) if d else chunk(place - s)
+        ref = fin.at[rows_of(core, p), at(d, k)]
+        return copy_to(ref, ref, qsend.at[s, d * SPLIT + k], qrecv.at[s, d * SPLIT + k], partner)
+
+    def q_recv(d, k, s):
+        p = chunk(place + s) if d else chunk(place - s)
+        ref = fin.at[rows_of(1 - core, p), at(d, k)]
+        return copy_to(ref, ref, qsend.at[s, d * SPLIT + k], qrecv.at[s, d * SPLIT + k], partner)
+
+    def s_copy(s):
+        return copy_to(sring.at[chunk(place - s)], sring.at[chunk(place - s)], ssend.at[s], srecv.at[s], right)
+
+    def s_recv(s):
+        p = chunk(place - s - 1)
+        return copy_to(sring.at[p], sring.at[p], ssend.at[s], srecv.at[s], right)
+
+    both = [(d, k) for k in range(SPLIT) for d in range(2)]
+    back = copy_to(gn_rem, gback, gsend.at[0], grecv.at[0], across)
+    small_p = copy_to(small, srec.at[0], gsend.at[1], grecv.at[1], partner)
+    small_x = copy_to(srec.at[1], srec.at[2], gsend.at[2], grecv.at[2], across)
+
+    def order(s):
+        return chunk(place - s), chunk(place + s)
+
+    small_p.start()
+    for s in range(1, chips // 2 + 1):
+        for q in order(s)[: 1 if 2 * s == chips else 2]:
+            p_copy(q).start()
+    p_copy(place).start()
+    back.start()
+
+    def part(d, k, q):
+        cs = at(d, k)
+        return g[rows_of(core, q), cs].astype(F32) + pbuf[q, :, cs].astype(F32)
+
+    def reduce_step(s, c):
+        @pl.when(s <= chips // 2)
+        def _():
+            p_copy(chunk(place - s)).wait_recv()
+
+            @pl.when(2 * s < chips)
+            def _():
+                p_copy(chunk(place + s)).wait_recv()
+
+        for d, k in both:
+            q = chunk(place + s) if d else chunk(place - s)
+
+            @pl.when(s == 1)
+            def _():
+                accout[s - 1, d * SPLIT + k] = part(d, k, q).astype(BF16)
+
+            @pl.when(s > 1)
+            def _():
+                a_copy(d, k, s - 2).wait_recv()
+                accout[s - 1, d * SPLIT + k] = (part(d, k, q) + accin[s - 2, d * SPLIT + k].astype(F32)).astype(BF16)
+
+            a_copy(d, k, s - 1).start()
+        return c
+
+    lax.fori_loop(1, chips, reduce_step, 0)
+    p_copy(place).wait_recv()
+    for d, k in both:
+        a_copy(d, k, chips - 2).wait_recv()
+        xout[d * SPLIT + k] = (part(d, k, place) + accin[chips - 2, d * SPLIT + k].astype(F32)).astype(BF16)
+        x_copy(d, k).start()
+    small_p.wait_recv()
+    srec[1] = small[...] + srec[0]
+    small_x.start()
+    back.wait_recv()
+    n = own.shape[0]
+
+    def norm_tile(i, c):
+        rs = tile_of(i)
+        xh, r = rows_norm(own[rs, :].astype(F32))
+        dy = gback[rs, :].astype(F32) * g1[...].reshape(1, -1)
+        dx = r * (dy - jnp.mean(dy, -1, keepdims=True) - xh * jnp.mean(dy * xh, -1, keepdims=True))
+        igrad[rs, :] = base[rs, :] + dx
+        return c
+
+    lax.fori_loop(0, n // TILE, norm_tile, 0)
+    small_x.wait_recv()
+    sring[place] = srec[1] + srec[2]
+    s_copy(0).start()
+    for d, k in both:
+        x_copy(d, k).wait_recv()
+        i = d * SPLIT + k
+        fin[rows_of(core, place), at(d, k)] = (xout[i].astype(F32) + xin[i].astype(F32)).astype(BF16)
+        f_copy(d, k, 0).start()
+        q_copy(d, k, 0).start()
+
+    def gather_step(s, c):
+        for d, k in both:
+            f_recv(d, k, s - 1).wait_recv()
+
+            @pl.when(s < chips - 1)
+            def _():
+                f_copy(d, k, s).start()
+
+            q_copy(d, k, s).start()
+        s_recv(s - 1).wait_recv()
+
+        @pl.when(s < chips - 1)
+        def _():
+            s_copy(s).start()
+        return c
+
+    lax.fori_loop(1, chips, gather_step, 0)
+
+    def finish(s, c):
+        for d, k in both:
+            q_recv(d, k, s).wait_recv()
+        return c
+
+    lax.fori_loop(0, chips, finish, 0)
+    total = sring[0]
+    for s in range(1, chips):
+        total = total + sring[s]
+    sout[...] = total
+
+    def drain(s, c):
+        for d, k in both:
+            q_copy(d, k, s).wait_send()
+
+            @pl.when(s < chips - 1)
+            def _():
+                a_copy(d, k, s).wait_send()
+                f_copy(d, k, s).wait_send()
+
+        @pl.when(s < chips - 1)
+        def _():
+            s_copy(s).wait_send()
+        p_copy(s).wait_send()
+        return c
+
+    lax.fori_loop(0, chips, drain, 0)
+    for d, k in both:
+        x_copy(d, k).wait_send()
+    for c in (back, small_p, small_x):
+        c.wait_send()
+
+
+def sum_call(n_seq, g, small, own, gn_rem, base, g1):
+    rows, cols = g.shape
+    n, width = own.shape
+    chips = n_seq // 2
+    cr, lanes, cw = rows // 2 // chips, 2 * SPLIT, cols // (2 * SPLIT)
+    V, D = pltpu.VMEM, pltpu.SemaphoreType.DMA
+    return pl.pallas_call(
+        functools.partial(sum_body, n_seq),
+        out_shape=(sds((rows, cols), BF16), sds(small.shape, F32), sds((n, width), F32)),
+        in_specs=[VM] * 6, out_specs=(VM,) * 3,
+        scratch_shapes=[
+            V((chips, cr, cols), BF16), V((chips - 1, lanes, cr, cw), BF16), V((chips - 1, lanes, cr, cw), BF16),
+            V((lanes, cr, cw), BF16), V((lanes, cr, cw), BF16),
+            V((3,) + small.shape, F32), V((chips,) + small.shape, F32), V((n, width), BF16),
+            D((chips,)), D((chips,)), D((chips - 1, lanes)), D((chips - 1, lanes)), D((lanes,)), D((lanes,)),
+            D((chips - 1, lanes)), D((chips - 1, lanes)), D((chips, lanes)), D((chips, lanes)),
+            D((chips - 1,)), D((chips - 1,)), D((3,)), D((3,))],
+        compiler_params=pltpu.CompilerParams(
+            vmem_limit_bytes=LIMIT, collective_id=2, has_side_effects=True),
+        name="sums",
+    )(g, small, own, gn_rem, base, g1)
+
+
+def finish_body(g, small, qkv, proj, fg, fb, qgg, kgg, sgg, sbg):
+    width = proj.shape[1]
+    qkv[...] = g[:, 0:3 * width].astype(F32)
+    proj[...] = g[:, 3 * width:].astype(F32)
+
+    @pl.when(pl.program_id(0) == 0)
+    def _():
+        for i, ref in enumerate((fg, fb, sgg, sbg)):
+            ref[...] = small[i:i + 1, :].reshape(width)
+        for i, ref in ((4, qgg), (5, kgg)):
+            folded = small[i:i + 1, 0:128]
+            for j in range(1, width // 128):
+                folded = folded + small[i:i + 1, j * 128:(j + 1) * 128]
+            folded = folded + pltpu.roll(folded, 64, 1)
+            ref[...] = folded[:, 0:64].reshape(64)
+
+
+def finish_call(g, small):
+    rows, cols = g.shape
+    width = cols // 4
+    step = 128
+    whole = lambda size: pl.BlockSpec((size,), lambda i: (0,))
+    return pl.pallas_call(
+        finish_body, grid=(rows // step,),
+        out_shape=(sds((rows, 3 * width), F32), sds((rows, width), F32), sds((width,), F32), sds((width,), F32),
+                   sds((64,), F32), sds((64,), F32), sds((width,), F32), sds((width,), F32)),
+        in_specs=[pl.BlockSpec((step, cols), lambda i: (i, 0)), pl.BlockSpec(small.shape, lambda i: (0, 0))],
+        out_specs=(pl.BlockSpec((step, 3 * width), lambda i: (i, 0)), pl.BlockSpec((step, width), lambda i: (i, 0)),
+                   whole(width), whole(width), whole(64), whole(64), whole(width), whole(width)),
+        name="finish",
+    )(g, small)
+
+
+def layer_body(n_seq, own, gy, seg, g1, b1, wqkv, qg, kg, wout, g2, b2, wup, wdown,
+               out, base, gn_rem, gall, small, upg, downg,
+               rem, fq, fk, ones, swap, vecs, normed, kk, vv, qq, rq, rk, qaug, att, mid,
+               sx, sg, wbuf, accin, accout, first, hid, gpre, blk, gs, prec, mine, xin,
+               dk, stage,
+               wsend, wrecv, asend, arecv, psend, precv, tsend, trecv, xsend, xrecv, gsem):
+    n, width = own.shape
+    f = wup.shape[0]
+    h = f // 2
+    chips = n_seq // 2
+    pairs = width // 128
+    tiles = n // TILE
+    core, place, right, left, partner = ring_places(n_seq)
+    x = lax.axis_index("pos")
+    right, left, partner, across = {"seq": right}, {"seq": left}, {"seq": partner}, {"pos": 1 - x}
+    greet((right, left, partner, across))
+
+    def slot(s, k, d):
+        return pl.ds(pl.multiple_of((k * chips + s) * f + d * h, h), h)
+
+    def w_copies(s):
+        return [copy_to(wbuf.at[slot(s, k, d)], wbuf.at[slot(s + 1, k, d)], wsend.at[d, k, s], wrecv.at[d, k, s],
+                        left if d else right) for d in range(2) for k in range(2)]
+
+    def a_copies(s):
+        rows = [pl.ds(d * h, h) for d in range(2)]
+        return [copy_to(accout.at[s - 1, :, rows[d]], accin.at[s - 1, :, rows[d]], asend.at[d, s - 1],
+                        arecv.at[d, s - 1], left if d else right) for d in range(2)]
+
+    def w_step(s):
+        for c in w_copies(s - 1):
+            c.wait_recv()
+
+        @pl.when(s < chips - 1)
+        def _():
+            for c in w_copies(s):
+                c.start()
+
+    def r_step(s):
+        for c in a_copies(s - 1):
+            c.wait_recv()
+        accout[s - 1] = (accout[s - 1].astype(F32) + accin[s - 2].astype(F32)).astype(BF16)
+        for c in a_copies(s):
+            c.start()
+
+    def t_copy(i):
+        rows = pl.ds(i * TILE, TILE)
+        return copy_to(own.at[rows], rem.at[rows], tsend.at[i], trecv.at[i], across)
+
+    def s_copy(i):
+        return copy_to(sx.at[pl.ds(i * TILE, TILE)], sx.at[pl.ds(n + i * TILE, TILE)], psend.at[3 + i],
+                       precv.at[3 + i], partner)
+
+    gy_copy = copy_to(gy, sg.at[pl.ds(n, n)], psend.at[0], precv.at[0], partner)
+    parts = (copy_to(gs.at[pl.ds(n, n)], prec.at[1], psend.at[1], precv.at[1], partner),
+             copy_to(blk.at[pl.ds(n, n)], prec.at[0], psend.at[2], precv.at[2], partner))
+    x_copy = copy_to(mine, xin, xsend.at[0], xrecv.at[0], across)
+
+    def w_first():
+        return [copy_to((wdown if k else wup).at[pl.ds(d * h, h)], wbuf.at[slot(1, k, d)], wsend.at[d, k, 0],
+                        wrecv.at[d, k, 0], left if d else right) for d in range(2) for k in range(2)]
+
+    for c in w_first():
+        c.start()
+    for i in range(tiles):
+        t_copy(i).start()
+    gy_copy.start()
+
+    at = pl.multiple_of(x * n, n)
+    labels = jnp.concatenate([seg[:, pl.ds(at, n)], seg[:, pl.ds(n - at, n)]], axis=1)
+    lane = lax.broadcasted_iota(jnp.int32, (128, 2 * n), 0) % 64
+    same = lane == labels
+    keyed = jnp.where((lane >= 6) & (lane <= 8), 1.0, jnp.where(same & (lane < 6), 1.0, 0.0))
+    fk[...] = keyed.T.astype(BF16)
+    away = jnp.where((lane < 6) & jnp.logical_not(same), -BIG, 0.0)
+    fq[...] = away[:, 0:n].T.astype(BF16)
+    ra = lax.broadcasted_iota(jnp.int32, ones.shape, 0) // 64
+    rb = lax.broadcasted_iota(jnp.int32, ones.shape, 1) // 64
+    ones[...] = jnp.where(ra == rb, 1.0, 0.0).astype(BF16)
+    swap[...] = jnp.where(ra[:128, :128] == rb[:128, :128], 0.0, 1.0).astype(BF16)
+    for i, v in enumerate((g1, b1, g2, b2)):
+        vecs[i:i + 1, :] = v[...].reshape(1, width)
+    for i, v in enumerate((qg, kg)):
+        r = v[...].reshape(1, 64)
+        vecs[4 + i:5 + i, :] = jnp.concatenate([r] * (width // 64), axis=1)
+    sg[0:n, :] = gy[...]
+    wbuf[0:f, :] = wup[...]
+    wbuf[chips * f:(chips + 1) * f, :] = wdown[...]
+    cols = ones.shape[0]
+
+    def project(xs, i, queries):
+        rows = tile_of(i)
+        low = (rows_norm(xs)[0] * vecs[0:1, :] + vecs[1:2, :]).astype(BF16)
+        normed[rows, :] = low
+        for block in range(0 if queries else width // cols, 3 * width // cols):
+            raw = dot(low, wqkv[:, block * cols:(block + 1) * cols])
+            part, a = divmod(block * cols, width)
+            lanes = slice(a, a + cols)
+            if part == 2:
+                vv[rows, lanes] = raw.astype(BF16)
+                continue
+            centred = raw - group_sum(raw, ones[...]) * (1 / 64)
+            scale = lax.rsqrt(group_sum(centred * centred, ones[...]) * (1 / 64) + EPS)
+            dst, rdst = (qq, rq) if part == 0 else (kk, rk)
+            dst[rows, lanes] = (centred * scale * vecs[4 + part:5 + part, lanes]).astype(BF16)
+            rdst[rows, lanes] = scale
+
+    def own_tile(i, c):
+        project(own[tile_of(i), :].astype(F32), i, True)
+        return c
+
+    lax.fori_loop(0, tiles, own_tile, 0)
+    w_step(1)
+    lane_t = lax.broadcasted_iota(jnp.int32, (TILE, 128), 1)
+    low_t = lane_t < 64
+    lane_n = lax.broadcasted_iota(jnp.int32, (n, 128), 1)
+    low_n = lane_n < 64
+
+    def attend(krows, size, add, after):
+        low_k = lax.broadcasted_iota(jnp.int32, (size, 128), 1) < 64
+
+        def pair(p, c):
+            lanes = tile_of(p, 128)
+            k, v, feat = kk[krows, lanes], vv[krows, lanes], fk[krows, :]
+            one = jnp.ones_like(v)
+            ks = (jnp.where(low_k, k, feat), jnp.where(low_k, feat, k))
+            vs = (jnp.where(low_k, v, one), jnp.where(low_k, one, v))
+
+            q, mask = qq[:, lanes], fq[...]
+            for a in range(2):
+                qa = jnp.where(low_n, q, mask) if a == 0 else jnp.where(low_n, mask, q)
+                e = jnp.exp2(dot(qa, ks[a], NT) * (LOG2E / 8)).astype(BF16)
+                o = dot(e, vs[a])
+                to = slice(a * n, (a + 1) * n)
+                blk[to, lanes] = blk[to, lanes] + o if add else o
+            if after is not None:
+                after(p)
+            return c
+
+        lax.fori_loop(0, pairs, pair, 0)
+
+    def middle_step(p):
+        @pl.when(p == 2)
+        def _():
+            w_step(2)
+
+    attend(slice(0, n), n, False, middle_step)
+    for i in range(tiles):
+        t_copy(i).wait_recv()
+        project(rem[i * TILE:(i + 1) * TILE, :].astype(F32), tiles + i, False)
+        w_step(3 + i)
+        attend(slice(n + i * TILE, n + (i + 1) * TILE), TILE, True, None)
+
+    def close(p, c):
+        lanes = tile_of(p, 128)
+
+        def tile(t, c):
+            rows = tile_of(t)
+            q, mask = qq[rows, lanes], fq[rows, :]
+            res = [blk[pl.ds(pl.multiple_of(a * n + t * TILE, TILE), TILE), lanes] for a in range(2)]
+            for a in range(2):
+                qa = jnp.where(low_t, q, mask) if a == 0 else jnp.where(low_t, mask, q)
+                shift = jnp.log(res[a]) * -8.0
+                hi, lo = two(shift)
+                lo2 = (shift - hi.astype(F32) - lo.astype(F32)).astype(BF16)
+                s = 64 * (1 - a)
+                qaug[p * 2 + a, rows, :] = jnp.where(
+                    lane_t == s + 6, hi, jnp.where(lane_t == s + 7, lo, jnp.where(lane_t == s + 8, lo2, qa)))
+            num = jnp.where(low_t, res[0], res[1])
+            den = pltpu.roll(jnp.where(low_t, res[1], res[0]), 64, 1)
+            att[rows, lanes] = (num / den).astype(BF16)
+            return c
+
+        lax.fori_loop(0, tiles, tile, 0)
+        return c
+
+    lax.fori_loop(0, pairs, close, 0)
+    for i in range(tiles):
+        rows = slice(i * TILE, (i + 1) * TILE)
+        m = own[rows, :].astype(F32) + dot(att[rows, :], wout[...])
+        mid[rows, :] = m
+        sx[rows, :] = (rows_norm(m)[0] * vecs[2:3, :] + vecs[3:4, :]).astype(BF16)
+        s_copy(i).start()
+    w_step(5)
+    quad = chips // 2
+    span = quad * f
+
+    def group(g, carry):
+        @pl.when(g == 0)
+        def _():
+            gy_copy.wait_recv()
+            for j in range(tiles):
+                s_copy(j).wait_recv()
+
+        @pl.when(g == 1)
+        def _():
+            w_step(6)
+            w_step(7)
+
+        up = wbuf.at[pl.ds(pl.multiple_of(g * span, span), span)]
+        down = wbuf.at[pl.ds(pl.multiple_of(chips * f + g * span, span), span)]
+
+        def tile(i, c):
+            rows = tile_of((i + g * tiles) % (2 * tiles))
+            acts, slopes = [], []
+            for j in range(span // TILE):
+                cs = slice(j * TILE, (j + 1) * TILE)
+                pre = dot(sx[rows, :], up[cs, :], NT)
+                gh = dot(sg[rows, :], down[cs, :], NT)
+                cdf = 0.5 + 0.5 * lax.erf(pre * 0.7071067811865476)
+                slope = cdf + pre * (jnp.exp(-0.5 * pre * pre) * 0.3989422804014327)
+                acts.append((pre * cdf).astype(BF16))
+                slopes.append((gh * slope).astype(BF16))
+                hid[rows, cs] = acts[-1]
+                gpre[rows, cs] = slopes[-1]
+            o = dot(jnp.concatenate(acts, 1), down[...])
+            s = dot(jnp.concatenate(slopes, 1), up[...])
+
+            @pl.when(g == 0)
+            def _():
+                blk[rows, :] = o
+                gs[rows, :] = s
+
+            @pl.when(g > 0)
+            def _():
+                blk[rows, :] += o
+                gs[rows, :] += s
+
+            @pl.when((g == 1) & (i == tiles - 1))
+            def _():
+                for c in parts:
+                    c.start()
+            return c
+
+        lax.fori_loop(0, 2 * tiles, tile, 0)
+
+        @pl.when(g == 1)
+        def _():
+            r_step(2)
+
+        def block(j, c):
+            for k, (lhs, rhs) in enumerate(((gpre, sx), (hid, sg))):
+                part = dot(lhs[:, pl.ds(pl.multiple_of(j * 2 * f, 2 * f), 2 * f)], rhs[...], TN)
+                for m in range(2):
+                    one = part[m * f:(m + 1) * f]
+                    at = g * quad + 2 * j + m
+
+                    @pl.when(at == 0)
+                    def _():
+                        first[k] = one
+
+                    @pl.when(at > 0)
+                    def _():
+                        accout[jnp.maximum(at - 1, 0), k] = one.astype(BF16)
+            return c
+
+        lax.fori_loop(0, quad // 2, block, 0)
+
+        @pl.when(g == 0)
+        def _():
+            for c in a_copies(1):
+                c.start()
+        return carry
+
+    lax.fori_loop(0, 2, group, 0)
+    r_step(3)
+
+    def w_drain(s, c):
+        for cp in w_copies(s):
+            cp.wait_send()
+        return c
+
+    lax.fori_loop(1, chips - 1, w_drain, 0)
+    for c in w_first():
+        c.wait_send()
+    for i in range(tiles):
+        s_copy(i).wait_send()
+    gbr, gat = sx.at[0:n], sx.at[n:2 * n]
+    small[...] = jnp.zeros_like(small)
+    parts[0].wait_recv()
+
+    def mid_tile(i, c):
+        rows = tile_of(i)
+        xh, r = rows_norm(mid[rows, :])
+        dy = gs[rows, :] + prec[1, rows, :]
+        small[2:3, :] += jnp.sum(dy * xh, axis=0, keepdims=True)
+        small[3:4, :] += jnp.sum(dy, axis=0, keepdims=True)
+        gd = dy * vecs[2:3, :]
+        dx = r * (gd - jnp.mean(gd, -1, keepdims=True) - xh * jnp.mean(gd * xh, -1, keepdims=True))
+        gm = gy[rows, :].astype(F32) + dx
+        base[rows, :] = gm
+        low = gm.astype(BF16)
+        gbr[rows, :] = low
+        gat[rows, :] = dot(low, wout[...], NT).astype(BF16)
+        return c
+
+    lax.fori_loop(0, tiles, mid_tile, 0)
+    parts[1].wait_recv()
+    out[...] = (mid[...] + (blk[0:n, :] + prec[0])).astype(BF16)
+
+    def flush(j, rows, lanes):
+        return pltpu.make_async_copy(stage.at[j], gall.at[rows, lanes], gsem.at[j])
+
+    def proj_tile(i, c):
+        rows = tile_of(i)
+        stage[i] = dot(att[:, rows], gbr[...], TN).astype(BF16)
+        flush(i, rows, pl.ds(3 * width, width)).start()
+        return c
+
+    lax.fori_loop(0, width // TILE, proj_tile, 0)
+    r_step(4)
+
+    def keys_of(j, rows):
+        return wbuf.at[pl.ds(pl.multiple_of(j * 2 * n + rows, TILE), TILE)]
+
+    def mix(part, rows):
+        return pl.ds(part * 2 * n + rows.start, rows.size)
+
+    ones_p = slice(0, 128)
+
+    def norm_back(dy, y, r, gain):
+        group = ones[ones_p, ones_p]
+        dy = dy * 0.125
+        y = y.astype(F32)
+        prod = dy * y
+        gd = dy * gain
+        m1 = group_sum(gd, group) * (1 / 64)
+        m2 = group_sum(prod, group) * (1 / 64)
+        inv = 1.0 / gain
+        return r * (gd - m1 - y * inv * m2), jnp.sum(prod, 0, keepdims=True) * inv
+
+    def pair(p, c):
+        @pl.when((p == 1) | (p == 3) | (p == 4))
+        def _():
+            r_step(5 + p // 2)
+
+        lanes = tile_of(p, 128)
+        do = gat[:, lanes]
+        delta = -group_sum(do.astype(F32) * att[:, lanes].astype(F32), swap[...])
+        hi, lo = two(delta)
+        zero = jnp.zeros_like(do)
+        das = []
+        for a in range(2):
+            s = 64 * (1 - a)
+            extra = jnp.where(lane_n == s, hi, jnp.where(lane_n == s + 1, lo, zero))
+            das.append(jnp.where(low_n, do, extra) if a == 0 else jnp.where(low_n, extra, do))
+
+        acc = [None, None]
+        for t in range(2):
+            rows = slice(t * n, (t + 1) * n)
+            k, v, feat = kk[rows, lanes], vv[rows, lanes], fk[rows, :]
+            one = jnp.ones_like(v)
+            dks, dvs = [], []
+            for a in range(2):
+                ka = jnp.where(low_n, k, feat) if a == 0 else jnp.where(low_n, feat, k)
+                va = jnp.where(low_n, v, one) if a == 0 else jnp.where(low_n, one, v)
+                qa = qaug[p * 2 + a]
+                e = jnp.exp2(dot(ka, qa, NT) * (LOG2E / 8))
+                ds = (e * dot(va, das[a], NT)).astype(BF16)
+                dvs.append(dot(e.astype(BF16), das[a]))
+                dks.append(dot(ds, qa))
+                dq = dot(ka, ds, TN)
+                acc[a] = dq if t == 0 else acc[a] + dq
+            dk[rows, :] = jnp.where(low_n, dks[0], dks[1])
+            wbuf[4 * n + t * n:4 * n + (t + 1) * n, lanes] = jnp.where(low_n, dvs[0], dvs[1]).astype(BF16)
+        low_s = lax.broadcasted_iota(jnp.int32, (128, n), 0) < 64
+        dq = jnp.where(low_s, acc[0], acc[1]).T
+        qa = jnp.where(low_n, qaug[p * 2], qaug[p * 2 + 1])
+        dx, gg = norm_back(dq, qa, rq[:, lanes], vecs[4:5, lanes])
+        wbuf[0:n, lanes] = dx.astype(BF16)
+        small[4:5, lanes] = gg
+        dx, gg = norm_back(dk[...], kk[:, lanes], rk[:, lanes], vecs[5:6, lanes])
+        wbuf[2 * n:4 * n, lanes] = dx.astype(BF16)
+        small[5:6, lanes] = gg
+        return c
+
+    lax.fori_loop(0, pairs, pair, 0)
+    for i in range(width // TILE):
+        flush(i, pl.ds(i * TILE, TILE), pl.ds(3 * width, width)).wait()
+    for c in a_copies(chips - 1):
+        c.wait_recv()
+    mine[...] = (first[...] + accin[chips - 2].astype(F32)).astype(BF16)
+    x_copy.start()
+
+    def gain_sums(xh, gn):
+        small[0:1, :] += jnp.sum(gn * xh, axis=0, keepdims=True)
+        small[1:2, :] += jnp.sum(gn, axis=0, keepdims=True)
+
+    def rem_tile(i, c):
+        rows = tile_of(i)
+        gn = (dot(wbuf[pl.ds(pl.multiple_of(3 * n + i * TILE, TILE), TILE), :], wqkv[:, width:2 * width], NT)
+              + dot(wbuf[pl.ds(pl.multiple_of(5 * n + i * TILE, TILE), TILE), :], wqkv[:, 2 * width:], NT))
+        gn_rem[rows, :] = gn.astype(BF16)
+        gain_sums(rows_norm(rem[rows, :].astype(F32))[0], gn)
+        return c
+
+    def own_back(i, c):
+        rows = tile_of(i)
+        gn = (dot(wbuf[rows, :], wqkv[:, 0:width], NT)
+              + dot(wbuf[pl.ds(pl.multiple_of(2 * n + i * TILE, TILE), TILE), :], wqkv[:, width:2 * width], NT)
+              + dot(wbuf[pl.ds(pl.multiple_of(4 * n + i * TILE, TILE), TILE), :], wqkv[:, 2 * width:], NT))
+        xh, r = rows_norm(own[rows, :].astype(F32))
+        gain_sums(xh, gn)
+        gd = gn * vecs[0:1, :]
+        base[rows, :] += r * (gd - jnp.mean(gd, -1, keepdims=True) - xh * jnp.mean(gd * xh, -1, keepdims=True))
+        return c
+
+    def qkv_tile(i, c):
+        rows = tile_of(i)
+        jobs = ((0, n, 0), (2 * n, 2 * n, 1), (4 * n, 2 * n, 2))
+        for j, (at, size, part) in enumerate(jobs):
+            stage[j] = dot(normed[0:size, rows], wbuf[at:at + size, :], TN).astype(BF16)
+            flush(j, rows, pl.ds(part * width, width)).start()
+        for j, (at, size, part) in enumerate(jobs):
+            flush(j, rows, pl.ds(part * width, width)).wait()
+        return c
+
+    lax.fori_loop(0, width // TILE, qkv_tile, 0)
+    lax.fori_loop(0, tiles, rem_tile, 0)
+    lax.fori_loop(0, tiles, own_back, 0)
+    x_copy.wait_recv()
+    total = mine[...].astype(F32) + xin[...].astype(F32)
+    upg[...] = total[0]
+    downg[...] = total[1]
+
+    def a_drain(s, c):
+        for cp in a_copies(s):
+            cp.wait_send()
+        return c
+
+    lax.fori_loop(1, chips, a_drain, 0)
+    for i in range(tiles):
+        t_copy(i).wait_send()
+    for c in (gy_copy, x_copy) + parts:
+        c.wait_send()
+
+
+def layer_call(n_seq, own, gy, seg, g1, b1, wqkv, qg, kg, wout, g2, b2, wup, wdown):
+    n, width = own.shape
+    f = wup.shape[0]
+    chips = n_seq // 2
+    heads = width // 64
+    tiles = n // TILE
+    V, D = pltpu.VMEM, pltpu.SemaphoreType.DMA
+    return pl.pallas_call(
+        functools.partial(layer_body, n_seq),
+        out_shape=(sds((n, width), BF16), sds((n, width), F32), sds((n, width), BF16),
+                   sds((width, 4 * width), BF16), sds((8, width), F32), sds((f, width), F32), sds((f, width), F32)),
+        in_specs=[VM] * 13,
+        out_specs=(VM, VM, VM, pl.BlockSpec(memory_space=pl.ANY), VM, VM, VM),
+        scratch_shapes=[
+            V((n, width), BF16), V((n, 128), BF16), V((2 * n, 128), BF16), V((256, 256), BF16), V((128, 128), BF16),
+            V((8, width), F32), V((2 * n, width), BF16), V((2 * n, width), BF16), V((2 * n, width), BF16),
+            V((n, width), BF16), V((n, width), F32), V((2 * n, width), F32), V((heads, n, 128), BF16),
+            V((n, width), BF16), V((n, width), F32),
+            V((2 * n, width), BF16), V((2 * n, width), BF16), V((chips * 2 * f, width), BF16),
+            V((chips - 1, 2, f, width), BF16), V((chips - 1, 2, f, width), BF16), V((2, f, width), F32),
+            V((2 * n, chips // 2 * f), BF16), V((2 * n, chips // 2 * f), BF16), V((2 * n, width), F32), V((2 * n, width), F32),
+            V((2, n, width), F32), V((2, f, width), BF16), V((2, f, width), BF16),
+            V((2 * n, 128), F32), V((3, TILE, width), BF16),
+            D((2, 2, chips - 1)), D((2, 2, chips - 1)), D((2, chips - 1)), D((2, chips - 1)),
+            D((3 + tiles,)), D((3 + tiles,)), D((tiles,)), D((tiles,)), D((1,)), D((1,)), D((3,))],
+        compiler_params=pltpu.CompilerParams(
+            vmem_limit_bytes=66 * 1000 * 1000, collective_id=1, has_side_effects=True),
+        name="layer",
+    )(own, gy, seg, g1, b1, wqkv, qg, kg, wout, g2, b2, wup, wdown)
+
+
+def local_one(tokens, segment_ids, first_gain, first_bias, w_qkv, query_gain, key_gain, w_out,
+              second_gain, second_bias, w_up, w_down, out_grad):
+    n_seq = lax.axis_size("seq")
+    own = tokens[0]
+    block_out, base, gn_rem, g, small, up_grad, down_grad = layer_call(
+        n_seq, own, out_grad[0], segment_ids, first_gain, first_bias, w_qkv, query_gain, key_gain, w_out,
+        second_gain, second_bias, w_up.T, w_down.T)
+    g, small, input_grad = sum_call(n_seq, g, small, own, gn_rem, base, first_gain)
+    qkv, proj, fg, fb, qgg, kgg, sgg, sbg = finish_call(g, small)
+    return (block_out[None], input_grad[None], fg, fb, qkv, qgg, kgg, proj, sgg, sbg, up_grad.T, down_grad.T)
 
 
 def layer_norm(rows, gain, shift):
@@ -276,38 +1075,16 @@
 
 
 def solution(mesh):
-    placed = (
-        P("seq", "pos", None),
-        P("seq", None),
-        P(),
-        P(),
-        P(),
-        P(),
-        P(),
-        P(),
-        P(),
-        P(),
-        P(None, "seq"),
-        P(None, "seq"),
-        P("seq", "pos", None),
-    )
-    return jax.shard_map(
-        local,
-        mesh=mesh,
-        in_specs=placed,
-        out_specs=(
-            P("seq", "pos", None),
-            P("seq", "pos", None),
-            P(),
-            P(),
-            P(),
-            P(),
-            P(),
-            P(),
-            P(),
-            P(),
-            P(None, "seq"),
-            P(None, "seq"),
-        ),
-        check_vma=False,
-    )
+    placed = (P("seq", "pos", None), P("seq", None), P(), P(), P(), P(), P(), P(), P(), P(),
+              P(None, "seq"), P(None, "seq"), P("seq", "pos", None))
+    outs = (P("seq", "pos", None), P("seq", "pos", None), P(), P(), P(), P(), P(), P(), P(), P(),
+            P(None, "seq"), P(None, "seq"))
+
+    def step(*args):
+        def run(*local_args):
+            one = local_args[0].shape[:2] == (1, 512) and (mesh.shape["pos"], mesh.shape["seq"]) == (2, 16)
+            return (local_one if one else local)(*local_args)
+
+        return jax.shard_map(run, mesh=mesh, in_specs=placed, out_specs=outs, check_vma=False)(*args)
+
+    return step

time: 747 us -> 225 us (0.30); the launches traced: 739 us -> 225 us
  waiting for transfers between devices: 379 us -> 0 us
  matrix products: 234 us -> 0 us
  Pallas kernels: 0 us -> 221 us
  blocking collectives: 41 us -> 0 us
  other arithmetic: 38.5 us -> 0 us
  local copies, waits for them, and re-layouts: 29.9 us -> 3.67 us
  between operations: 15.4 us -> 0.69 us
    dot_general x18 -> x0, matrix products: 234 us -> none  [the longest x1 54.4 us: backward_block(): jnp.einsum('bhqk,bqhd->bkhd', grad_scores, query_blk, preferred_element_t...]
    pallas_call x0 -> x3, Pallas kernels: none -> 221 us  [the longest x1 141 us: layer_call(): pl.pallas_call(functools.partial(layer_body, n_seq), out_shape=(sds((n, w...]
    psum x2 -> x0, waiting for transfers between devices: 159 us -> none  [the longest x1 159 us: local(): lax.psum((qkv_part, proj_part, first_gain_part, first_bias_part, query_ga...]
    reduce_scatter x4 -> x0, waiting for transfers between devices: 116 us -> none  [the longest x1 78.7 us: local(): lax.psum_scatter(down_full.astype(jnp.bfloat16), 'seq', scatter_dimension...]
    all_gather x4 -> x0, waiting for transfers between devices: 103 us -> none  [the longest x1 41.5 us: local(): lax.all_gather(w_up, 'seq', axis=1, tiled=True)]
    psum x1 -> x0, blocking collectives: 41 us -> none  [local(): lax.psum((qkv_part, proj_part, first_gain_part, first_bias_part, query_ga...]
    reduce_sum x11 -> x0, other arithmetic: 21.8 us -> none  [the longest x1 12 us: forward_block(): totals = jnp.sum(expd, axis=-1, keepdims=True)]
    unnamed x123 -> x12, local copies, waits for them, and re-layouts: 25.3 us -> 3.67 us
  transfers between devices with their start and end apart: 10 -> 0, of which waited for: 8 -> 0; matrix products, arithmetic and copies ran while one was open for 25% -> 0% of each run, Pallas kernels for 0% -> 0%
where the time goes in v2:
time: 225 us
  Pallas kernels  221 us (98%)
  local copies, waits for them, and re-layouts  3.67 us (2%)
    pallas_call x1, Pallas kernels, layer_call(): pl.pallas_call(functools.partial(layer_body, n_seq), out_shape=(sds((n, w...  141 us
    pallas_call x1, Pallas kernels, sum_call(): pl.pallas_call(functools.partial(sum_body, n_seq), out_shape=(sds((rows,...  72.4 us
    pallas_call x1, Pallas kernels, finish_call(): pl.pallas_call(finish_body, grid=(rows // step,), out_shape=(sds((rows, 3...  7.07 us

profile of v2, /device:TPU:0, one launch (start us, length us, event | category | flops | bytes accessed | tf_op | source)
XLA Modules:
  0.0 225.2 jit_solution(13270520110106542791)
XLA Ops:
  0.6 141.3 %layer.1 = (bf16[512,768]{1,0:T(8,128)(2,1)}, f32[512,768]{1,0:T(8,128)}, bf16[512,768]{1,0:T(8,128)(2,1)}, bf16[768,3072]{1,0:T(8,128)(2,1)}, f32[8,768]{1,0:T(...) custom-call(bf16[512,768]{1,0:T(8,128)(2,1)} %bitcast.8, bf16[512,768]{1,0:T(8,128)(2,1)} %bitcast.11, s32[1,1024]{1,0:T(1,128)} %seg.1, ...), custom_call_target="tpu_custom_call" | custom-call | tf_op jit(solution)/shard_map/layer/pallas_call | solution.py:772
  142.0 72.4 %sums.1 = (bf16[768,3072]{1,0:T(8,128)(2,1)}, f32[8,768]{1,0:T(8,128)}, f32[512,768]{1,0:T(8,128)}) custom-call(bf16[768,3072]{1,0:T(8,128)(2,1)} %get-tuple-element.31.g, f32[8,768]{1,0:T(8,128)} %get-tuple-element.32.small, bf16[512,768]{1,0:T(8,128)(2,1)} %bitcast.9, bf16[512,768]{1,0:T(8,128)(2,1)} %get-tuple-element.33.gn_rem, ...), custom_call_target="tpu_custom_call" | custom-call | tf_op jit(solution)/shard_map/sums/pallas_call | solution.py:278
  214.4 0.0 copy-start.1
  214.4 0.0 copy-start
  214.4 7.1 %finish.1 = (f32[768,2304]{1,0:T(8,128)}, f32[768,768]{1,0:T(8,128)}, f32[768]{0:T(1024)}, f32[768]{0:T(1024)}, f32[64]{0:T(128)}, /*index=5*/f32[64]{0:T(128)}, f32[768]{0:T(1024)}, f32[768]{0:T(1024)}) custom-call(bf16[768,3072]{1,0:T(8,128)(2,1)} %get-tuple-element.36.g, f32[8,768]{1,0:T(8,128)} %get-tuple-element.37.small), custom_call_target="tpu_custom_call" | custom-call | tf_op jit(solution)/shard_map/finish/pallas_call | solution.py:317
  221.5 0.0 copy-done.1
  221.5 0.0 copy-start.3
  221.5 0.9 copy.29
  222.4 0.0 copy-done
  222.4 0.0 copy-start.2
  222.4 1.1 copy.30
  223.6 0.0 copy-done.3
  223.6 0.8 copy.31
  224.4 0.0 copy-done.2
  224.4 0.8 copy.32
Async XLA Ops:
  214.4 7.1 %copy-start.1 = (bf16[512,768]{1,0:T(8,128)(2,1)S(1)}, bf16[512,768]{1,0:T(8,128)(2,1)}, u32[]{:S(2)}) copy-start(bf16[512,768]{1,0:T(8,128)(2,1)} %get-tuple-element.30) | copy-start | bytes 2359300
  214.4 8.0 %copy-start = (f32[512,768]{1,0:T(8,128)S(1)}, f32[512,768]{1,0:T(8,128)}, u32[]{:S(2)}) copy-start(f32[512,768]{1,0:T(8,128)} %get-tuple-element.35) | copy-start | bytes 4718596
  221.5 2.0 copy-start.3
  222.4 2.0 copy-start.2

commit v3 on v2

--- a/solution.py
+++ b/solution.py
@@ -84,8 +84,8 @@
 SPLIT = 2
 
 
-def sum_body(n_seq, g, small, own, gn_rem, base, g1, fin, sout, igrad,
-             pbuf, accin, accout, xin, xout, srec, sring, gback,
+def sum_body(n_seq, g, small, own, gn_rem, base, g1, mine, fin, sout, igrad, upg, downg,
+             other, pbuf, accin, accout, xin, xout, srec, sring, gback,
              psend, precv, asend, arecv, xsend, xrecv, fsend, frecv, qsend, qrecv, ssend, srecv, gsend, grecv):
     rows, cols = g.shape
     chips = n_seq // 2
@@ -148,6 +148,7 @@
     back = copy_to(gn_rem, gback, gsend.at[0], grecv.at[0], across)
     small_p = copy_to(small, srec.at[0], gsend.at[1], grecv.at[1], partner)
     small_x = copy_to(srec.at[1], srec.at[2], gsend.at[2], grecv.at[2], across)
+    ffn_x = copy_to(mine, other, gsend.at[3], grecv.at[3], across)
 
     def order(s):
         return chunk(place - s), chunk(place + s)
@@ -158,6 +159,7 @@
             p_copy(q).start()
     p_copy(place).start()
     back.start()
+    ffn_x.start()
 
     def part(d, k, q):
         cs = at(d, k)
@@ -208,6 +210,10 @@
         return c
 
     lax.fori_loop(0, n // TILE, norm_tile, 0)
+    ffn_x.wait_recv()
+    total = mine[...].astype(F32) + other[...].astype(F32)
+    upg[...] = total[0]
+    downg[...] = total[1]
     small_x.wait_recv()
     sring[place] = srec[1] + srec[2]
     s_copy(0).start()
@@ -265,11 +271,11 @@
     lax.fori_loop(0, chips, drain, 0)
     for d, k in both:
         x_copy(d, k).wait_send()
-    for c in (back, small_p, small_x):
+    for c in (back, small_p, small_x, ffn_x):
         c.wait_send()
 
 
-def sum_call(n_seq, g, small, own, gn_rem, base, g1):
+def sum_call(n_seq, g, small, own, gn_rem, base, g1, mine):
     rows, cols = g.shape
     n, width = own.shape
     chips = n_seq // 2
@@ -277,19 +283,21 @@
     V, D = pltpu.VMEM, pltpu.SemaphoreType.DMA
     return pl.pallas_call(
         functools.partial(sum_body, n_seq),
-        out_shape=(sds((rows, cols), BF16), sds(small.shape, F32), sds((n, width), F32)),
-        in_specs=[VM] * 6, out_specs=(VM,) * 3,
+        out_shape=(sds((rows, cols), BF16), sds(small.shape, F32), sds((n, width), F32),
+                   sds(mine.shape[1:], F32), sds(mine.shape[1:], F32)),
+        in_specs=[VM] * 7, out_specs=(VM,) * 5,
         scratch_shapes=[
+            V(mine.shape, BF16),
             V((chips, cr, cols), BF16), V((chips - 1, lanes, cr, cw), BF16), V((chips - 1, lanes, cr, cw), BF16),
             V((lanes, cr, cw), BF16), V((lanes, cr, cw), BF16),
             V((3,) + small.shape, F32), V((chips,) + small.shape, F32), V((n, width), BF16),
             D((chips,)), D((chips,)), D((chips - 1, lanes)), D((chips - 1, lanes)), D((lanes,)), D((lanes,)),
             D((chips - 1, lanes)), D((chips - 1, lanes)), D((chips, lanes)), D((chips, lanes)),
-            D((chips - 1,)), D((chips - 1,)), D((3,)), D((3,))],
+            D((chips - 1,)), D((chips - 1,)), D((4,)), D((4,))],
         compiler_params=pltpu.CompilerParams(
             vmem_limit_bytes=LIMIT, collective_id=2, has_side_effects=True),
         name="sums",
-    )(g, small, own, gn_rem, base, g1)
+    )(g, small, own, gn_rem, base, g1, mine)
 
 
 def finish_body(g, small, qkv, proj, fg, fb, qgg, kgg, sgg, sbg):
@@ -326,11 +334,11 @@
 
 
 def layer_body(n_seq, own, gy, seg, g1, b1, wqkv, qg, kg, wout, g2, b2, wup, wdown,
-               out, base, gn_rem, gall, small, upg, downg,
+               out, base, gn_rem, gall, small, mine,
                rem, fq, fk, ones, swap, vecs, normed, kk, vv, qq, rq, rk, qaug, att, mid,
-               sx, sg, wbuf, accin, accout, first, hid, gpre, blk, gs, prec, mine, xin,
+               sx, sg, wbuf, accin, accout, first, hid, gpre, blk, gs, prec,
                dk, stage,
-               wsend, wrecv, asend, arecv, psend, precv, tsend, trecv, xsend, xrecv, gsem):
+               wsend, wrecv, asend, arecv, psend, precv, tsend, trecv, gsem):
     n, width = own.shape
     f = wup.shape[0]
     h = f // 2
@@ -345,30 +353,38 @@
     def slot(s, k, d):
         return pl.ds(pl.multiple_of((k * chips + s) * f + d * h, h), h)
 
-    def w_copies(s):
-        return [copy_to(wbuf.at[slot(s, k, d)], wbuf.at[slot(s + 1, k, d)], wsend.at[d, k, s], wrecv.at[d, k, s],
-                        left if d else right) for d in range(2) for k in range(2)]
-
-    def a_copies(s):
+    def w_copies(s, k):
+        return [copy_to(wbuf.at[slot(s, k, d)] if s else (wdown if k else wup).at[pl.ds(d * h, h)],
+                        wbuf.at[slot(s + 1, k, d)], wsend.at[d, k, s], wrecv.at[d, k, s],
+                        left if d else right) for d in range(2)]
+
+    def a_copies(s, k):
         rows = [pl.ds(d * h, h) for d in range(2)]
-        return [copy_to(accout.at[s - 1, :, rows[d]], accin.at[s - 1, :, rows[d]], asend.at[d, s - 1],
-                        arecv.at[d, s - 1], left if d else right) for d in range(2)]
-
-    def w_step(s):
-        for c in w_copies(s - 1):
+        return [copy_to(accout.at[s - 1, k, rows[d]], accin.at[s - 1, k, rows[d]], asend.at[d, k, s - 1],
+                        arecv.at[d, k, s - 1], left if d else right) for d in range(2)]
+
+    def w_step(i):
+        s, k = i // 2 + 1, i % 2
+        for c in w_copies(s - 1, k):
             c.wait_recv()
-
-        @pl.when(s < chips - 1)
-        def _():
-            for c in w_copies(s):
+        if s < chips - 1:
+            for c in w_copies(s, k):
                 c.start()
 
-    def r_step(s):
-        for c in a_copies(s - 1):
+    def r_step(j):
+        s, k = j // 2 + 1, j % 2
+        for c in a_copies(s, k):
             c.wait_recv()
-        accout[s - 1] = (accout[s - 1].astype(F32) + accin[s - 2].astype(F32)).astype(BF16)
-        for c in a_copies(s):
-            c.start()
+        if s < chips - 1:
+            accout[s, k] = (accout[s, k].astype(F32) + accin[s - 1, k].astype(F32)).astype(BF16)
+            for c in a_copies(s + 1, k):
+                c.start()
+
+    def at_points(now, points, step):
+        for when, item in points:
+            @pl.when(now == when)
+            def _():
+                step(item)
 
     def t_copy(i):
         rows = pl.ds(i * TILE, TILE)
@@ -381,14 +397,10 @@
     gy_copy = copy_to(gy, sg.at[pl.ds(n, n)], psend.at[0], precv.at[0], partner)
     parts = (copy_to(gs.at[pl.ds(n, n)], prec.at[1], psend.at[1], precv.at[1], partner),
              copy_to(blk.at[pl.ds(n, n)], prec.at[0], psend.at[2], precv.at[2], partner))
-    x_copy = copy_to(mine, xin, xsend.at[0], xrecv.at[0], across)
-
-    def w_first():
-        return [copy_to((wdown if k else wup).at[pl.ds(d * h, h)], wbuf.at[slot(1, k, d)], wsend.at[d, k, 0],
-                        wrecv.at[d, k, 0], left if d else right) for d in range(2) for k in range(2)]
-
-    for c in w_first():
-        c.start()
+
+    for k in range(2):
+        for c in w_copies(0, k):
+            c.start()
     for i in range(tiles):
         t_copy(i).start()
     gy_copy.start()
@@ -437,7 +449,7 @@
         return c
 
     lax.fori_loop(0, tiles, own_tile, 0)
-    w_step(1)
+    w_step(0)
     lane_t = lax.broadcasted_iota(jnp.int32, (TILE, 128), 1)
     low_t = lane_t < 64
     lane_n = lax.broadcasted_iota(jnp.int32, (n, 128), 1)
@@ -466,17 +478,14 @@
 
         lax.fori_loop(0, pairs, pair, 0)
 
-    def middle_step(p):
-        @pl.when(p == 2)
-        def _():
-            w_step(2)
-
-    attend(slice(0, n), n, False, middle_step)
+    attend(slice(0, n), n, False, lambda p: at_points(p, ((1, 1), (4, 2)), w_step))
     for i in range(tiles):
         t_copy(i).wait_recv()
         project(rem[i * TILE:(i + 1) * TILE, :].astype(F32), tiles + i, False)
-        w_step(3 + i)
-        attend(slice(n + i * TILE, n + (i + 1) * TILE), TILE, True, None)
+        if i == 0:
+            w_step(3)
+        attend(slice(n + i * TILE, n + (i + 1) * TILE), TILE, True,
+               lambda p: at_points(p, ((1, 5),) if i else ((5, 4),), w_step))
 
     def close(p, c):
         lanes = tile_of(p, 128)
@@ -502,69 +511,46 @@
         return c
 
     lax.fori_loop(0, pairs, close, 0)
+    w_step(6)
     for i in range(tiles):
         rows = slice(i * TILE, (i + 1) * TILE)
         m = own[rows, :].astype(F32) + dot(att[rows, :], wout[...])
         mid[rows, :] = m
         sx[rows, :] = (rows_norm(m)[0] * vecs[2:3, :] + vecs[3:4, :]).astype(BF16)
         s_copy(i).start()
-    w_step(5)
     quad = chips // 2
-    span = quad * f
-
-    def group(g, carry):
-        @pl.when(g == 0)
-        def _():
-            gy_copy.wait_recv()
-            for j in range(tiles):
-                s_copy(j).wait_recv()
-
-        @pl.when(g == 1)
-        def _():
-            w_step(6)
-            w_step(7)
-
-        up = wbuf.at[pl.ds(pl.multiple_of(g * span, span), span)]
-        down = wbuf.at[pl.ds(pl.multiple_of(chips * f + g * span, span), span)]
+    gy_copy.wait_recv()
+    for j in range(tiles):
+        s_copy(j).wait_recv()
+
+    def feed(begin, span, lanes, turn, after):
+        up = wbuf.at[begin:begin + span]
+        down = wbuf.at[chips * f + begin:chips * f + begin + span]
 
         def tile(i, c):
-            rows = tile_of((i + g * tiles) % (2 * tiles))
+            rows = tile_of((i + turn) % (2 * tiles))
             acts, slopes = [], []
             for j in range(span // TILE):
                 cs = slice(j * TILE, (j + 1) * TILE)
+                to = slice(lanes + j * TILE, lanes + (j + 1) * TILE)
                 pre = dot(sx[rows, :], up[cs, :], NT)
                 gh = dot(sg[rows, :], down[cs, :], NT)
                 cdf = 0.5 + 0.5 * lax.erf(pre * 0.7071067811865476)
                 slope = cdf + pre * (jnp.exp(-0.5 * pre * pre) * 0.3989422804014327)
                 acts.append((pre * cdf).astype(BF16))
                 slopes.append((gh * slope).astype(BF16))
-                hid[rows, cs] = acts[-1]
-                gpre[rows, cs] = slopes[-1]
+                hid[rows, to] = acts[-1]
+                gpre[rows, to] = slopes[-1]
             o = dot(jnp.concatenate(acts, 1), down[...])
-            s = dot(jnp.concatenate(slopes, 1), up[...])
-
-            @pl.when(g == 0)
-            def _():
-                blk[rows, :] = o
-                gs[rows, :] = s
-
-            @pl.when(g > 0)
-            def _():
-                blk[rows, :] += o
-                gs[rows, :] += s
-
-            @pl.when((g == 1) & (i == tiles - 1))
-            def _():
-                for c in parts:
-                    c.start()
+            t = dot(jnp.concatenate(slopes, 1), up[...])
+            blk[rows, :] = blk[rows, :] + o if begin else o
+            gs[rows, :] = gs[rows, :] + t if begin else t
+            after(i)
             return c
 
         lax.fori_loop(0, 2 * tiles, tile, 0)
 
-        @pl.when(g == 1)
-        def _():
-            r_step(2)
-
+    def outer(g):
         def block(j, c):
             for k, (lhs, rhs) in enumerate(((gpre, sx), (hid, sg))):
                 part = dot(lhs[:, pl.ds(pl.multiple_of(j * 2 * f, 2 * f), 2 * f)], rhs[...], TN)
@@ -583,23 +569,33 @@
 
         lax.fori_loop(0, quad // 2, block, 0)
 
-        @pl.when(g == 0)
+    half_way = quad * f
+    last = 2 * quad * f - TILE
+    feed(0, half_way, 0, 0, lambda i: at_points(i, ((0, 7), (1, 8), (3, 9)), w_step))
+    outer(0)
+    w_step(10)
+    w_step(11)
+    for k in range(2):
+        for c in a_copies(1, k):
+            c.start()
+    feed(half_way, last - half_way, 0, tiles, lambda i: None)
+    w_step(12)
+    w_step(13)
+
+    def send_parts(i):
+        @pl.when(i == tiles - 1)
         def _():
-            for c in a_copies(1):
+            for c in parts:
                 c.start()
-        return carry
-
-    lax.fori_loop(0, 2, group, 0)
-    r_step(3)
-
-    def w_drain(s, c):
-        for cp in w_copies(s):
-            cp.wait_send()
-        return c
-
-    lax.fori_loop(1, chips - 1, w_drain, 0)
-    for c in w_first():
-        c.wait_send()
+
+    feed(last, TILE, last - half_way, tiles, send_parts)
+    r_step(0)
+    outer(1)
+
+    for j in range(chips - 1):
+        for k in range(2):
+            for c in w_copies(j, k):
+                c.wait_send()
     for i in range(tiles):
         s_copy(i).wait_send()
     gbr, gat = sx.at[0:n], sx.at[n:2 * n]
@@ -622,6 +618,7 @@
         return c
 
     lax.fori_loop(0, tiles, mid_tile, 0)
+    r_step(1)
     parts[1].wait_recv()
     out[...] = (mid[...] + (blk[0:n, :] + prec[0])).astype(BF16)
 
@@ -635,7 +632,6 @@
         return c
 
     lax.fori_loop(0, width // TILE, proj_tile, 0)
-    r_step(4)
 
     def keys_of(j, rows):
         return wbuf.at[pl.ds(pl.multiple_of(j * 2 * n + rows, TILE), TILE)]
@@ -657,10 +653,7 @@
         return r * (gd - m1 - y * inv * m2), jnp.sum(prod, 0, keepdims=True) * inv
 
     def pair(p, c):
-        @pl.when((p == 1) | (p == 3) | (p == 4))
-        def _():
-            r_step(5 + p // 2)
-
+        at_points(p, ((1, 3), (2, 4), (4, 7), (5, 8)), r_step)
         lanes = tile_of(p, 128)
         do = gat[:, lanes]
         delta = -group_sum(do.astype(F32) * att[:, lanes].astype(F32), swap[...])
@@ -674,6 +667,8 @@
 
         acc = [None, None]
         for t in range(2):
+            if t:
+                at_points(p, ((0, 2), (2, 5), (3, 6)), r_step)
             rows = slice(t * n, (t + 1) * n)
             k, v, feat = kk[rows, lanes], vv[rows, lanes], fk[rows, :]
             one = jnp.ones_like(v)
@@ -704,10 +699,7 @@
     lax.fori_loop(0, pairs, pair, 0)
     for i in range(width // TILE):
         flush(i, pl.ds(i * TILE, TILE), pl.ds(3 * width, width)).wait()
-    for c in a_copies(chips - 1):
-        c.wait_recv()
-    mine[...] = (first[...] + accin[chips - 2].astype(F32)).astype(BF16)
-    x_copy.start()
+    r_step(9)
 
     def gain_sums(xh, gn):
         small[0:1, :] += jnp.sum(gn * xh, axis=0, keepdims=True)
@@ -740,25 +732,22 @@
             flush(j, rows, pl.ds(part * width, width)).start()
         for j, (at, size, part) in enumerate(jobs):
             flush(j, rows, pl.ds(part * width, width)).wait()
+        at_points(i, ((0, 10), (2, 11)), r_step)
         return c
 
     lax.fori_loop(0, width // TILE, qkv_tile, 0)
     lax.fori_loop(0, tiles, rem_tile, 0)
+    r_step(12)
     lax.fori_loop(0, tiles, own_back, 0)
-    x_copy.wait_recv()
-    total = mine[...].astype(F32) + xin[...].astype(F32)
-    upg[...] = total[0]
-    downg[...] = total[1]
-
-    def a_drain(s, c):
-        for cp in a_copies(s):
-            cp.wait_send()
-        return c
-
-    lax.fori_loop(1, chips, a_drain, 0)
+    r_step(13)
+    mine[...] = (first[...] + accin[chips - 2].astype(F32)).astype(BF16)
+    for j in range(1, chips):
+        for k in range(2):
+            for c in a_copies(j, k):
+                c.wait_send()
     for i in range(tiles):
         t_copy(i).wait_send()
-    for c in (gy_copy, x_copy) + parts:
+    for c in (gy_copy,) + parts:
         c.wait_send()
 
 
@@ -772,9 +761,9 @@
     return pl.pallas_call(
         functools.partial(layer_body, n_seq),
         out_shape=(sds((n, width), BF16), sds((n, width), F32), sds((n, width), BF16),
-                   sds((width, 4 * width), BF16), sds((8, width), F32), sds((f, width), F32), sds((f, width), F32)),
+                   sds((width, 4 * width), BF16), sds((8, width), F32), sds((2, f, width), BF16)),
         in_specs=[VM] * 13,
-        out_specs=(VM, VM, VM, pl.BlockSpec(memory_space=pl.ANY), VM, VM, VM),
+        out_specs=(VM, VM, VM, pl.BlockSpec(memory_space=pl.ANY), VM, VM),
         scratch_shapes=[
             V((n, width), BF16), V((n, 128), BF16), V((2 * n, 128), BF16), V((256, 256), BF16), V((128, 128), BF16),
             V((8, width), F32), V((2 * n, width), BF16), V((2 * n, width), BF16), V((2 * n, width), BF16),
@@ -783,10 +772,10 @@
             V((2 * n, width), BF16), V((2 * n, width), BF16), V((chips * 2 * f, width), BF16),
             V((chips - 1, 2, f, width), BF16), V((chips - 1, 2, f, width), BF16), V((2, f, width), F32),
             V((2 * n, chips // 2 * f), BF16), V((2 * n, chips // 2 * f), BF16), V((2 * n, width), F32), V((2 * n, width), F32),
-            V((2, n, width), F32), V((2, f, width), BF16), V((2, f, width), BF16),
+            V((2, n, width), F32),
             V((2 * n, 128), F32), V((3, TILE, width), BF16),
-            D((2, 2, chips - 1)), D((2, 2, chips - 1)), D((2, chips - 1)), D((2, chips - 1)),
-            D((3 + tiles,)), D((3 + tiles,)), D((tiles,)), D((tiles,)), D((1,)), D((1,)), D((3,))],
+            D((2, 2, chips - 1)), D((2, 2, chips - 1)), D((2, 2, chips - 1)), D((2, 2, chips - 1)),
+            D((3 + tiles,)), D((3 + tiles,)), D((tiles,)), D((tiles,)), D((3,))],
         compiler_params=pltpu.CompilerParams(
             vmem_limit_bytes=66 * 1000 * 1000, collective_id=1, has_side_effects=True),
         name="layer",
@@ -797,10 +786,10 @@
               second_gain, second_bias, w_up, w_down, out_grad):
     n_seq = lax.axis_size("seq")
     own = tokens[0]
-    block_out, base, gn_rem, g, small, up_grad, down_grad = layer_call(
+    block_out, base, gn_rem, g, small, mine = layer_call(
         n_seq, own, out_grad[0], segment_ids, first_gain, first_bias, w_qkv, query_gain, key_gain, w_out,
         second_gain, second_bias, w_up.T, w_down.T)
-    g, small, input_grad = sum_call(n_seq, g, small, own, gn_rem, base, first_gain)
+    g, small, input_grad, up_grad, down_grad = sum_call(n_seq, g, small, own, gn_rem, base, first_gain, mine)
     qkv, proj, fg, fb, qgg, kgg, sgg, sbg = finish_call(g, small)
     return (block_out[None], input_grad[None], fg, fb, qkv, qgg, kgg, proj, sgg, sbg, up_grad.T, down_grad.T)
 

time: 225 us -> 195 us (0.87)
  Pallas kernels: 221 us -> 190 us
    pallas_call x1, Pallas kernels: 141 us -> 106 us  [layer_call(): pl.pallas_call(functools.partial(layer_body, n_seq), out_shape=(sds((n, w...]
    pallas_call x1, Pallas kernels: 72.4 us -> 77.1 us  [sum_call(): pl.pallas_call(functools.partial(sum_body, n_seq), out_shape=(sds((rows,...]
where the time goes in v3:
time: 195 us
  Pallas kernels  190 us (97%)
  local copies, waits for them, and re-layouts  3.67 us (2%)
    pallas_call x1, Pallas kernels, layer_call(): pl.pallas_call(functools.partial(layer_body, n_seq), out_shape=(sds((n, w...  106 us
    pallas_call x1, Pallas kernels, sum_call(): pl.pallas_call(functools.partial(sum_body, n_seq), out_shape=(sds((rows,...  77.1 us
    pallas_call x1, Pallas kernels, finish_call(): pl.pallas_call(finish_body, grid=(rows // step,), out_shape=(sds((rows, 3...  7.07 us

profile of v3, /device:TPU:0, one launch (start us, length us, event | category | flops | bytes accessed | tf_op | source)
XLA Modules:
  0.0 194.8 jit_solution(18395362667996701465)
XLA Ops:
  0.6 106.3 %layer.1 = (bf16[512,768]{1,0:T(8,128)(2,1)}, f32[512,768]{1,0:T(8,128)}, bf16[512,768]{1,0:T(8,128)(2,1)}, bf16[768,3072]{1,0:T(8,128)(2,1)}, f32[8,768]{1,0:T(8,128)}, /*index=5*/bf16[2,192,768]{2,1,0:T(8,128)(2,1)}) custom-call(bf16[512,768]{1,0:T(8,128)(2,1)} %bitcast.8, bf16[512,768]{1,0:T(8,128)(2,1)} %bitcast.11, s32[1,1024]{1,0:T(1,128)} %seg.1, ...), custom_call_target="tpu_custom_call" | custom-call | tf_op jit(solution)/shard_map/layer/pallas_call | solution.py:761
  106.9 77.1 %sums.1 = (bf16[768,3072]{1,0:T(8,128)(2,1)}, f32[8,768]{1,0:T(8,128)}, f32[512,768]{1,0:T(8,128)}, f32[192,768]{1,0:T(8,128)}, f32[192,768]{1,0:T(8,128)}) custom-call(bf16[768,3072]{1,0:T(8,128)(2,1)} %get-tuple-element.32.g, f32[8,768]{1,0:T(8,128)} %get-tuple-element.33.small, bf16[512,768]{1,0:T(8,128)(2,1)} %bitcast.9, ...), custom_call_target="tpu_custom_call" | custom-call | tf_op jit(solution)/shard_map/sums/pallas_call | solution.py:284
  184.0 0.0 copy-start.1
  184.0 0.0 copy-start
  184.0 7.1 %finish.1 = (f32[768,2304]{1,0:T(8,128)}, f32[768,768]{1,0:T(8,128)}, f32[768]{0:T(1024)}, f32[768]{0:T(1024)}, f32[64]{0:T(128)}, /*index=5*/f32[64]{0:T(128)}, f32[768]{0:T(1024)}, f32[768]{0:T(1024)}) custom-call(bf16[768,3072]{1,0:T(8,128)(2,1)} %get-tuple-element.38.g, f32[8,768]{1,0:T(8,128)} %get-tuple-element.39.small), custom_call_target="tpu_custom_call" | custom-call | tf_op jit(solution)/shard_map/finish/pallas_call | solution.py:325
  191.1 0.0 copy-done.1
  191.1 0.0 copy-start.3
  191.1 0.9 copy.29
  192.0 0.0 copy-done
  192.0 0.0 copy-start.2
  192.0 1.1 copy.30
  193.1 0.0 copy-done.3
  193.1 0.8 copy.31
  193.9 0.0 copy-done.2
  193.9 0.8 copy.32
Async XLA Ops:
  184.0 7.1 %copy-start.1 = (bf16[512,768]{1,0:T(8,128)(2,1)S(1)}, bf16[512,768]{1,0:T(8,128)(2,1)}, u32[]{:S(2)}) copy-start(bf16[512,768]{1,0:T(8,128)(2,1)} %get-tuple-element.31) | copy-start | bytes 2359300
  184.0 8.0 %copy-start = (f32[512,768]{1,0:T(8,128)S(1)}, f32[512,768]{1,0:T(8,128)}, u32[]{:S(2)}) copy-start(f32[512,768]{1,0:T(8,128)} %get-tuple-element.37) | copy-start | bytes 4718596
  191.1 2.0 %copy-start.3 = (f32[192,768]{1,0:T(8,128)S(1)}, f32[192,768]{1,0:T(8,128)}, u32[]{:S(2)}) copy-start(f32[192,768]{1,0:T(8,128)} %get-tuple-element.48) | copy-start | bytes 1769476
  192.0 2.0 %copy-start.2 = (f32[192,768]{1,0:T(8,128)S(1)}, f32[192,768]{1,0:T(8,128)}, u32[]{:S(2)}) copy-start(f32[192,768]{1,0:T(8,128)} %get-tuple-element.49) | copy-start | bytes 1769476

commit v4 on v3

--- a/solution.py
+++ b/solution.py
@@ -81,17 +81,12 @@
     pl.semaphore_wait(barrier, len(targets))
 
 
-SPLIT = 2
-
-
-def sum_body(n_seq, g, small, own, gn_rem, base, g1, mine, fin, sout, igrad, upg, downg,
-             other, pbuf, accin, accout, xin, xout, srec, sring, gback,
-             psend, precv, asend, arecv, xsend, xrecv, fsend, frecv, qsend, qrecv, ssend, srecv, gsend, grecv):
-    rows, cols = g.shape
+def sum_body(n_seq, quarter, small, gn_rem, mine, fin, sout, gback, other,
+             accin, accout, srec, sring,
+             asend, arecv, xsend, xrecv, fsend, frecv, qsend, qrecv, ssend, srecv, gsend, grecv):
+    qrows, cols = quarter.shape
     chips = n_seq // 2
-    half = rows // 2
-    cr = half // chips
-    cw = cols // (2 * SPLIT)
+    cw, pr, hr = cols // chips, qrows // 4, qrows // 2
     core, place, right, left, partner = ring_places(n_seq)
     x = lax.axis_index("pos")
     right, left, partner, across = {"seq": right}, {"seq": left}, {"seq": partner}, {"pos": 1 - x}
@@ -100,42 +95,33 @@
     def chunk(p):
         return (p + 2 * chips) % chips
 
-    def at(d, k):
-        return pl.ds((d * SPLIT + k) * cw, cw)
-
-    def rows_of(c, p):
-        return pl.ds(pl.multiple_of(c * half + p * cr, cr), cr)
-
-    def p_copy(q):
-        return copy_to(g.at[rows_of(1 - core, q)], pbuf.at[q], psend.at[q], precv.at[q], partner)
-
-    def a_copy(d, k, s):
-        return copy_to(accout.at[s, d * SPLIT + k], accin.at[s, d * SPLIT + k], asend.at[s, d * SPLIT + k],
-                       arecv.at[s, d * SPLIT + k], left if d else right)
-
-    def x_copy(d, k):
-        i = d * SPLIT + k
-        return copy_to(xout.at[i], xin.at[i], xsend.at[i], xrecv.at[i], across)
-
-    def f_copy(d, k, s):
-        p = chunk(place + s) if d else chunk(place - s)
-        ref = fin.at[rows_of(core, p), at(d, k)]
-        return copy_to(ref, ref, fsend.at[s, d * SPLIT + k], frecv.at[s, d * SPLIT + k], left if d else right)
-
-    def f_recv(d, k, s):
-        p = chunk(place + s + 1) if d else chunk(place - s - 1)
-        ref = fin.at[rows_of(core, p), at(d, k)]
-        return copy_to(ref, ref, fsend.at[s, d * SPLIT + k], frecv.at[s, d * SPLIT + k], left if d else right)
-
-    def q_copy(d, k, s):
-        p = chunk(place + s) if d else chunk(place - s)
-        ref = fin.at[rows_of(core, p), at(d, k)]
-        return copy_to(ref, ref, qsend.at[s, d * SPLIT + k], qrecv.at[s, d * SPLIT + k], partner)
-
-    def q_recv(d, k, s):
-        p = chunk(place + s) if d else chunk(place - s)
-        ref = fin.at[rows_of(1 - core, p), at(d, k)]
-        return copy_to(ref, ref, qsend.at[s, d * SPLIT + k], qrecv.at[s, d * SPLIT + k], partner)
+    def lanes_of(p):
+        return pl.ds(pl.multiple_of(p * cw, cw), cw)
+
+    def rows_of(c, o, d):
+        side = 1 - x if o else x
+        return pl.ds(pl.multiple_of(c * 2 * qrows + side * qrows + d * hr, hr), hr)
+
+    def a_copy(i, s):
+        return copy_to(accout.at[s, i], accin.at[s, i], asend.at[s, i], arecv.at[s, i], left if i // 2 else right)
+
+    def x_piece(i, side, p):
+        ref = fin.at[pl.ds(pl.multiple_of(core * 2 * qrows + side * qrows + i * pr, pr), pr), lanes_of(p)]
+        return copy_to(ref, ref, xsend.at[i], xrecv.at[i], across)
+
+    def ring_copy(d, o, s, p):
+        ref = fin.at[rows_of(core, o, d), lanes_of(p)]
+        return copy_to(ref, ref, fsend.at[s, d * 2 + o], frecv.at[s, d * 2 + o], left if d else right)
+
+    def f_copy(d, o, s):
+        return ring_copy(d, o, s, chunk(place + s) if d else chunk(place - s))
+
+    def f_recv(d, o, s):
+        return ring_copy(d, o, s, chunk(place + s + 1) if d else chunk(place - s - 1))
+
+    def pair_copy(c, d, o, s):
+        ref = fin.at[rows_of(c, o, d), lanes_of(chunk(place + s) if d else chunk(place - s))]
+        return copy_to(ref, ref, qsend.at[s, d * 2 + o], qrecv.at[s, d * 2 + o], partner)
 
     def s_copy(s):
         return copy_to(sring.at[chunk(place - s)], sring.at[chunk(place - s)], ssend.at[s], srecv.at[s], right)
@@ -144,95 +130,69 @@
         p = chunk(place - s - 1)
         return copy_to(sring.at[p], sring.at[p], ssend.at[s], srecv.at[s], right)
 
-    both = [(d, k) for k in range(SPLIT) for d in range(2)]
     back = copy_to(gn_rem, gback, gsend.at[0], grecv.at[0], across)
     small_p = copy_to(small, srec.at[0], gsend.at[1], grecv.at[1], partner)
     small_x = copy_to(srec.at[1], srec.at[2], gsend.at[2], grecv.at[2], across)
     ffn_x = copy_to(mine, other, gsend.at[3], grecv.at[3], across)
-
-    def order(s):
-        return chunk(place - s), chunk(place + s)
+    pieces = (0, 2, 1, 3)
+    both = [(d, o) for o in range(2) for d in range(2)]
 
     small_p.start()
-    for s in range(1, chips // 2 + 1):
-        for q in order(s)[: 1 if 2 * s == chips else 2]:
-            p_copy(q).start()
-    p_copy(place).start()
-    back.start()
-    ffn_x.start()
-
-    def part(d, k, q):
-        cs = at(d, k)
-        return g[rows_of(core, q), cs].astype(F32) + pbuf[q, :, cs].astype(F32)
+
+    def part(i, q):
+        return quarter[i * pr:(i + 1) * pr, lanes_of(q)].astype(F32)
 
     def reduce_step(s, c):
-        @pl.when(s <= chips // 2)
-        def _():
-            p_copy(chunk(place - s)).wait_recv()
-
-            @pl.when(2 * s < chips)
-            def _():
-                p_copy(chunk(place + s)).wait_recv()
-
-        for d, k in both:
-            q = chunk(place + s) if d else chunk(place - s)
+        for i in pieces:
+            q = chunk(place + s) if i // 2 else chunk(place - s)
 
             @pl.when(s == 1)
             def _():
-                accout[s - 1, d * SPLIT + k] = part(d, k, q).astype(BF16)
+                accout[s - 1, i] = part(i, q).astype(BF16)
 
             @pl.when(s > 1)
             def _():
-                a_copy(d, k, s - 2).wait_recv()
-                accout[s - 1, d * SPLIT + k] = (part(d, k, q) + accin[s - 2, d * SPLIT + k].astype(F32)).astype(BF16)
-
-            a_copy(d, k, s - 1).start()
+                a_copy(i, s - 2).wait_recv()
+                accout[s - 1, i] = (part(i, q) + accin[s - 2, i].astype(F32)).astype(BF16)
+
+            a_copy(i, s - 1).start()
+
+        @pl.when(s == 1)
+        def _():
+            back.start()
+            small_p.wait_recv()
+            srec[1] = small[...] + srec[0]
+            small_x.start()
         return c
 
     lax.fori_loop(1, chips, reduce_step, 0)
-    p_copy(place).wait_recv()
-    for d, k in both:
-        a_copy(d, k, chips - 2).wait_recv()
-        xout[d * SPLIT + k] = (part(d, k, place) + accin[chips - 2, d * SPLIT + k].astype(F32)).astype(BF16)
-        x_copy(d, k).start()
-    small_p.wait_recv()
-    srec[1] = small[...] + srec[0]
-    small_x.start()
-    back.wait_recv()
-    n = own.shape[0]
-
-    def norm_tile(i, c):
-        rs = tile_of(i)
-        xh, r = rows_norm(own[rs, :].astype(F32))
-        dy = gback[rs, :].astype(F32) * g1[...].reshape(1, -1)
-        dx = r * (dy - jnp.mean(dy, -1, keepdims=True) - xh * jnp.mean(dy * xh, -1, keepdims=True))
-        igrad[rs, :] = base[rs, :] + dx
-        return c
-
-    lax.fori_loop(0, n // TILE, norm_tile, 0)
-    ffn_x.wait_recv()
-    total = mine[...].astype(F32) + other[...].astype(F32)
-    upg[...] = total[0]
-    downg[...] = total[1]
+    for i in pieces:
+        a_copy(i, chips - 2).wait_recv()
+        at = pl.ds(pl.multiple_of(core * 2 * qrows + x * qrows + i * pr, pr), pr)
+        fin[at, lanes_of(place)] = (part(i, place) + accin[chips - 2, i].astype(F32)).astype(BF16)
+        x_piece(i, x, place).start()
+        if i % 2:
+            f_copy(i // 2, 0, 0).start()
+            pair_copy(core, i // 2, 0, 0).start()
     small_x.wait_recv()
     sring[place] = srec[1] + srec[2]
     s_copy(0).start()
-    for d, k in both:
-        x_copy(d, k).wait_recv()
-        i = d * SPLIT + k
-        fin[rows_of(core, place), at(d, k)] = (xout[i].astype(F32) + xin[i].astype(F32)).astype(BF16)
-        f_copy(d, k, 0).start()
-        q_copy(d, k, 0).start()
+    for i in pieces:
+        x_piece(i, 1 - x, place).wait_recv()
+        if i % 2:
+            f_copy(i // 2, 1, 0).start()
+            pair_copy(core, i // 2, 1, 0).start()
+    ffn_x.start()
 
     def gather_step(s, c):
-        for d, k in both:
-            f_recv(d, k, s - 1).wait_recv()
+        for d, o in both:
+            f_recv(d, o, s - 1).wait_recv()
 
             @pl.when(s < chips - 1)
             def _():
-                f_copy(d, k, s).start()
-
-            q_copy(d, k, s).start()
+                f_copy(d, o, s).start()
+
+            pair_copy(core, d, o, s).start()
         s_recv(s - 1).wait_recv()
 
         @pl.when(s < chips - 1)
@@ -243,67 +203,78 @@
     lax.fori_loop(1, chips, gather_step, 0)
 
     def finish(s, c):
-        for d, k in both:
-            q_recv(d, k, s).wait_recv()
+        for d, o in both:
+            pair_copy(1 - core, d, o, s).wait_recv()
         return c
 
-    lax.fori_loop(0, chips, finish, 0)
     total = sring[0]
     for s in range(1, chips):
         total = total + sring[s]
     sout[...] = total
+    lax.fori_loop(0, chips, finish, 0)
+    back.wait_recv()
+    ffn_x.wait_recv()
 
     def drain(s, c):
-        for d, k in both:
-            q_copy(d, k, s).wait_send()
+        for d, o in both:
+            pair_copy(core, d, o, s).wait_send()
 
             @pl.when(s < chips - 1)
             def _():
-                a_copy(d, k, s).wait_send()
-                f_copy(d, k, s).wait_send()
+                a_copy(d * 2 + o, s).wait_send()
+                f_copy(d, o, s).wait_send()
 
         @pl.when(s < chips - 1)
         def _():
             s_copy(s).wait_send()
-        p_copy(s).wait_send()
         return c
 
     lax.fori_loop(0, chips, drain, 0)
-    for d, k in both:
-        x_copy(d, k).wait_send()
+    for i in pieces:
+        x_piece(i, x, place).wait_send()
     for c in (back, small_p, small_x, ffn_x):
         c.wait_send()
 
 
-def sum_call(n_seq, g, small, own, gn_rem, base, g1, mine):
-    rows, cols = g.shape
-    n, width = own.shape
+def sum_call(n_seq, quarter, small, gn_rem, mine):
+    qrows, cols = quarter.shape
     chips = n_seq // 2
-    cr, lanes, cw = rows // 2 // chips, 2 * SPLIT, cols // (2 * SPLIT)
+    pr, cw = qrows // 4, cols // chips
     V, D = pltpu.VMEM, pltpu.SemaphoreType.DMA
     return pl.pallas_call(
         functools.partial(sum_body, n_seq),
-        out_shape=(sds((rows, cols), BF16), sds(small.shape, F32), sds((n, width), F32),
-                   sds(mine.shape[1:], F32), sds(mine.shape[1:], F32)),
-        in_specs=[VM] * 7, out_specs=(VM,) * 5,
+        out_shape=(sds((4 * qrows, cols), BF16), sds(small.shape, F32), sds(gn_rem.shape, BF16),
+                   sds(mine.shape, BF16)),
+        in_specs=[VM] * 4, out_specs=(VM,) * 4,
         scratch_shapes=[
-            V(mine.shape, BF16),
-            V((chips, cr, cols), BF16), V((chips - 1, lanes, cr, cw), BF16), V((chips - 1, lanes, cr, cw), BF16),
-            V((lanes, cr, cw), BF16), V((lanes, cr, cw), BF16),
-            V((3,) + small.shape, F32), V((chips,) + small.shape, F32), V((n, width), BF16),
-            D((chips,)), D((chips,)), D((chips - 1, lanes)), D((chips - 1, lanes)), D((lanes,)), D((lanes,)),
-            D((chips - 1, lanes)), D((chips - 1, lanes)), D((chips, lanes)), D((chips, lanes)),
+            V((chips - 1, 4, pr, cw), BF16), V((chips - 1, 4, pr, cw), BF16),
+            V((3,) + small.shape, F32), V((chips,) + small.shape, F32),
+            D((chips - 1, 4)), D((chips - 1, 4)), D((4,)), D((4,)),
+            D((chips - 1, 4)), D((chips - 1, 4)), D((chips, 4)), D((chips, 4)),
             D((chips - 1,)), D((chips - 1,)), D((4,)), D((4,))],
         compiler_params=pltpu.CompilerParams(
             vmem_limit_bytes=LIMIT, collective_id=2, has_side_effects=True),
         name="sums",
-    )(g, small, own, gn_rem, base, g1, mine)
-
-
-def finish_body(g, small, qkv, proj, fg, fb, qgg, kgg, sgg, sbg):
+    )(quarter, small, gn_rem, mine)
+
+
+def finish_body(g, small, own, gback, base, g1, mine, other, block, qkv, proj, fg, fb, qgg, kgg, sgg, sbg,
+                igrad, upg, downg, out):
     width = proj.shape[1]
-    qkv[...] = g[:, 0:3 * width].astype(F32)
-    proj[...] = g[:, 3 * width:].astype(F32)
+    proj[...] = g[:, 0:width].astype(F32)
+    for j in range(3):
+        for part in range(3):
+            at = (j + 1) * width + part * TILE
+            qkv[:, part * width + j * TILE:part * width + (j + 1) * TILE] = g[:, at:at + TILE].astype(F32)
+    xh, r = rows_norm(own[...].astype(F32))
+    dy = gback[...].astype(F32) * g1[...].reshape(1, width)
+    dx = r * (dy - jnp.mean(dy, -1, keepdims=True) - xh * jnp.mean(dy * xh, -1, keepdims=True))
+    igrad[...] = base[...] + dx
+    out[...] = block[...]
+
+    total = mine[...].astype(F32) + other[...].astype(F32)
+    upg[...] = total[0]
+    downg[...] = total[1]
 
     @pl.when(pl.program_id(0) == 0)
     def _():
@@ -317,28 +288,34 @@
             ref[...] = folded[:, 0:64].reshape(64)
 
 
-def finish_call(g, small):
+def finish_call(g, small, own, gback, base, g1, mine, other, block):
     rows, cols = g.shape
-    width = cols // 4
-    step = 128
+    n, width = own.shape
+    f = mine.shape[1]
+    steps = 2
     whole = lambda size: pl.BlockSpec((size,), lambda i: (0,))
+    strip = lambda size, lanes: pl.BlockSpec((size // steps, lanes), lambda i: (i, 0))
+    ffn_in = pl.BlockSpec((2, f // steps, width), lambda i: (0, i, 0))
     return pl.pallas_call(
-        finish_body, grid=(rows // step,),
+        finish_body, grid=(steps,),
         out_shape=(sds((rows, 3 * width), F32), sds((rows, width), F32), sds((width,), F32), sds((width,), F32),
-                   sds((64,), F32), sds((64,), F32), sds((width,), F32), sds((width,), F32)),
-        in_specs=[pl.BlockSpec((step, cols), lambda i: (i, 0)), pl.BlockSpec(small.shape, lambda i: (0, 0))],
-        out_specs=(pl.BlockSpec((step, 3 * width), lambda i: (i, 0)), pl.BlockSpec((step, width), lambda i: (i, 0)),
-                   whole(width), whole(width), whole(64), whole(64), whole(width), whole(width)),
+                   sds((64,), F32), sds((64,), F32), sds((width,), F32), sds((width,), F32),
+                   sds((n, width), F32), sds((f, width), F32), sds((f, width), F32), sds((n, width), BF16)),
+        in_specs=[strip(rows, cols), pl.BlockSpec(small.shape, lambda i: (0, 0)), strip(n, width), strip(n, width),
+                  strip(n, width), whole(width), ffn_in, ffn_in, strip(n, width)],
+        out_specs=(strip(rows, 3 * width), strip(rows, width),
+                   whole(width), whole(width), whole(64), whole(64), whole(width), whole(width),
+                   strip(n, width), strip(f, width), strip(f, width), strip(n, width)),
         name="finish",
-    )(g, small)
+    )(g, small, own, gback, base, g1, mine, other, block)
 
 
 def layer_body(n_seq, own, gy, seg, g1, b1, wqkv, qg, kg, wout, g2, b2, wup, wdown,
-               out, base, gn_rem, gall, small, mine,
+               out, base, gn_rem, quarter, small, mine,
                rem, fq, fk, ones, swap, vecs, normed, kk, vv, qq, rq, rk, qaug, att, mid,
                sx, sg, wbuf, accin, accout, first, hid, gpre, blk, gs, prec,
-               dk, stage,
-               wsend, wrecv, asend, arecv, psend, precv, tsend, trecv, gsem):
+               dk, pbuf, xin,
+               wsend, wrecv, asend, arecv, psend, precv, tsend, trecv, gsend, grecv, xsend, xrecv):
     n, width = own.shape
     f = wup.shape[0]
     h = f // 2
@@ -622,16 +599,50 @@
     parts[1].wait_recv()
     out[...] = (mid[...] + (blk[0:n, :] + prec[0])).astype(BF16)
 
-    def flush(j, rows, lanes):
-        return pltpu.make_async_copy(stage.at[j], gall.at[rows, lanes], gsem.at[j])
+    groups = (hid, gpre, sg, kk)
+    hr, qr = width // 2, width // 4
+
+    def g_copy(j):
+        return copy_to(groups[j].at[pl.ds(pl.multiple_of((1 - core) * hr, hr), hr)], pbuf.at[j], gsend.at[j],
+                       grecv.at[j], partner)
+
+    def x_copy(j):
+        return copy_to(groups[j].at[pl.ds(width, qr)], xin.at[j], xsend.at[j], xrecv.at[j], across)
+
+    def chip_sum(j, side):
+        return (groups[j][pl.ds(pl.multiple_of(core * hr + side * qr, qr), qr), :].astype(F32)
+                + pbuf[j, pl.ds(pl.multiple_of(side * qr, qr), qr), :].astype(F32))
+
+    def middle_sum(j):
+        g_copy(j).wait_recv()
+        groups[j][width:width + qr, :] = chip_sum(j, 1 - x).astype(BF16)
+        x_copy(j).start()
+
+    def last_sum(j):
+        x_copy(j).wait_recv()
+        quarter[:, j * width:(j + 1) * width] = (chip_sum(j, x) + xin[j].astype(F32)).astype(BF16)
 
     def proj_tile(i, c):
         rows = tile_of(i)
-        stage[i] = dot(att[:, rows], gbr[...], TN).astype(BF16)
-        flush(i, rows, pl.ds(3 * width, width)).start()
+        hid[rows, :] = dot(att[:, rows], gbr[...], TN).astype(BF16)
         return c
 
     lax.fori_loop(0, width // TILE, proj_tile, 0)
+    g_copy(0).start()
+
+    def qkv_group(j, points):
+        lanes = slice((j - 1) * TILE, j * TILE)
+
+        def tile(i, c):
+            rows = tile_of(i)
+            for part, (at, size) in enumerate(((0, n), (2 * n, 2 * n), (4 * n, 2 * n))):
+                groups[j][rows, part * TILE:(part + 1) * TILE] = dot(
+                    normed[0:size, rows], wbuf[at:at + size, lanes], TN).astype(BF16)
+            at_points(i, points, r_step)
+            return c
+
+        lax.fori_loop(0, width // TILE, tile, 0)
+        g_copy(j).start()
 
     def keys_of(j, rows):
         return wbuf.at[pl.ds(pl.multiple_of(j * 2 * n + rows, TILE), TILE)]
@@ -653,7 +664,9 @@
         return r * (gd - m1 - y * inv * m2), jnp.sum(prod, 0, keepdims=True) * inv
 
     def pair(p, c):
-        at_points(p, ((1, 3), (2, 4), (4, 7), (5, 8)), r_step)
+        at_points(p, ((1, 3), (2, 5), (3, 6), (4, 8), (5, 9)), r_step)
+        at_points(p, ((1, 0),), middle_sum)
+        at_points(p, ((3, 0), (5, 1)), last_sum)
         lanes = tile_of(p, 128)
         do = gat[:, lanes]
         delta = -group_sum(do.astype(F32) * att[:, lanes].astype(F32), swap[...])
@@ -668,7 +681,8 @@
         acc = [None, None]
         for t in range(2):
             if t:
-                at_points(p, ((0, 2), (2, 5), (3, 6)), r_step)
+                at_points(p, ((0, 2),), r_step)
+                at_points(p, ((2, 1), (4, 2)), middle_sum)
             rows = slice(t * n, (t + 1) * n)
             k, v, feat = kk[rows, lanes], vv[rows, lanes], fk[rows, :]
             one = jnp.ones_like(v)
@@ -694,12 +708,12 @@
         dx, gg = norm_back(dk[...], kk[:, lanes], rk[:, lanes], vecs[5:6, lanes])
         wbuf[2 * n:4 * n, lanes] = dx.astype(BF16)
         small[5:6, lanes] = gg
+        at_points(p, ((1, 4), (3, 7), (5, 10)), r_step)
+        at_points(p, ((1, 1), (3, 2)), lambda j: qkv_group(j, ()))
         return c
 
     lax.fori_loop(0, pairs, pair, 0)
-    for i in range(width // TILE):
-        flush(i, pl.ds(i * TILE, TILE), pl.ds(3 * width, width)).wait()
-    r_step(9)
+    qkv_group(3, ((1, 11),))
 
     def gain_sums(xh, gn):
         small[0:1, :] += jnp.sum(gn * xh, axis=0, keepdims=True)
@@ -724,20 +738,10 @@
         base[rows, :] += r * (gd - jnp.mean(gd, -1, keepdims=True) - xh * jnp.mean(gd * xh, -1, keepdims=True))
         return c
 
-    def qkv_tile(i, c):
-        rows = tile_of(i)
-        jobs = ((0, n, 0), (2 * n, 2 * n, 1), (4 * n, 2 * n, 2))
-        for j, (at, size, part) in enumerate(jobs):
-            stage[j] = dot(normed[0:size, rows], wbuf[at:at + size, :], TN).astype(BF16)
-            flush(j, rows, pl.ds(part * width, width)).start()
-        for j, (at, size, part) in enumerate(jobs):
-            flush(j, rows, pl.ds(part * width, width)).wait()
-        at_points(i, ((0, 10), (2, 11)), r_step)
-        return c
-
-    lax.fori_loop(0, width // TILE, qkv_tile, 0)
     lax.fori_loop(0, tiles, rem_tile, 0)
+    middle_sum(3)
     r_step(12)
+    last_sum(2)
     lax.fori_loop(0, tiles, own_back, 0)
     r_step(13)
     mine[...] = (first[...] + accin[chips - 2].astype(F32)).astype(BF16)
@@ -747,6 +751,10 @@
                 c.wait_send()
     for i in range(tiles):
         t_copy(i).wait_send()
+    last_sum(3)
+    for j in range(4):
+        g_copy(j).wait_send()
+        x_copy(j).wait_send()
     for c in (gy_copy,) + parts:
         c.wait_send()
 
@@ -761,9 +769,9 @@
     return pl.pallas_call(
         functools.partial(layer_body, n_seq),
         out_shape=(sds((n, width), BF16), sds((n, width), F32), sds((n, width), BF16),
-                   sds((width, 4 * width), BF16), sds((8, width), F32), sds((2, f, width), BF16)),
+                   sds((width // 4, 4 * width), BF16), sds((8, width), F32), sds((2, f, width), BF16)),
         in_specs=[VM] * 13,
-        out_specs=(VM, VM, VM, pl.BlockSpec(memory_space=pl.ANY), VM, VM),
+        out_specs=(VM,) * 6,
         scratch_shapes=[
             V((n, width), BF16), V((n, 128), BF16), V((2 * n, 128), BF16), V((256, 256), BF16), V((128, 128), BF16),
             V((8, width), F32), V((2 * n, width), BF16), V((2 * n, width), BF16), V((2 * n, width), BF16),
@@ -773,9 +781,10 @@
             V((chips - 1, 2, f, width), BF16), V((chips - 1, 2, f, width), BF16), V((2, f, width), F32),
             V((2 * n, chips // 2 * f), BF16), V((2 * n, chips // 2 * f), BF16), V((2 * n, width), F32), V((2 * n, width), F32),
             V((2, n, width), F32),
-            V((2 * n, 128), F32), V((3, TILE, width), BF16),
+            V((2 * n, 128), F32), V((4, width // 2, width), BF16), V((4, width // 4, width), BF16),
             D((2, 2, chips - 1)), D((2, 2, chips - 1)), D((2, 2, chips - 1)), D((2, 2, chips - 1)),
-            D((3 + tiles,)), D((3 + tiles,)), D((tiles,)), D((tiles,)), D((3,))],
+            D((3 + tiles,)), D((3 + tiles,)), D((tiles,)), D((tiles,)),
+            D((4,)), D((4,)), D((4,)), D((4,))],
         compiler_params=pltpu.CompilerParams(
             vmem_limit_bytes=66 * 1000 * 1000, collective_id=1, has_side_effects=True),
         name="layer",
@@ -786,11 +795,12 @@
               second_gain, second_bias, w_up, w_down, out_grad):
     n_seq = lax.axis_size("seq")
     own = tokens[0]
-    block_out, base, gn_rem, g, small, mine = layer_call(
+    block_out, base, gn_rem, quarter, small, mine = layer_call(
         n_seq, own, out_grad[0], segment_ids, first_gain, first_bias, w_qkv, query_gain, key_gain, w_out,
         second_gain, second_bias, w_up.T, w_down.T)
-    g, small, input_grad, up_grad, down_grad = sum_call(n_seq, g, small, own, gn_rem, base, first_gain, mine)
-    qkv, proj, fg, fb, qgg, kgg, sgg, sbg = finish_call(g, small)
+    g, small, gback, other = sum_call(n_seq, quarter, small, gn_rem, mine)
+    qkv, proj, fg, fb, qgg, kgg, sgg, sbg, input_grad, up_grad, down_grad, block_out = finish_call(
+        g, small, own, gback, base, first_gain, mine, other, block_out)
     return (block_out[None], input_grad[None], fg, fb, qkv, qgg, kgg, proj, sgg, sbg, up_grad.T, down_grad.T)
 
 

time: 195 us -> 182 us (0.933)
  Pallas kernels: 190 us -> 181 us
  local copies, waits for them, and re-layouts: 3.67 us -> 0 us
    pallas_call x2, Pallas kernels: 84.1 us -> 68.6 us  [the longest x1 60.5 us: sum_call(): pl.pallas_call(functools.partial(sum_body, n_seq), out_shape=(sds((4 * qr...]
    pallas_call x1, Pallas kernels: 106 us -> 112 us  [layer_call(): pl.pallas_call(functools.partial(layer_body, n_seq), out_shape=(sds((n, w...]
    unnamed x12 -> x0, local copies, waits for them, and re-layouts: 3.67 us -> none
where the time goes in v4:
time: 182 us; the launch traced here: 181 us
  Pallas kernels  181 us (99%)
    pallas_call x1, Pallas kernels, layer_call(): pl.pallas_call(functools.partial(layer_body, n_seq), out_shape=(sds((n, w...  112 us
    pallas_call x1, Pallas kernels, sum_call(): pl.pallas_call(functools.partial(sum_body, n_seq), out_shape=(sds((4 * qr...  60.5 us
    pallas_call x1, Pallas kernels, finish_call(): pl.pallas_call(finish_body, grid=(steps,), out_shape=(sds((rows, 3 * widt...  8.09 us

profile of v4, /device:TPU:0, one launch (start us, length us, event | category | flops | bytes accessed | tf_op | source)
XLA Modules:
  0.0 181.4 jit_solution(370791756100917646)
XLA Ops:
  0.6 112.0 %layer.1 = (bf16[512,768]{1,0:T(8,128)(2,1)}, f32[512,768]{1,0:T(8,128)}, bf16[512,768]{1,0:T(8,128)(2,1)}, bf16[192,3072]{1,0:T(8,128)(2,1)}, f32[8,768]{1,0:T(8,128)}, /*index=5*/bf16[2,192,768]{2,1,0:T(8,128)(2,1)}) custom-call(bf16[512,768]{1,0:T(8,128)(2,1)} %bitcast.8, bf16[512,768]{1,0:T(8,128)(2,1)} %bitcast.10, s32[1,1024]{1,0:T(1,128)} %seg.1, ...), custom_call_target="tpu_custom_call" | custom-call | tf_op jit(solution)/shard_map/layer/pallas_call | solution.py:769
  112.7 60.5 %sums.1 = (bf16[768,3072]{1,0:T(8,128)(2,1)}, f32[8,768]{1,0:T(8,128)}, bf16[512,768]{1,0:T(8,128)(2,1)}, bf16[2,192,768]{2,1,0:T(8,128)(2,1)}) custom-call(bf16[192,3072]{1,0:T(8,128)(2,1)} %get-tuple-element.34.quarter, f32[8,768]{1,0:T(8,128)} %get-tuple-element.35.small, bf16[512,768]{1,0:T(8,128)(2,1)} %get-tuple-element.36.gn_rem, ...), custom_call_target="tpu_custom_call" | custom-call | tf_op jit(solution)/shard_map/sums/pallas_call | solution.py:244
  173.2 8.1 %finish.1 = (f32[768,2304]{1,0:T(8,128)}, f32[768,768]{1,0:T(8,128)}, f32[768]{0:T(1024)}, f32[768]{0:T(1024)}, f32[64]{0:T(128)}, /*index=5*/f32[64]{0:T(128)},...) custom-call(bf16[768,3072]{1,0:T(8,128)(2,1)} %get-tuple-element.38., ...), custom_call_target="tpu_custom_call" | custom-call | tf_op jit(solution)/shard_map/finish/pallas_call | solution.py:299

commit v5 on v4

--- a/solution.py
+++ b/solution.py
@@ -102,26 +102,29 @@
         side = 1 - x if o else x
         return pl.ds(pl.multiple_of(c * 2 * qrows + side * qrows + d * hr, hr), hr)
 
-    def a_copy(i, s):
-        return copy_to(accout.at[s, i], accin.at[s, i], asend.at[s, i], arecv.at[s, i], left if i // 2 else right)
+    half = chips // 2
+
+    def a_copy(d, i, s):
+        return copy_to(accout.at[s - 1, d, i], accin.at[s - 1, d, i], asend.at[s - 1, d, i], arecv.at[s - 1, d, i],
+                       left if d else right)
 
     def x_piece(i, side, p):
         ref = fin.at[pl.ds(pl.multiple_of(core * 2 * qrows + side * qrows + i * pr, pr), pr), lanes_of(p)]
         return copy_to(ref, ref, xsend.at[i], xrecv.at[i], across)
 
-    def ring_copy(d, o, s, p):
-        ref = fin.at[rows_of(core, o, d), lanes_of(p)]
-        return copy_to(ref, ref, fsend.at[s, d * 2 + o], frecv.at[s, d * 2 + o], left if d else right)
-
-    def f_copy(d, o, s):
-        return ring_copy(d, o, s, chunk(place + s) if d else chunk(place - s))
-
-    def f_recv(d, o, s):
-        return ring_copy(d, o, s, chunk(place + s + 1) if d else chunk(place - s - 1))
-
-    def pair_copy(c, d, o, s):
-        ref = fin.at[rows_of(c, o, d), lanes_of(chunk(place + s) if d else chunk(place - s))]
-        return copy_to(ref, ref, qsend.at[s, d * 2 + o], qrecv.at[s, d * 2 + o], partner)
+    def ring_copy(d, o, e, s, p):
+        ref = fin.at[rows_of(core, o, e), lanes_of(p)]
+        return copy_to(ref, ref, fsend.at[s, d, o * 2 + e], frecv.at[s, d, o * 2 + e], left if d else right)
+
+    def f_copy(d, o, e, s):
+        return ring_copy(d, o, e, s, chunk(place + s) if d else chunk(place - s))
+
+    def f_recv(d, o, e, s):
+        return ring_copy(d, o, e, s, chunk(place + s + 1) if d else chunk(place - s - 1))
+
+    def pair_copy(c, d, o, e, s):
+        ref = fin.at[rows_of(c, o, e), lanes_of(chunk(place + s) if d else chunk(place - s))]
+        return copy_to(ref, ref, qsend.at[s, d, o * 2 + e], qrecv.at[s, d, o * 2 + e], partner)
 
     def s_copy(s):
         return copy_to(sring.at[chunk(place - s)], sring.at[chunk(place - s)], ssend.at[s], srecv.at[s], right)
@@ -130,109 +133,97 @@
         p = chunk(place - s - 1)
         return copy_to(sring.at[p], sring.at[p], ssend.at[s], srecv.at[s], right)
 
-    back = copy_to(gn_rem, gback, gsend.at[0], grecv.at[0], across)
+    n = gn_rem.shape[0]
+    backs = [copy_to(gn_rem.at[pl.ds(i * n // 2, n // 2)], gback.at[pl.ds(i * n // 2, n // 2)],
+                     gsend.at[4 * i], grecv.at[4 * i], across) for i in range(2)]
     small_p = copy_to(small, srec.at[0], gsend.at[1], grecv.at[1], partner)
     small_x = copy_to(srec.at[1], srec.at[2], gsend.at[2], grecv.at[2], across)
     ffn_x = copy_to(mine, other, gsend.at[3], grecv.at[3], across)
     pieces = (0, 2, 1, 3)
-    both = [(d, o) for o in range(2) for d in range(2)]
+    halves = [(o, e) for o in range(2) for e in range(2)]
+    arrivals = [(d, o, e, s) for s in range(1, half + 1) for o, e in halves for d in range(2) if s < half or e == d]
+    pairs = [(0, o, e, 0) for o, e in halves] + arrivals
 
     small_p.start()
 
     def part(i, q):
         return quarter[i * pr:(i + 1) * pr, lanes_of(q)].astype(F32)
 
-    def reduce_step(s, c):
-        for i in pieces:
-            q = chunk(place + s) if i // 2 else chunk(place - s)
-
-            @pl.when(s == 1)
-            def _():
-                accout[s - 1, i] = part(i, q).astype(BF16)
-
-            @pl.when(s > 1)
-            def _():
-                a_copy(i, s - 2).wait_recv()
-                accout[s - 1, i] = (part(i, q) + accin[s - 2, i].astype(F32)).astype(BF16)
-
-            a_copy(i, s - 1).start()
-
-        @pl.when(s == 1)
-        def _():
-            back.start()
+    def reduce_piece(d, i, s, first):
+        q = chunk(place - (half + 1 - s)) if d else chunk(place + (half + 1 - s))
+        value = part(i, q)
+        if not first:
+            a_copy(d, i, s - 1).wait_recv()
+            value = value + accin[s - 2, d, i].astype(F32)
+        accout[s - 1, d, i] = value.astype(BF16)
+        a_copy(d, i, s).start()
+
+    hops = [(d, i, s) for s in range(1, half + 1) for i in (2, 3, 0, 1) for d in range(2)]
+    hops = [(d, (i + 2 * d) % 4, s) for d, i, s in hops]
+    hops = [(d, i, s) for d, i, s in hops if s > 1 or i // 2 == d]
+    for d, i, s in hops:
+        reduce_piece(d, i, s, s == (1 if i // 2 == d else 2))
+        if (d, i, s) == hops[7]:
+            backs[0].start()
             small_p.wait_recv()
             srec[1] = small[...] + srec[0]
             small_x.start()
-        return c
-
-    lax.fori_loop(1, chips, reduce_step, 0)
+
+    def own_start(o, e):
+        for d in range(2):
+            f_copy(d, o, e, 0).start()
+        pair_copy(core, 0, o, e, 0).start()
+
     for i in pieces:
-        a_copy(i, chips - 2).wait_recv()
+        total = part(i, place)
+        for d in range(2):
+            a_copy(d, i, half).wait_recv()
+            total = total + accin[half - 1, d, i].astype(F32)
         at = pl.ds(pl.multiple_of(core * 2 * qrows + x * qrows + i * pr, pr), pr)
-        fin[at, lanes_of(place)] = (part(i, place) + accin[chips - 2, i].astype(F32)).astype(BF16)
+        fin[at, lanes_of(place)] = total.astype(BF16)
         x_piece(i, x, place).start()
         if i % 2:
-            f_copy(i // 2, 0, 0).start()
-            pair_copy(core, i // 2, 0, 0).start()
+            own_start(0, i // 2)
+    backs[1].start()
     small_x.wait_recv()
     sring[place] = srec[1] + srec[2]
     s_copy(0).start()
     for i in pieces:
         x_piece(i, 1 - x, place).wait_recv()
         if i % 2:
-            f_copy(i // 2, 1, 0).start()
-            pair_copy(core, i // 2, 1, 0).start()
+            own_start(1, i // 2)
     ffn_x.start()
 
-    def gather_step(s, c):
-        for d, o in both:
-            f_recv(d, o, s - 1).wait_recv()
-
-            @pl.when(s < chips - 1)
-            def _():
-                f_copy(d, o, s).start()
-
-            pair_copy(core, d, o, s).start()
-        s_recv(s - 1).wait_recv()
-
-        @pl.when(s < chips - 1)
-        def _():
-            s_copy(s).start()
-        return c
-
-    lax.fori_loop(1, chips, gather_step, 0)
-
-    def finish(s, c):
-        for d, o in both:
-            pair_copy(1 - core, d, o, s).wait_recv()
-        return c
+    for at, (d, o, e, s) in enumerate(arrivals):
+        f_recv(d, o, e, s - 1).wait_recv()
+        if s < half - 1 or (s == half - 1 and e == d):
+            f_copy(d, o, e, s).start()
+        pair_copy(core, d, o, e, s).start()
+        if at % 4 == 3:
+            step = at // 4
+            s_recv(step).wait_recv()
+            if step < chips - 2:
+                s_copy(step + 1).start()
 
     total = sring[0]
     for s in range(1, chips):
         total = total + sring[s]
     sout[...] = total
-    lax.fori_loop(0, chips, finish, 0)
-    back.wait_recv()
-    ffn_x.wait_recv()
-
-    def drain(s, c):
-        for d, o in both:
-            pair_copy(core, d, o, s).wait_send()
-
-            @pl.when(s < chips - 1)
-            def _():
-                a_copy(d * 2 + o, s).wait_send()
-                f_copy(d, o, s).wait_send()
-
-        @pl.when(s < chips - 1)
-        def _():
-            s_copy(s).wait_send()
-        return c
-
-    lax.fori_loop(0, chips, drain, 0)
+    for d, o, e, s in pairs:
+        pair_copy(1 - core, d, o, e, s).wait_recv()
+    for c in backs + [ffn_x]:
+        c.wait_recv()
+    for d, o, e, s in pairs:
+        pair_copy(core, d, o, e, s).wait_send()
+    for d, o, e, s in arrivals:
+        f_copy(d, o, e, s - 1).wait_send()
+    for s in range(chips - 1):
+        s_copy(s).wait_send()
     for i in pieces:
         x_piece(i, x, place).wait_send()
-    for c in (back, small_p, small_x, ffn_x):
+    for d, i, s in hops:
+        a_copy(d, i, s).wait_send()
+    for c in backs + [small_p, small_x, ffn_x]:
         c.wait_send()
 
 
@@ -245,13 +236,14 @@
         functools.partial(sum_body, n_seq),
         out_shape=(sds((4 * qrows, cols), BF16), sds(small.shape, F32), sds(gn_rem.shape, BF16),
                    sds(mine.shape, BF16)),
-        in_specs=[VM] * 4, out_specs=(VM,) * 4,
+        in_specs=[VM, VM] + [pl.BlockSpec(memory_space=pl.ANY)] * 2,
+        out_specs=(VM, VM) + (pl.BlockSpec(memory_space=pl.ANY),) * 2,
         scratch_shapes=[
-            V((chips - 1, 4, pr, cw), BF16), V((chips - 1, 4, pr, cw), BF16),
+            V((chips // 2, 2, 4, pr, cw), BF16), V((chips // 2, 2, 4, pr, cw), BF16),
             V((3,) + small.shape, F32), V((chips,) + small.shape, F32),
-            D((chips - 1, 4)), D((chips - 1, 4)), D((4,)), D((4,)),
-            D((chips - 1, 4)), D((chips - 1, 4)), D((chips, 4)), D((chips, 4)),
-            D((chips - 1,)), D((chips - 1,)), D((4,)), D((4,))],
+            D((chips // 2, 2, 4)), D((chips // 2, 2, 4)), D((4,)), D((4,)),
+            D((chips // 2, 2, 4)), D((chips // 2, 2, 4)), D((chips // 2 + 1, 2, 4)), D((chips // 2 + 1, 2, 4)),
+            D((chips - 1,)), D((chips - 1,)), D((5,)), D((5,))],
         compiler_params=pltpu.CompilerParams(
             vmem_limit_bytes=LIMIT, collective_id=2, has_side_effects=True),
         name="sums",
@@ -310,12 +302,12 @@
     )(g, small, own, gback, base, g1, mine, other, block)
 
 
-def layer_body(n_seq, own, gy, seg, g1, b1, wqkv, qg, kg, wout, g2, b2, wup, wdown,
+def layer_body(n_seq, own, gy, seg, g1, b1, far_qkv, qg, kg, far_out, g2, b2, wup, wdown,
                out, base, gn_rem, quarter, small, mine,
                rem, fq, fk, ones, swap, vecs, normed, kk, vv, qq, rq, rk, qaug, att, mid,
                sx, sg, wbuf, accin, accout, first, hid, gpre, blk, gs, prec,
-               dk, pbuf, xin,
-               wsend, wrecv, asend, arecv, psend, precv, tsend, trecv, gsend, grecv, xsend, xrecv):
+               dk, pbuf, xin, wqkv, wout,
+               wsend, wrecv, asend, arecv, psend, precv, tsend, trecv, gsend, grecv, xsend, xrecv, lsem):
     n, width = own.shape
     f = wup.shape[0]
     h = f // 2
@@ -325,6 +317,10 @@
     core, place, right, left, partner = ring_places(n_seq)
     x = lax.axis_index("pos")
     right, left, partner, across = {"seq": right}, {"seq": left}, {"seq": partner}, {"pos": 1 - x}
+    fetch = [pltpu.make_async_copy(far, near, lsem.at[i]) for i, (far, near) in
+             enumerate(((far_qkv, wqkv), (far_out, wout)))]
+    for c in fetch:
+        c.start()
     greet((right, left, partner, across))
 
     def slot(s, k, d):
@@ -407,7 +403,7 @@
     def project(xs, i, queries):
         rows = tile_of(i)
         low = (rows_norm(xs)[0] * vecs[0:1, :] + vecs[1:2, :]).astype(BF16)
-        normed[rows, :] = low
+        normed[:, rows] = low.T
         for block in range(0 if queries else width // cols, 3 * width // cols):
             raw = dot(low, wqkv[:, block * cols:(block + 1) * cols])
             part, a = divmod(block * cols, width)
@@ -425,6 +421,7 @@
         project(own[tile_of(i), :].astype(F32), i, True)
         return c
 
+    fetch[0].wait()
     lax.fori_loop(0, tiles, own_tile, 0)
     w_step(0)
     lane_t = lax.broadcasted_iota(jnp.int32, (TILE, 128), 1)
@@ -489,6 +486,7 @@
 
     lax.fori_loop(0, pairs, close, 0)
     w_step(6)
+    fetch[1].wait()
     for i in range(tiles):
         rows = slice(i * TILE, (i + 1) * TILE)
         m = own[rows, :].astype(F32) + dot(att[rows, :], wout[...])
@@ -637,7 +635,7 @@
             rows = tile_of(i)
             for part, (at, size) in enumerate(((0, n), (2 * n, 2 * n), (4 * n, 2 * n))):
                 groups[j][rows, part * TILE:(part + 1) * TILE] = dot(
-                    normed[0:size, rows], wbuf[at:at + size, lanes], TN).astype(BF16)
+                    normed[rows, 0:size], wbuf[at:at + size, lanes]).astype(BF16)
             at_points(i, points, r_step)
             return c
 
@@ -725,6 +723,7 @@
               + dot(wbuf[pl.ds(pl.multiple_of(5 * n + i * TILE, TILE), TILE), :], wqkv[:, 2 * width:], NT))
         gn_rem[rows, :] = gn.astype(BF16)
         gain_sums(rows_norm(rem[rows, :].astype(F32))[0], gn)
+        at_points(i, ((0, 3),), middle_sum)
         return c
 
     def own_back(i, c):
@@ -739,7 +738,6 @@
         return c
 
     lax.fori_loop(0, tiles, rem_tile, 0)
-    middle_sum(3)
     r_step(12)
     last_sum(2)
     lax.fori_loop(0, tiles, own_back, 0)
@@ -770,11 +768,11 @@
         functools.partial(layer_body, n_seq),
         out_shape=(sds((n, width), BF16), sds((n, width), F32), sds((n, width), BF16),
                    sds((width // 4, 4 * width), BF16), sds((8, width), F32), sds((2, f, width), BF16)),
-        in_specs=[VM] * 13,
+        in_specs=[VM] * 5 + [pl.BlockSpec(memory_space=pl.ANY), VM, VM, pl.BlockSpec(memory_space=pl.ANY)] + [VM] * 4,
         out_specs=(VM,) * 6,
         scratch_shapes=[
             V((n, width), BF16), V((n, 128), BF16), V((2 * n, 128), BF16), V((256, 256), BF16), V((128, 128), BF16),
-            V((8, width), F32), V((2 * n, width), BF16), V((2 * n, width), BF16), V((2 * n, width), BF16),
+            V((8, width), F32), V((width, 2 * n), BF16), V((2 * n, width), BF16), V((2 * n, width), BF16),
             V((n, width), BF16), V((n, width), F32), V((2 * n, width), F32), V((heads, n, 128), BF16),
             V((n, width), BF16), V((n, width), F32),
             V((2 * n, width), BF16), V((2 * n, width), BF16), V((chips * 2 * f, width), BF16),
@@ -782,9 +780,10 @@
             V((2 * n, chips // 2 * f), BF16), V((2 * n, chips // 2 * f), BF16), V((2 * n, width), F32), V((2 * n, width), F32),
             V((2, n, width), F32),
             V((2 * n, 128), F32), V((4, width // 2, width), BF16), V((4, width // 4, width), BF16),
+            V(wqkv.shape, BF16), V(wout.shape, BF16),
             D((2, 2, chips - 1)), D((2, 2, chips - 1)), D((2, 2, chips - 1)), D((2, 2, chips - 1)),
             D((3 + tiles,)), D((3 + tiles,)), D((tiles,)), D((tiles,)),
-            D((4,)), D((4,)), D((4,)), D((4,))],
+            D((4,)), D((4,)), D((4,)), D((4,)), D((2,))],
         compiler_params=pltpu.CompilerParams(
             vmem_limit_bytes=66 * 1000 * 1000, collective_id=1, has_side_effects=True),
         name="layer",

time: 182 us -> 170 us (0.934)
  Pallas kernels: 181 us -> 169 us
    pallas_call x1, Pallas kernels: 60.5 us -> 49.8 us  [sum_call(): pl.pallas_call(functools.partial(sum_body, n_seq), out_shape=(sds((4 * qr...]
where the time goes in v5:
time: 170 us
  Pallas kernels  169 us (99%)
    pallas_call x1, Pallas kernels, layer_call(): pl.pallas_call(functools.partial(layer_body, n_seq), out_shape=(sds((n, w...  111 us
    pallas_call x1, Pallas kernels, sum_call(): pl.pallas_call(functools.partial(sum_body, n_seq), out_shape=(sds((4 * qr...  49.8 us
    pallas_call x1, Pallas kernels, finish_call(): pl.pallas_call(finish_body, grid=(steps,), out_shape=(sds((rows, 3 * widt...  8.09 us

profile of v5, /device:TPU:0, one launch (start us, length us, event | category | flops | bytes accessed | tf_op | source)
XLA Modules:
  0.0 169.8 jit_solution(2974925986600075013)
XLA Ops:
  0.6 111.1 %layer.1 = (bf16[512,768]{1,0:T(8,128)(2,1)}, f32[512,768]{1,0:T(8,128)}, bf16[512,768]{1,0:T(8,128)(2,1)}, bf16[192,3072]{1,0:T(8,128)(2,1)}, f32[8,768]{1,0:T(8,128)}, /*index=5*/bf16[2,192,768]{2,1,0:T(8,128)(2,1)}) custom-call(bf16[512,768]{1,0:T(8,128)(2,1)} %bitcast.8, bf16[512,768]{1,0:T(8,128)(2,1)} %bitcast.10, s32[1,1024]{1,0:T(1,128)} %seg.1, ...), custom_call_target="tpu_custom_call" | custom-call | tf_op jit(solution)/shard_map/layer/pallas_call | solution.py:767
  111.8 49.8 %sums.1 = (bf16[768,3072]{1,0:T(8,128)(2,1)}, f32[8,768]{1,0:T(8,128)}, bf16[512,768]{1,0:T(8,128)(2,1)}, bf16[2,192,768]{2,1,0:T(8,128)(2,1)}) custom-call(bf16[192,3072]{1,0:T(8,128)(2,1)} %get-tuple-element.34.quarter, f32[8,768]{1,0:T(8,128)} %get-tuple-element.35.small, bf16[512,768]{1,0:T(8,128)(2,1)} %get-tuple-element.36.gn_rem, ...), custom_call_target="tpu_custom_call" | custom-call | tf_op jit(solution)/shard_map/sums/pallas_call | solution.py:235
  161.6 8.1 %finish.1 = (f32[768,2304]{1,0:T(8,128)}, f32[768,768]{1,0:T(8,128)}, f32[768]{0:T(1024)}, f32[768]{0:T(1024)}, f32[64]{0:T(128)}, /*index=5*/f32[64]{0:T(128)},...) custom-call(bf16[768,3072]{1,0:T(8,128)(2,1)} %get-tuple-element.38., ...), custom_call_target="tpu_custom_call" | custom-call | tf_op jit(solution)/shard_map/finish/pallas_call | solution.py:291

commit v6 on v5

--- a/solution.py
+++ b/solution.py
@@ -81,9 +81,9 @@
     pl.semaphore_wait(barrier, len(targets))
 
 
-def sum_body(n_seq, quarter, small, gn_rem, mine, fin, sout, gback, other,
-             accin, accout, srec, sring,
-             asend, arecv, xsend, xrecv, fsend, frecv, qsend, qrecv, ssend, srecv, gsend, grecv):
+def sum_body(n_seq, quarter, small, gn_rem, mine, far_fin, sout, gback, other,
+             fin, accin, accout, srec, sring,
+             asend, arecv, xsend, xrecv, fsend, frecv, qsend, qrecv, ssend, srecv, gsend, grecv, osem):
     qrows, cols = quarter.shape
     chips = n_seq // 2
     cw, pr, hr = cols // chips, qrows // 4, qrows // 2
@@ -194,11 +194,23 @@
             own_start(1, i // 2)
     ffn_x.start()
 
+    def store(c, p):
+        block = (pl.ds(pl.multiple_of(c * 2 * qrows, 2 * qrows), 2 * qrows), lanes_of(p))
+        return pltpu.make_async_copy(fin.at[block], far_fin.at[block], osem.at[c, p])
+
+    def store_hop(c, s):
+        store(c, chunk(place - s)).start()
+        if 0 < s < half:
+            store(c, chunk(place + s)).start()
+
+    store_hop(core, 0)
     for at, (d, o, e, s) in enumerate(arrivals):
         f_recv(d, o, e, s - 1).wait_recv()
         if s < half - 1 or (s == half - 1 and e == d):
             f_copy(d, o, e, s).start()
         pair_copy(core, d, o, e, s).start()
+        if at + 1 == len(arrivals) or arrivals[at + 1][3] > s:
+            store_hop(core, s)
         if at % 4 == 3:
             step = at // 4
             s_recv(step).wait_recv()
@@ -209,8 +221,10 @@
     for s in range(1, chips):
         total = total + sring[s]
     sout[...] = total
-    for d, o, e, s in pairs:
+    for at, (d, o, e, s) in enumerate(pairs):
         pair_copy(1 - core, d, o, e, s).wait_recv()
+        if at + 1 == len(pairs) or pairs[at + 1][3] > s:
+            store_hop(1 - core, s)
     for c in backs + [ffn_x]:
         c.wait_recv()
     for d, o, e, s in pairs:
@@ -223,6 +237,9 @@
         x_piece(i, x, place).wait_send()
     for d, i, s in hops:
         a_copy(d, i, s).wait_send()
+    for c in range(2):
+        for p in range(chips):
+            store(c, p).wait()
     for c in backs + [small_p, small_x, ffn_x]:
         c.wait_send()
 
@@ -237,13 +254,14 @@
         out_shape=(sds((4 * qrows, cols), BF16), sds(small.shape, F32), sds(gn_rem.shape, BF16),
                    sds(mine.shape, BF16)),
         in_specs=[VM, VM] + [pl.BlockSpec(memory_space=pl.ANY)] * 2,
-        out_specs=(VM, VM) + (pl.BlockSpec(memory_space=pl.ANY),) * 2,
+        out_specs=(pl.BlockSpec(memory_space=pl.ANY), VM) + (pl.BlockSpec(memory_space=pl.ANY),) * 2,
         scratch_shapes=[
+            V((4 * qrows, cols), BF16),
             V((chips // 2, 2, 4, pr, cw), BF16), V((chips // 2, 2, 4, pr, cw), BF16),
             V((3,) + small.shape, F32), V((chips,) + small.shape, F32),
             D((chips // 2, 2, 4)), D((chips // 2, 2, 4)), D((4,)), D((4,)),
             D((chips // 2, 2, 4)), D((chips // 2, 2, 4)), D((chips // 2 + 1, 2, 4)), D((chips // 2 + 1, 2, 4)),
-            D((chips - 1,)), D((chips - 1,)), D((5,)), D((5,))],
+            D((chips - 1,)), D((chips - 1,)), D((5,)), D((5,)), D((2, chips))],
         compiler_params=pltpu.CompilerParams(
             vmem_limit_bytes=LIMIT, collective_id=2, has_side_effects=True),
         name="sums",
@@ -303,11 +321,11 @@
 
 
 def layer_body(n_seq, own, gy, seg, g1, b1, far_qkv, qg, kg, far_out, g2, b2, wup, wdown,
-               out, base, gn_rem, quarter, small, mine,
+               far_block, far_base, far_gn, far_quarter, small, far_mine,
                rem, fq, fk, ones, swap, vecs, normed, kk, vv, qq, rq, rk, qaug, att, mid,
                sx, sg, wbuf, accin, accout, first, hid, gpre, blk, gs, prec,
-               dk, pbuf, xin, wqkv, wout,
-               wsend, wrecv, asend, arecv, psend, precv, tsend, trecv, gsend, grecv, xsend, xrecv, lsem):
+               dk, pbuf, xin, wqkv, wout, out, base, gn_rem, quarter, mine,
+               wsend, wrecv, asend, arecv, psend, precv, tsend, trecv, gsend, grecv, xsend, xrecv, lsem, osem):
     n, width = own.shape
     f = wup.shape[0]
     h = f // 2
@@ -321,6 +339,10 @@
              enumerate(((far_qkv, wqkv), (far_out, wout)))]
     for c in fetch:
         c.start()
+    early, late = pl.ds(0, 3 * width), pl.ds(3 * width, width)
+    stores = [pltpu.make_async_copy(near, far, osem.at[i]) for i, (near, far) in enumerate((
+        (out, far_block), (gn_rem, far_gn), (base, far_base), (mine, far_mine),
+        (quarter.at[:, early], far_quarter.at[:, early]), (quarter.at[:, late], far_quarter.at[:, late])))]
     greet((right, left, partner, across))
 
     def slot(s, k, d):
@@ -596,6 +618,7 @@
     r_step(1)
     parts[1].wait_recv()
     out[...] = (mid[...] + (blk[0:n, :] + prec[0])).astype(BF16)
+    stores[0].start()
 
     groups = (hid, gpre, sg, kk)
     hr, qr = width // 2, width // 4
@@ -738,11 +761,15 @@
         return c
 
     lax.fori_loop(0, tiles, rem_tile, 0)
+    stores[1].start()
     r_step(12)
     last_sum(2)
+    stores[4].start()
     lax.fori_loop(0, tiles, own_back, 0)
+    stores[2].start()
     r_step(13)
     mine[...] = (first[...] + accin[chips - 2].astype(F32)).astype(BF16)
+    stores[3].start()
     for j in range(1, chips):
         for k in range(2):
             for c in a_copies(j, k):
@@ -750,6 +777,9 @@
     for i in range(tiles):
         t_copy(i).wait_send()
     last_sum(3)
+    stores[5].start()
+    for c in stores:
+        c.wait()
     for j in range(4):
         g_copy(j).wait_send()
         x_copy(j).wait_send()
@@ -769,7 +799,7 @@
         out_shape=(sds((n, width), BF16), sds((n, width), F32), sds((n, width), BF16),
                    sds((width // 4, 4 * width), BF16), sds((8, width), F32), sds((2, f, width), BF16)),
         in_specs=[VM] * 5 + [pl.BlockSpec(memory_space=pl.ANY), VM, VM, pl.BlockSpec(memory_space=pl.ANY)] + [VM] * 4,
-        out_specs=(VM,) * 6,
+        out_specs=(pl.BlockSpec(memory_space=pl.ANY),) * 4 + (VM, pl.BlockSpec(memory_space=pl.ANY)),
         scratch_shapes=[
             V((n, width), BF16), V((n, 128), BF16), V((2 * n, 128), BF16), V((256, 256), BF16), V((128, 128), BF16),
             V((8, width), F32), V((width, 2 * n), BF16), V((2 * n, width), BF16), V((2 * n, width), BF16),
@@ -781,9 +811,11 @@
             V((2, n, width), F32),
             V((2 * n, 128), F32), V((4, width // 2, width), BF16), V((4, width // 4, width), BF16),
             V(wqkv.shape, BF16), V(wout.shape, BF16),
+            V((n, width), BF16), V((n, width), F32), V((n, width), BF16), V((width // 4, 4 * width), BF16),
+            V((2, f, width), BF16),
             D((2, 2, chips - 1)), D((2, 2, chips - 1)), D((2, 2, chips - 1)), D((2, 2, chips - 1)),
             D((3 + tiles,)), D((3 + tiles,)), D((tiles,)), D((tiles,)),
-            D((4,)), D((4,)), D((4,)), D((4,)), D((2,))],
+            D((4,)), D((4,)), D((4,)), D((4,)), D((2,)), D((6,))],
         compiler_params=pltpu.CompilerParams(
             vmem_limit_bytes=66 * 1000 * 1000, collective_id=1, has_side_effects=True),
         name="layer",

time: 170 us -> 169 us (level)
  no operation moved by 1% of the time
where the time goes in v6:
time: 169 us
  Pallas kernels  168 us (99%)
    pallas_call x1, Pallas kernels, layer_call(): pl.pallas_call(functools.partial(layer_body, n_seq), out_shape=(sds((n, w...  110 us
    pallas_call x1, Pallas kernels, sum_call(): pl.pallas_call(functools.partial(sum_body, n_seq), out_shape=(sds((4 * qr...  49.6 us
    pallas_call x1, Pallas kernels, finish_call(): pl.pallas_call(finish_body, grid=(steps,), out_shape=(sds((rows, 3 * widt...  8.09 us

profile of v6, /device:TPU:0, one launch (start us, length us, event | category | flops | bytes accessed | tf_op | source)
XLA Modules:
  0.0 168.8 jit_solution(8328073279868946489)
XLA Ops:
  0.6 110.3 %layer.1 = (bf16[512,768]{1,0:T(8,128)(2,1)}, f32[512,768]{1,0:T(8,128)}, bf16[512,768]{1,0:T(8,128)(2,1)}, bf16[192,3072]{1,0:T(8,128)(2,1)}, f32[8,768]{1,0:T(8,128)}, /*index=5*/bf16[2,192,768]{2,1,0:T(8,128)(2,1)}) custom-call(bf16[512,768]{1,0:T(8,128)(2,1)} %bitcast.8, bf16[512,768]{1,0:T(8,128)(2,1)} %bitcast.10, s32[1,1024]{1,0:T(1,128)} %seg.1, ...), custom_call_target="tpu_custom_call" | custom-call | tf_op jit(solution)/shard_map/layer/pallas_call | solution.py:797
  110.9 49.6 %sums.1 = (bf16[768,3072]{1,0:T(8,128)(2,1)}, f32[8,768]{1,0:T(8,128)}, bf16[512,768]{1,0:T(8,128)(2,1)}, bf16[2,192,768]{2,1,0:T(8,128)(2,1)}) custom-call(bf16[192,3072]{1,0:T(8,128)(2,1)} %get-tuple-element.34.quarter, f32[8,768]{1,0:T(8,128)} %get-tuple-element.35.small, bf16[512,768]{1,0:T(8,128)(2,1)} %get-tuple-element.36.gn_rem, ...), custom_call_target="tpu_custom_call" | custom-call | tf_op jit(solution)/shard_map/sums/pallas_call | solution.py:252
  160.5 8.1 %finish.1 = (f32[768,2304]{1,0:T(8,128)}, f32[768,768]{1,0:T(8,128)}, f32[768]{0:T(1024)}, f32[768]{0:T(1024)}, f32[64]{0:T(128)}, /*index=5*/f32[64]{0:T(128)},...) custom-call(bf16[768,3072]{1,0:T(8,128)(2,1)} %get-tuple-element.38., ...), custom_call_target="tpu_custom_call" | custom-call | tf_op jit(solution)/shard_map/finish/pallas_call | solution.py:309

commit v7 on v6

--- a/solution.py
+++ b/solution.py
@@ -762,11 +762,11 @@
 
     lax.fori_loop(0, tiles, rem_tile, 0)
     stores[1].start()
-    r_step(12)
     last_sum(2)
     stores[4].start()
     lax.fori_loop(0, tiles, own_back, 0)
     stores[2].start()
+    r_step(12)
     r_step(13)
     mine[...] = (first[...] + accin[chips - 2].astype(F32)).astype(BF16)
     stores[3].start()

time: 169 us -> 169 us (level)
  no operation moved by 1% of the time
where the time goes in v7:
time: 169 us
  Pallas kernels  168 us (99%)
    pallas_call x1, Pallas kernels, layer_call(): pl.pallas_call(functools.partial(layer_body, n_seq), out_shape=(sds((n, w...  110 us
    pallas_call x1, Pallas kernels, sum_call(): pl.pallas_call(functools.partial(sum_body, n_seq), out_shape=(sds((4 * qr...  49.6 us
    pallas_call x1, Pallas kernels, finish_call(): pl.pallas_call(finish_body, grid=(steps,), out_shape=(sds((rows, 3 * widt...  8.09 us

profile of v7, /device:TPU:0, one launch (start us, length us, event | category | flops | bytes accessed | tf_op | source)
XLA Modules:
  0.0 168.8 jit_solution(17781141024137228482)
XLA Ops:
  0.6 110.3 %layer.1 = (bf16[512,768]{1,0:T(8,128)(2,1)}, f32[512,768]{1,0:T(8,128)}, bf16[512,768]{1,0:T(8,128)(2,1)}, bf16[192,3072]{1,0:T(8,128)(2,1)}, f32[8,768]{1,0:T(8,128)}, /*index=5*/bf16[2,192,768]{2,1,0:T(8,128)(2,1)}) custom-call(bf16[512,768]{1,0:T(8,128)(2,1)} %bitcast.8, bf16[512,768]{1,0:T(8,128)(2,1)} %bitcast.10, s32[1,1024]{1,0:T(1,128)} %seg.1, ...), custom_call_target="tpu_custom_call" | custom-call | tf_op jit(solution)/shard_map/layer/pallas_call | solution.py:797
  110.9 49.6 %sums.1 = (bf16[768,3072]{1,0:T(8,128)(2,1)}, f32[8,768]{1,0:T(8,128)}, bf16[512,768]{1,0:T(8,128)(2,1)}, bf16[2,192,768]{2,1,0:T(8,128)(2,1)}) custom-call(bf16[192,3072]{1,0:T(8,128)(2,1)} %get-tuple-element.34.quarter, f32[8,768]{1,0:T(8,128)} %get-tuple-element.35.small, bf16[512,768]{1,0:T(8,128)(2,1)} %get-tuple-element.36.gn_rem, ...), custom_call_target="tpu_custom_call" | custom-call | tf_op jit(solution)/shard_map/sums/pallas_call | solution.py:252
  160.5 8.1 %finish.1 = (f32[768,2304]{1,0:T(8,128)}, f32[768,768]{1,0:T(8,128)}, f32[768]{0:T(1024)}, f32[768]{0:T(1024)}, f32[64]{0:T(128)}, /*index=5*/f32[64]{0:T(128)},...) custom-call(bf16[768,3072]{1,0:T(8,128)(2,1)} %get-tuple-element.38., ...), custom_call_target="tpu_custom_call" | custom-call | tf_op jit(solution)/shard_map/finish/pallas_call | solution.py:309
